TPU v7x, 128 devices: a whole 4x4x4 slice. The times are simulated.
128 devices in a mesh: section: 8 (over y, z_lo), dp: 16 (over z_hi, x, core).
Axes of the slice: x: 4, y: 4, z: 4 (z_hi: 2, z_lo: 2; z = z_hi * 2 + z_lo), core: 2. Of those that a mesh axis runs over, the one named last changes fastest.
Arguments:
- images: bfloat16 [32, 16, 16, 768], P('dp'), may hold values from -6 to 6
- roster: int32 [16, 2], P('dp'), may hold values from 0 to 1, each once within a row
- cotangent: bfloat16 [32, 16, 16, 768], P('dp'), may hold values from -6 to 6
- depth_kernel: bfloat16 [8, 7, 7, 768], P('section'), may hold values from -0.875 to 0.875
- up_weight: bfloat16 [8, 768, 3072], P('section'), may hold values from -0.21875 to 0.21875
- down_weight: bfloat16 [8, 3072, 768], P('section'), may hold values from -0.109375 to 0.109375
- layer_scale: float32 [8, 768], P('section'), may hold values from 0.3 to 1
- master: float32 [8, 55744, 128], P('section', 'dp'), may hold values from -0.75 to 0.75
- first_moment: float32 [8, 55744, 128], P('section', 'dp'), may hold values from -6 to 6
- second_moment: float32 [8, 55744, 128], P('section', 'dp'), may hold values from 0.05 to 5
- bucket_bounds: int32 [8, 49], P('section'), may hold values from 0 to 37168, as said below
- bucket_owner: int32 [8, 48], P('section'), may hold values from 0 to 15, as said below
Outputs:
- section_outputs: bfloat16 [8, 32, 16, 16, 768], P('section', 'dp')
- new_master: float32 [8, 55744, 128], P('section', 'dp')
- new_first_moment: float32 [8, 55744, 128], P('section', 'dp')
- new_second_moment: float32 [8, 55744, 128], P('section', 'dp')
Inputs may be any that keep to these rules, and one draw needn't show every extreme that they name: `roster`: each row names every slot once. `bucket_bounds`: in each block's row the bounds never fall, the first is 0 and the last is 37168. `bucket_owner`: in each block every owner is named by 3 buckets; the buckets of one owner hold at most 3484 rows together, and some owner holds exactly 3484.
All inputs are finite; a program needn't handle non-finite values.
Results may differ from a plain program's by a relative error of at most 0.028.
Values may be sent and summed in bfloat16 or wider, within the bound.
No kernel may reach another device: no remote copies, remote signals or barrier semaphores. Data moves between devices by JAX's collectives and lax.ppermute only.
A program may use at most 128 MiB of HBM per device.

v0:
```python
import jax
import jax.numpy as jnp
from jax import lax
from jax.sharding import PartitionSpec as P

GRAN = 128


beta_one = 0.9
beta_two = 0.95
learn_rate = 0.01
decay_rate = 0.1
adam_eps = 1e-08
norm_eps = 1e-06
first_fix = 1.0 - 0.9**10
second_fix = 1.0 - 0.95**10


def shifted(block, axis, distance):
    devices = range(lax.axis_size(axis))
    route = [(i - distance, i) for i in devices if i - distance in devices]
    return lax.ppermute(block, axis, route)


def depthwise(inputs, kernel):
    reach = (kernel.shape[0] - 1) // 2
    return lax.conv_general_dilated(
        inputs,
        kernel[:, :, None, :],
        (1, 1),
        ((reach, reach), (reach, reach)),
        dimension_numbers=("NHWC", "HWIO", "NHWC"),
        feature_group_count=inputs.shape[-1],
        preferred_element_type=jnp.float32,
    )


def gelu_slope(values):
    cumulative = 0.5 * (1.0 + lax.erf(values * 0.7071067811865476))
    return cumulative + values * jnp.exp(-0.5 * values * values) * 0.3989422804014327


def normalize(conv_rows):
    centred = conv_rows - jnp.mean(conv_rows, axis=-1, keepdims=True)
    inv_std = lax.rsqrt(jnp.mean(centred * centred, axis=-1, keepdims=True) + norm_eps)
    return (centred * inv_std, inv_std)


def block_forward(block_in, kernel, up_matrix, down_matrix, scale_row):
    channels = block_in.shape[-1]
    conv_rows = depthwise(block_in, kernel).reshape(-1, channels)
    normed_f, inv_std = normalize(conv_rows)
    normed = normed_f.astype(jnp.bfloat16)
    hidden_pre = jnp.dot(normed, up_matrix, preferred_element_type=jnp.float32)
    hidden = jax.nn.gelu(hidden_pre, approximate=False).astype(jnp.bfloat16)
    branch = jnp.dot(hidden, down_matrix, preferred_element_type=jnp.float32)
    block_out = block_in.reshape(-1, channels).astype(jnp.float32) + scale_row * branch
    return (block_out.astype(jnp.bfloat16).reshape(block_in.shape), conv_rows, hidden_pre, branch)


def block_backward(
    grad_out, block_in, conv_rows, hidden_pre, branch, kernel, up_matrix, down_matrix, scale_row
):
    channels = block_in.shape[-1]
    out_rows = grad_out.reshape(-1, channels).astype(jnp.float32)
    scaled = (out_rows * scale_row).astype(jnp.bfloat16)
    scale_terms = out_rows * branch
    hidden = jax.nn.gelu(hidden_pre, approximate=False).astype(jnp.bfloat16)
    grad_hidden = lax.dot_general(
        scaled, down_matrix, (((1,), (1,)), ((), ())), preferred_element_type=jnp.float32
    )
    grad_pre = (grad_hidden * gelu_slope(hidden_pre)).astype(jnp.bfloat16)
    normed_f, inv_std = normalize(conv_rows)
    normed = normed_f.astype(jnp.bfloat16)
    grad_normed = lax.dot_general(
        grad_pre, up_matrix, (((1,), (1,)), ((), ())), preferred_element_type=jnp.float32
    )
    grad_conv = inv_std * (
        grad_normed
        - jnp.mean(grad_normed, axis=-1, keepdims=True)
        - normed_f * jnp.mean(grad_normed * normed_f, axis=-1, keepdims=True)
    )
    grad_conv = grad_conv.astype(jnp.bfloat16).reshape(block_in.shape)
    back_conv = depthwise(grad_conv, kernel[::-1, ::-1])
    grad_in = (
        (out_rows + back_conv.reshape(-1, channels)).astype(jnp.bfloat16).reshape(block_in.shape)
    )
    return (grad_in, scaled, hidden, grad_pre, normed, grad_conv, scale_terms)


def kernel_grad(block_in, grad_conv, kernel):
    reach = (kernel.shape[0] - 1) // 2
    padded = jnp.pad(block_in, ((reach, reach), (reach, reach), (0, 0)))
    return lax.conv_general_dilated(
        padded[None],
        grad_conv[:, :, None, :],
        (1, 1),
        ((0, 0), (0, 0)),
        dimension_numbers=("NHWC", "HWIO", "NHWC"),
        feature_group_count=block_in.shape[-1],
        preferred_element_type=jnp.float32,
    )[0]


def owner_slots(bounds, owners, owner_id, slot_count, empty_row):
    lengths = bounds[1:] - bounds[:-1]
    mine = (owners == owner_id).astype(jnp.int32)
    taken = lengths * mine
    offsets = jnp.cumsum(taken) - taken
    slot_ids = jnp.arange(slot_count, dtype=jnp.int32)[:, None]
    hits = (
        (mine[None, :] > 0)
        & (slot_ids >= offsets[None, :])
        & (slot_ids < (offsets + lengths)[None, :])
    )
    found = jnp.sum(jnp.where(hits, bounds[:-1][None, :] + slot_ids - offsets[None, :], 0), axis=1)
    return jnp.where(jnp.any(hits, axis=1), found, empty_row)


def pass_forward(activation):
    return shifted(activation, "section", 1)


def pass_backward(gradient):
    return shifted(gradient, "section", -1)


def body(
    images,
    roster,
    cotangent,
    depth_kernel,
    up_weight,
    down_weight,
    layer_scale,
    master,
    first_moment,
    second_moment,
    bucket_bounds,
    bucket_owner,
):
    section_count = lax.axis_size("section")
    replica_count = lax.axis_size("dp")
    section_index = lax.axis_index("section")
    owner_index = lax.axis_index("dp")
    micro_count, height, breadth, channels = images.shape
    kernel = depth_kernel[0]
    up_matrix = up_weight[0]
    down_matrix = down_weight[0]
    scale_row = layer_scale[0]
    hidden_width = up_matrix.shape[1]
    positions = height * breadth
    slot_order = roster[0]
    blank_image = jnp.zeros((height, breadth, channels), jnp.bfloat16)

    def forward_slot(stash, slot, received):
        active = (slot >= 0) & (slot < micro_count)
        safe_slot = jnp.clip(slot, 0, micro_count - 1)
        first_input = images[slot_order[safe_slot]]
        block_in = jnp.where(section_index == 0, first_input, received)

        def forward_compute_slot(held):
            held_in, held_conv, held_pre, held_branch, held_out = held
            block_out, conv_rows, hidden_pre, branch = block_forward(
                block_in[None], kernel, up_matrix, down_matrix, scale_row
            )
            block_out = block_out[0]
            return (
                block_out,
                (
                    held_in.at[safe_slot].set(block_in),
                    held_conv.at[safe_slot].set(conv_rows),
                    held_pre.at[safe_slot].set(hidden_pre),
                    held_branch.at[safe_slot].set(branch),
                    held_out.at[safe_slot].set(block_out),
                ),
            )

        def forward_empty_slot(held):
            return (blank_image, held)

        return lax.cond(active, forward_compute_slot, forward_empty_slot, stash)

    def backward_slot(stash, totals, slot, received):
        active = (slot >= 0) & (slot < micro_count)
        safe_slot = jnp.clip(slot, 0, micro_count - 1)
        grad_out = jnp.where(section_index == section_count - 1, cotangent[safe_slot], received)
        held_in, held_conv, held_pre, held_branch, held_out = stash

        def backward_compute_slot(sums):
            kernel_sum, up_sum, down_sum, scale_sum = sums
            block_in = held_in[safe_slot]
            grad_in, scaled, hidden, grad_pre, normed, grad_conv, scale_terms = block_backward(
                grad_out[None],
                block_in[None],
                held_conv[safe_slot],
                held_pre[safe_slot],
                held_branch[safe_slot],
                kernel,
                up_matrix,
                down_matrix,
                scale_row,
            )
            kernel_sum = kernel_sum + kernel_grad(block_in, grad_conv[0], kernel)
            up_sum = up_sum + lax.dot_general(
                normed, grad_pre, (((0,), (0,)), ((), ())), preferred_element_type=jnp.float32
            )
            down_sum = down_sum + lax.dot_general(
                hidden, scaled, (((0,), (0,)), ((), ())), preferred_element_type=jnp.float32
            )
            scale_sum = scale_sum + jnp.sum(scale_terms, axis=0)
            return (grad_in[0], (kernel_sum, up_sum, down_sum, scale_sum))

        def backward_empty_slot(sums):
            return (blank_image, sums)

        return lax.cond(active, backward_compute_slot, backward_empty_slot, totals)

    stash = (
        jnp.zeros((micro_count, height, breadth, channels), jnp.bfloat16),
        jnp.zeros((micro_count, positions, channels), jnp.float32),
        jnp.zeros((micro_count, positions, hidden_width), jnp.float32),
        jnp.zeros((micro_count, positions, channels), jnp.float32),
        jnp.zeros((micro_count, height, breadth, channels), jnp.bfloat16),
    )
    totals = (
        jnp.zeros(kernel.shape, jnp.float32),
        jnp.zeros((channels, hidden_width), jnp.float32),
        jnp.zeros((hidden_width, channels), jnp.float32),
        jnp.zeros((channels,), jnp.float32),
    )

    def forward_tick(tick_index, loop_state):
        previous, held = loop_state
        received = pass_forward(previous)
        return forward_slot(held, tick_index - section_index, received)

    last_out, stash = lax.fori_loop(
        0, micro_count + section_count - 1, forward_tick, (blank_image, stash)
    )

    def backward_tick(tick_index, loop_state):
        previous, sums = loop_state
        received = pass_backward(previous)
        return backward_slot(
            stash, sums, tick_index - (section_count - 1 - section_index), received
        )

    last_grad, totals = lax.fori_loop(
        0, micro_count + section_count - 1, backward_tick, (blank_image, totals)
    )
    kernel_sum, up_sum, down_sum, scale_sum = totals
    flat_grad = jnp.concatenate(
        [kernel_sum.reshape(-1), up_sum.reshape(-1), down_sum.reshape(-1), scale_sum]
    ).astype(jnp.bfloat16)
    flat_grad = lax.optimization_barrier(flat_grad).astype(jnp.float32)
    row_count = flat_grad.shape[0] // GRAN
    owner_rows = -(-row_count // replica_count)
    unit_count = owner_rows * replica_count
    slot_count = master.shape[1]
    grad_rows = jnp.concatenate(
        [
            flat_grad.reshape(row_count, GRAN),
            jnp.zeros((unit_count - row_count + 1, GRAN), jnp.float32),
        ],
        axis=0,
    )
    bounds = bucket_bounds[0]
    owners = bucket_owner[0]
    summed = lax.psum(grad_rows[:unit_count].astype(jnp.bfloat16), "dp").astype(jnp.float32)
    summed = jnp.concatenate([summed, jnp.zeros((1, GRAN), jnp.float32)], axis=0)
    grad = summed[owner_slots(bounds, owners, owner_index, slot_count, unit_count)]
    grad = grad / replica_count
    new_first = beta_one * first_moment[0] + (1.0 - beta_one) * grad
    new_second = beta_two * second_moment[0] + (1.0 - beta_two) * grad * grad
    update = (
        new_first / first_fix / (jnp.sqrt(new_second / second_fix) + adam_eps)
        + decay_rate * master[0]
    )
    new_master = master[0] - learn_rate * update
    return (stash[4][None], new_master[None], new_first[None], new_second[None])


def solution(mesh):
    placed = (
        P("dp", None, None, None),
        P("dp", None),
        P("dp", None, None, None),
        P("section", None, None, None),
        P("section", None, None),
        P("section", None, None),
        P("section", None),
        P("section", "dp", None),
        P("section", "dp", None),
        P("section", "dp", None),
        P("section", None),
        P("section", None),
    )
    return jax.shard_map(
        body,
        mesh=mesh,
        in_specs=placed,
        out_specs=(
            P("section", "dp", None, None, None),
            P("section", "dp", None),
            P("section", "dp", None),
            P("section", "dp", None),
        ),
        check_vma=False,
    )
```

profile of v0, /device:TPU:0, one launch (start us, length us, event | category | flops | bytes accessed | tf_op | source)
XLA Modules:
  0.0 1258.1 jit_solution(7210364101206052478)
XLA Ops:
  9.0 3.4 broadcast_in_dim.80
  14.6 299.6 %while.52 = (s32[]{:T(128)}, bf16[16,16,768]{2,1,0:T(8,128)(2,1)}, bf16[2,16,16,768]{3,2,1,0:T(8,128)(2,1)}, f32[2,256,768]{2,1,0:T(8,128)S(1)}, f32[2,256,3072]...) while((s32[]{:T(128)}, bf16[16,16,768]{2,1,0:T(8,128)(2,1)}, ...), condition=%wide.region_7.0_spmd, body=%wide.region_0.7_spmd.sunk | while | flops 2486329600 | bytes 55546536 | solution.py:238
  14.6 3.9 collective-permute-start
  18.6 8.6 collective-permute-done
  27.2 40.8 %conditional.4 = (bf16[16,16,768]{2,1,0:T(8,128)(2,1)}, bf16[2,16,16,768]{3,2,1,0:T(8,128)(2,1)}, f32[2,256,768]{2,1,0:T(8,128)S(1)}, f32[2,256,3072]{2,1,0:T(8,...) conditional(s32[]{:T(128)} %convert_element_type.138, (bf16[2,16,16,768]{3,2,1,0:T(8,128)(2,1)}, ...), branch_computations={%region_1.1_spmd, %region_2.6_spmd} | conditional | flops 2486329600 | bytes 53973268 | solution.py:182
  35.7 8.6 fusion.152
  46.3 7.7 fusion.3
  54.0 8.6 fusion.15
  69.3 8.1 collective-permute-done
  77.4 40.8 %conditional.4 = (bf16[16,16,768]{2,1,0:T(8,128)(2,1)}, bf16[2,16,16,768]{3,2,1,0:T(8,128)(2,1)}, f32[2,256,768]{2,1,0:T(8,128)S(1)}, f32[2,256,3072]{2,1,0:T(8,...) conditional(s32[]{:T(128)} %convert_element_type.138, (bf16[2,16,16,768]{3,2,1,0:T(8,128)(2,1)}, ...), branch_computations={%region_1.1_spmd, %region_2.6_spmd} | conditional | flops 2486329600 | bytes 53973268 | solution.py:182
  85.9 8.6 fusion.152
  96.5 7.7 fusion.3
  104.2 8.6 fusion.15
  118.2 4.3 collective-permute-start
  122.5 7.2 collective-permute-done
  130.5 44.3 %collective-permute-start = (bf16[16,16,768]{2,1,0:T(8,128)(2,1)}, bf16[16,16,768]{2,1,0:T(8,128)(2,1)S(1)}, u32[]{:S(2)}, u32[]{:S(2)}) collective-permute-start(bf16[16,16,768]{2,1,0:T(8,128)(2,1)} %get-tuple-element.1440), channel_id=1, source_target_pairs={{0,16},{16,32},{32,48},{48,64},{64,80},{80,96},{96,112},{1,17},{17... | collective-permute-start | bytes 1179656 | tf_op jit(solution)/shard_map/while/body/eval_jaxpr/ppermute | solution.py:22
  174.8 6.3 collective-permute-done
  181.9 4.3 collective-permute-start
  186.2 5.6 collective-permute-done
  192.6 44.5 %collective-permute-start = (bf16[16,16,768]{2,1,0:T(8,128)(2,1)}, bf16[16,16,768]{2,1,0:T(8,128)(2,1)S(1)}, u32[]{:S(2)}, u32[]{:S(2)}) collective-permute-start(bf16[16,16,768]{2,1,0:T(8,128)(2,1)} %get-tuple-element.1440), channel_id=1, source_target_pairs={{0,16},{16,32},{32,48},{48,64},{64,80},{80,96},{96,112},{1,17},{17... | collective-permute-start | bytes 1179656 | tf_op jit(solution)/shard_map/while/body/eval_jaxpr/ppermute | solution.py:22
  237.1 5.6 collective-permute-done
  243.5 5.2 collective-permute-start
  248.7 5.6 collective-permute-done
  255.0 41.3 %collective-permute-start = (bf16[16,16,768]{2,1,0:T(8,128)(2,1)}, bf16[16,16,768]{2,1,0:T(8,128)(2,1)S(1)}, u32[]{:S(2)}, u32[]{:S(2)}) collective-permute-start(bf16[16,16,768]{2,1,0:T(8,128)(2,1)} %get-tuple-element.1440), channel_id=1, source_target_pairs={{0,16},{16,32},{32,48},{48,64},{64,80},{80,96},{96,112},{1,17},{17... | collective-permute-start | bytes 1179656 | tf_op jit(solution)/shard_map/while/body/eval_jaxpr/ppermute | solution.py:22
  296.4 5.7 collective-permute-done
  302.8 5.1 collective-permute-start
  307.9 5.6 collective-permute-done
  315.0 4.8 broadcast_in_dim.83
  319.8 4.3 broadcast_in_dim.84
  324.7 649.3 %while.53 = (s32[]{:T(128)}, bf16[16,16,768]{2,1,0:T(8,128)(2,1)}, f32[7,7,768]{2,1,0:T(8,128)S(1)}, f32[768,3072]{1,0:T(8,128)}, f32[3072,768]{1,0:T(8,128)}, /...) while((s32[]{:T(128)}, bf16[16,16,768]{2,1,0:T(8,128)(2,1)}, ...), condition=%wide.region_16.0_spmd, body=%wide.region_8.16_spmd.sunk | while | flops 4936299520 | bytes 245418480 | solution.py:249
  326.3 48.5 %collective-permute-done.1 = bf16[16,16,768]{2,1,0:T(8,128)(2,1)S(1)} collective-permute-done((bf16[16,16,768]{2,1,0:T(8,128)(2,1)}, bf16[16,16,768]{2,1,0:T(8,128)(2,1)S(1)}, u32[]{:S(2)}, u32[]{:S(2)}) %collective-permute-start.1) | collective-permute-done | bytes 393248 | tf_op jit(solution)/shard_map/while/body/eval_jaxpr/ppermute | solution.py:22
  376.9 8.6 collective-permute-done.1
  387.6 55.5 %collective-permute-done.1 = bf16[16,16,768]{2,1,0:T(8,128)(2,1)S(1)} collective-permute-done((bf16[16,16,768]{2,1,0:T(8,128)(2,1)}, bf16[16,16,768]{2,1,0:T(8,128)(2,1)S(1)}, u32[]{:S(2)}, u32[]{:S(2)}) %collective-permute-start.1) | collective-permute-done | bytes 393248 | tf_op jit(solution)/shard_map/while/body/eval_jaxpr/ppermute | solution.py:22
  445.2 8.6 collective-permute-done.1
  455.9 51.1 %collective-permute-done.1 = bf16[16,16,768]{2,1,0:T(8,128)(2,1)S(1)} collective-permute-done((bf16[16,16,768]{2,1,0:T(8,128)(2,1)}, bf16[16,16,768]{2,1,0:T(8,128)(2,1)S(1)}, u32[]{:S(2)}, u32[]{:S(2)}) %collective-permute-start.1) | collective-permute-done | bytes 393248 | tf_op jit(solution)/shard_map/while/body/eval_jaxpr/ppermute | solution.py:22
  509.0 8.6 collective-permute-done.1
  519.7 33.3 %collective-permute-done.1 = bf16[16,16,768]{2,1,0:T(8,128)(2,1)S(1)} collective-permute-done((bf16[16,16,768]{2,1,0:T(8,128)(2,1)}, bf16[16,16,768]{2,1,0:T(8,128)(2,1)S(1)}, u32[]{:S(2)}, u32[]{:S(2)}) %collective-permute-start.1) | collective-permute-done | bytes 393248 | tf_op jit(solution)/shard_map/while/body/eval_jaxpr/ppermute | solution.py:22
  555.1 317.4 %collective-permute-done.1 = bf16[16,16,768]{2,1,0:T(8,128)(2,1)S(1)} collective-permute-done((bf16[16,16,768]{2,1,0:T(8,128)(2,1)}, bf16[16,16,768]{2,1,0:T(8,128)(2,1)S(1)}, u32[]{:S(2)}, u32[]{:S(2)}) %collective-permute-start.1) | collective-permute-done | bytes 393248 | tf_op jit(solution)/shard_map/while/body/eval_jaxpr/ppermute | solution.py:22
  872.5 45.3 %conditional.5 = (bf16[16,16,768]{2,1,0:T(8,128)(2,1)}, f32[7,7,768]{2,1,0:T(8,128)S(1)}, f32[768,3072]{1,0:T(8,128)}, f32[3072,768]{1,0:T(8,128)}, f32[768]{0:T(1024)}) conditional(s32[]{:T(128)} %convert_element_type.139, (f32[7,7,768]{2,1,0:T(8,128)S(1)}, f32[768,3072]{1,0:T(8,128)}, f32[3072,768]{1,0:T(8,128)}, f32[768]{0:T(1024)}) %tuple.137, ...), branch_computations={%region_9.9_spmd, %region_10.15_spmd} | conditional | flops 4936299520 | bytes 243845184 | solution.py:217
  875.5 6.4 fusion.51
  884.5 3.4 rev.4
  887.9 5.8 fusion.107
  896.1 7.3 fusion.100
  905.8 8.3 convolution_add_fusion
  919.1 9.5 collective-permute-done.1
  928.5 45.3 %conditional.5 = (bf16[16,16,768]{2,1,0:T(8,128)(2,1)}, f32[7,7,768]{2,1,0:T(8,128)S(1)}, f32[768,3072]{1,0:T(8,128)}, f32[3072,768]{1,0:T(8,128)}, f32[768]{0:T(1024)}) conditional(s32[]{:T(128)} %convert_element_type.139, (f32[7,7,768]{2,1,0:T(8,128)S(1)}, f32[768,3072]{1,0:T(8,128)}, f32[3072,768]{1,0:T(8,128)}, f32[768]{0:T(1024)}) %tuple.137, ...), branch_computations={%region_9.9_spmd, %region_10.15_spmd} | conditional | flops 4936299520 | bytes 243845184 | solution.py:217
  931.6 6.4 fusion.51
  940.6 3.4 rev.4
  944.0 5.8 fusion.107
  952.2 7.3 fusion.100
  961.9 8.3 convolution_add_fusion
  974.7 6.3 convert.25
  981.0 9.2 reshape.381
  990.3 4.7 convert_bitcast_fusion
  995.0 3.6 copy.62
  998.6 16.7 %pad_maximum_fusion = bf16[4756992]{0:T(1024)(128)(2,1)S(1)} fusion(bf16[768]{0:T(1024)(128)(2,1)S(1)} %convert.26, bf16[2359296]{0:T(1024)(128)(2,1)} %reshape.381, bf16[2359296]{0:T(1024)(128)(2,1)} %bitcast.124, bf16[37632]{0:T(1024)(128)(2,1)S(1)} %reshape.379), kind=kLoop, calls=%fused_computation.200 | loop fusion | flops 38055936 | bytes 19027968 | tf_op jit(solution)/shard_map/concatenate | solution.py:253
  1015.3 6.1 pad_slice_fusion
  1023.2 165.1 %all-reduce.5.cloned.1.call-done = bf16[37168,128]{1,0:T(8,128)(2,1)} async-done(((bf16[37168,128]{1,0:T(8,128)(2,1)}), bf16[37168,128]{1,0:T(8,128)(2,1)}) %all-reduce.5.cloned.1.call-update) | async-done | bytes 9515024 | tf_op jit(solution)/shard_map/psum | solution.py:270
  1188.3 10.9 pad_convert_fusion
  1199.2 12.3 gather_fusion
  1211.5 4.0 multiply_subtract_fusion
  1215.4 12.0 copy.56
  1227.5 11.8 copy.57
  1239.3 11.8 copy.58
  (220 shorter events, 97.6 us)
Async XLA Ops:
  7.2 1181.1 %all-reduce.5.cloned.1.call-start = ((), (), s32[]{:S(2)}) async-start(), calls=%async_computation | async-start | bytes 19030016 | tf_op jit(solution)/shard_map/psum | solution.py:270
  9.0 5.6 copy-start.11
  14.6 12.6 %collective-permute-start = (bf16[16,16,768]{2,1,0:T(8,128)(2,1)}, bf16[16,16,768]{2,1,0:T(8,128)(2,1)S(1)}, u32[]{:S(2)}, u32[]{:S(2)}) collective-permute-start(bf16[16,16,768]{2,1,0:T(8,128)(2,1)} %get-tuple-element.1440), channel_id=1, source_target_pairs={{0,16},{16,32},{32,48},{48,64},{64,80},{80,96},{96,112},{1,17},{17... | collective-permute-start | bytes 1179656 | tf_op jit(solution)/shard_map/while/body/eval_jaxpr/ppermute | solution.py:22
  33.6 10.7 copy-start.2
  46.1 7.9 slice-start.10
  46.2 7.7 copy-start.3
  46.3 7.7 slice-start.11
  68.0 9.4 collective-permute-start
  83.8 10.7 copy-start.2
  96.3 7.9 slice-start.10
  96.4 7.7 copy-start.3
  96.4 7.7 slice-start.11
  118.2 11.5 collective-permute-start
  130.5 50.7 %collective-permute-start = (bf16[16,16,768]{2,1,0:T(8,128)(2,1)}, bf16[16,16,768]{2,1,0:T(8,128)(2,1)S(1)}, u32[]{:S(2)}, u32[]{:S(2)}) collective-permute-start(bf16[16,16,768]{2,1,0:T(8,128)(2,1)} %get-tuple-element.1440), channel_id=1, source_target_pairs={{0,16},{16,32},{32,48},{48,64},{64,80},{80,96},{96,112},{1,17},{17... | collective-permute-start | bytes 1179656 | tf_op jit(solution)/shard_map/while/body/eval_jaxpr/ppermute | solution.py:22
  181.9 9.9 collective-permute-start
  192.6 50.1 %collective-permute-start = (bf16[16,16,768]{2,1,0:T(8,128)(2,1)}, bf16[16,16,768]{2,1,0:T(8,128)(2,1)S(1)}, u32[]{:S(2)}, u32[]{:S(2)}) collective-permute-start(bf16[16,16,768]{2,1,0:T(8,128)(2,1)} %get-tuple-element.1440), channel_id=1, source_target_pairs={{0,16},{16,32},{32,48},{48,64},{64,80},{80,96},{96,112},{1,17},{17... | collective-permute-start | bytes 1179656 | tf_op jit(solution)/shard_map/while/body/eval_jaxpr/ppermute | solution.py:22
  243.5 10.8 collective-permute-start
  255.0 47.0 %collective-permute-start = (bf16[16,16,768]{2,1,0:T(8,128)(2,1)}, bf16[16,16,768]{2,1,0:T(8,128)(2,1)S(1)}, u32[]{:S(2)}, u32[]{:S(2)}) collective-permute-start(bf16[16,16,768]{2,1,0:T(8,128)(2,1)} %get-tuple-element.1440), channel_id=1, source_target_pairs={{0,16},{16,32},{32,48},{48,64},{64,80},{80,96},{96,112},{1,17},{17... | collective-permute-start | bytes 1179656 | tf_op jit(solution)/shard_map/while/body/eval_jaxpr/ppermute | solution.py:22
  302.8 10.7 collective-permute-start
  325.0 49.8 %collective-permute-start.1 = (bf16[16,16,768]{2,1,0:T(8,128)(2,1)}, bf16[16,16,768]{2,1,0:T(8,128)(2,1)S(1)}, u32[]{:S(2)}, u32[]{:S(2)}) collective-permute-start(bf16[16,16,768]{2,1,0:T(8,128)(2,1)} %get-tuple-element.1496), channel_id=1, source_target_pairs={{16,0},{32,16},{48,32},{64,48},{80,64},{96,80},{112,96},{17,1},{33... | collective-permute-start | bytes 1179656 | tf_op jit(solution)/shard_map/while/body/eval_jaxpr/ppermute | solution.py:22
  375.6 9.9 collective-permute-start.1
  386.3 56.8 %collective-permute-start.1 = (bf16[16,16,768]{2,1,0:T(8,128)(2,1)}, bf16[16,16,768]{2,1,0:T(8,128)(2,1)S(1)}, u32[]{:S(2)}, u32[]{:S(2)}) collective-permute-start(bf16[16,16,768]{2,1,0:T(8,128)(2,1)} %get-tuple-element.1496), channel_id=1, source_target_pairs={{16,0},{32,16},{48,32},{64,48},{80,64},{96,80},{112,96},{17,1},{33... | collective-permute-start | bytes 1179656 | tf_op jit(solution)/shard_map/while/body/eval_jaxpr/ppermute | solution.py:22
  443.9 9.9 collective-permute-start.1
  454.6 52.4 %collective-permute-start.1 = (bf16[16,16,768]{2,1,0:T(8,128)(2,1)}, bf16[16,16,768]{2,1,0:T(8,128)(2,1)S(1)}, u32[]{:S(2)}, u32[]{:S(2)}) collective-permute-start(bf16[16,16,768]{2,1,0:T(8,128)(2,1)} %get-tuple-element.1496), channel_id=1, source_target_pairs={{16,0},{32,16},{48,32},{64,48},{80,64},{96,80},{112,96},{17,1},{33... | collective-permute-start | bytes 1179656 | tf_op jit(solution)/shard_map/while/body/eval_jaxpr/ppermute | solution.py:22
  507.7 9.9 collective-permute-start.1
  518.4 34.6 %collective-permute-start.1 = (bf16[16,16,768]{2,1,0:T(8,128)(2,1)}, bf16[16,16,768]{2,1,0:T(8,128)(2,1)S(1)}, u32[]{:S(2)}, u32[]{:S(2)}) collective-permute-start(bf16[16,16,768]{2,1,0:T(8,128)(2,1)} %get-tuple-element.1496), channel_id=1, source_target_pairs={{16,0},{32,16},{48,32},{64,48},{80,64},{96,80},{112,96},{17,1},{33... | collective-permute-start | bytes 1179656 | tf_op jit(solution)/shard_map/while/body/eval_jaxpr/ppermute | solution.py:22
  553.8 318.7 %collective-permute-start.1 = (bf16[16,16,768]{2,1,0:T(8,128)(2,1)}, bf16[16,16,768]{2,1,0:T(8,128)(2,1)S(1)}, u32[]{:S(2)}, u32[]{:S(2)}) collective-permute-start(bf16[16,16,768]{2,1,0:T(8,128)(2,1)} %get-tuple-element.1496), channel_id=1, source_target_pairs={{16,0},{32,16},{48,32},{64,48},{80,64},{96,80},{112,96},{17,1},{33... | collective-permute-start | bytes 1179656 | tf_op jit(solution)/shard_map/while/body/eval_jaxpr/ppermute | solution.py:22
  872.5 0.7 copy-start.5
  875.4 6.5 slice-start.3
  875.5 6.4 slice-start.4
  893.8 2.2 copy-start.4
  894.7 11.0 slice-start.5
  896.0 7.5 slice-start
  896.0 7.4 copy-start.6
  896.0 7.4 slice-start.1
  896.0 7.4 slice-start.2
  896.0 9.7 slice-start.6
  896.1 9.7 slice-start.7
  896.1 9.7 slice-start.8
  903.5 2.2 copy-start.7
  903.5 2.3 slice-start.9
  905.7 8.4 copy-start
  905.8 12.0 copy-start.8
  914.1 3.7 copy-start.1
  917.8 10.8 collective-permute-start.1
  928.5 0.7 copy-start.5
  931.5 6.5 slice-start.3
  931.6 6.4 slice-start.4
  949.9 2.2 copy-start.4
  950.8 11.0 slice-start.5
  952.1 7.5 slice-start
  952.1 7.4 copy-start.6
  952.1 7.4 slice-start.1
  952.1 7.4 slice-start.2
  952.1 9.7 slice-start.6
  952.1 9.7 slice-start.7
  952.2 9.7 slice-start.8
  959.5 2.2 copy-start.7
  959.6 2.3 slice-start.9
  961.8 8.4 copy-start
  961.9 12.0 copy-start.8
  970.2 3.7 copy-start.1
  1021.4 0.7 copy-start.9
  1021.4 0.7 copy-start.10
Sparse Core Ops, SparseCore 0:
  1021.6 166.6 all-reduce.4
where the time goes:
time: 1270 us; the launch traced here: 1260 us
  waiting for transfers between devices  764 us (60%)
  starting transfers between devices  166 us (13%)
  matrix products  113 us (9%)
  local copies, waits for them, and re-layouts  112 us (9%)
  other arithmetic  82.5 us (6%)
  between operations  14.4 us (1%)
    ppermute x18, waiting for transfers between devices, shifted(): return lax.ppermute(block, axis, route)  599 us
    ppermute x18, starting transfers between devices, shifted(): return lax.ppermute(block, axis, route)  166 us
    psum x1, waiting for transfers between devices, body(): lax.psum(grad_rows[:unit_count].astype(jnp.bfloat16), 'dp')  165 us
    unnamed x10, local copies, waits for them, and re-layouts  39.8 us
    conv_general_dilated x4, matrix products, depthwise(): lax.conv_general_dilated(inputs, kernel[:, :, None, :], (1, 1), ((reach,...  28.9 us
  transfers between devices with their start and end apart: 19, of which 19 were waited for; matrix products, arithmetic and copies ran while one was open for 0% of the time, Pallas kernels for 0%

commit v1 on v0

v1 whole, which is shorter than its diff:
```python
import functools

import jax
import jax.numpy as jnp
from jax import lax
from jax.experimental import pallas as pl
from jax.experimental.pallas import tpu as pltpu
from jax.sharding import PartitionSpec as P

beta_one = 0.9
beta_two = 0.95
learn_rate = 0.01
decay_rate = 0.1
adam_eps = 1e-08
norm_eps = 1e-06
first_fix = 1.0 - 0.9**10
second_fix = 1.0 - 0.95**10

LANES = 128
MARGIN = 8
STEP = 64
F32 = jnp.float32
BF16 = jnp.bfloat16
ANY = pl.BlockSpec(memory_space=pl.ANY)
SMEM = pl.BlockSpec(memory_space=pltpu.SMEM)
VMEM = pl.BlockSpec(memory_space=pltpu.VMEM)
PARAMS = pltpu.CompilerParams(vmem_limit_bytes=56 * 1024 * 1024)


def rolled(count):
    def wrap(fn):
        lax.fori_loop(0, count, lambda i, c: (fn(i), c)[1], 0)

    return wrap


def pad_map(pad, image, reach, height, breadth):
    chunks = pad.shape[0]
    for c in range(chunks):
        for r in range(pad.shape[1]):
            if r < reach or r >= reach + height:
                pad[c, r] = jnp.zeros(pad.shape[2:], F32)
            else:
                pad[c, r, :MARGIN] = jnp.zeros((MARGIN, LANES), F32)
                pad[c, r, MARGIN + breadth :] = jnp.zeros((MARGIN, LANES), F32)
                pad[c, r, MARGIN : MARGIN + breadth] = image[
                    (r - reach) * breadth : (r - reach + 1) * breadth,
                    c * LANES : (c + 1) * LANES,
                ].astype(F32)


def depthwise(pad, taps, result, side, height, breadth, flip):
    reach = (side - 1) // 2
    halves = breadth // 8

    @rolled(pad.shape[0])
    def _(c):
        sums = [[None] * halves for _ in range(height)]
        for b in range(side):
            weights = []
            for a in range(side):
                t = a * side + b
                t = side * side - 1 - t if flip else t
                weights.append(jnp.broadcast_to(taps[c, pl.ds(t, 1), :], (8, LANES)))
            for r in range(height + 2 * reach):
                for w in range(halves):
                    value = pad[c, r, pl.ds(MARGIN - reach + b + 8 * w, 8), :]
                    for a in range(side):
                        i = r - a
                        if 0 <= i < height:
                            term = value * weights[a]
                            sums[i][w] = term if sums[i][w] is None else sums[i][w] + term
        columns = pl.ds(pl.multiple_of(c * LANES, LANES), LANES)
        for i in range(height):
            for w in range(halves):
                result[pl.ds(i * breadth + 8 * w, 8), columns] = sums[i][w]


def forward_kernel(
    dims, sc, xr, images, taps, scale, up, down, *refs
):
    side, height, breadth, width = dims
    out_o, x_o, n_o, istd_o, hid_o, slope_o, branch_o, y = refs[7:15]
    xv, pad, conv, nv, iv, upv, downv, hv, sv, acc, yv, sems = refs[15:]
    positions, channels = xv.shape
    reach = (side - 1) // 2

    @pl.when(sc[0] > 0)
    def _():
        slot = sc[2]
        up_in = pltpu.make_async_copy(up, upv, sems.at[0])
        down_in = pltpu.make_async_copy(down, downv, sems.at[1])

        @pl.when(sc[1] > 0)
        def _():
            cp = pltpu.make_async_copy(images.at[sc[3]], xv, sems.at[2])
            cp.start()
            up_in.start()
            down_in.start()
            cp.wait()

        @pl.when(sc[1] == 0)
        def _():
            cp = pltpu.make_async_copy(xr, xv, sems.at[2])
            cp.start()
            up_in.start()
            down_in.start()
            cp.wait()

        x_out = pltpu.make_async_copy(xv, x_o.at[slot], sems.at[3])
        x_out.start()
        pad_map(pad, xv, reach, height, breadth)
        depthwise(pad, taps, conv, side, height, breadth, False)
        block = 64
        for p in range(0, positions, block):
            rows = conv[p : p + block, :]
            centred = rows - jnp.mean(rows, axis=-1, keepdims=True)
            inv_std = lax.rsqrt(jnp.mean(centred * centred, axis=-1, keepdims=True) + norm_eps)
            nv[p : p + block, :] = (centred * inv_std).astype(BF16)
            iv[p : p + block, :] = jnp.broadcast_to(inv_std, (block, LANES))
        n_out = pltpu.make_async_copy(nv, n_o.at[slot], sems.at[4])
        n_out.start()
        i_out = pltpu.make_async_copy(iv, istd_o.at[slot], sems.at[5])
        i_out.start()
        up_in.wait()
        down_in.wait()
        step = 512
        for k in range(0, width, step):
            pre = jnp.dot(nv[...], upv[:, k : k + step], preferred_element_type=F32)
            cdf = 0.5 * (1.0 + lax.erf(pre * 0.7071067811865476))
            hidden = (pre * cdf).astype(BF16)
            hv[:, k : k + step] = hidden
            bell = jnp.exp(-0.5 * pre * pre) * 0.3989422804014327
            sv[:, k : k + step] = (cdf + pre * bell).astype(BF16)
            part = jnp.dot(hidden, downv[k : k + step, :], preferred_element_type=F32)
            if k == 0:
                acc[...] = part
            else:
                acc[...] += part
        yv[...] = (xv[...].astype(F32) + scale[...] * acc[...]).astype(BF16)
        y_out = pltpu.make_async_copy(yv, y, sems.at[6])
        y_out.start()
        o_out = pltpu.make_async_copy(yv, out_o.at[slot], sems.at[7])
        o_out.start()
        h_out = pltpu.make_async_copy(hv, hid_o.at[slot], sems.at[8])
        h_out.start()
        s_out = pltpu.make_async_copy(sv, slope_o.at[slot], sems.at[9])
        s_out.start()
        b_out = pltpu.make_async_copy(acc, branch_o.at[slot], sems.at[10])
        b_out.start()
        for cp in (x_out, n_out, i_out, y_out, o_out, h_out, s_out, b_out):
            cp.wait()


def backward_kernel(
    dims, sc, gr, cotangent, taps, scale, up, down, n_i, istd_i, slope_i, *refs
):
    side, height, breadth, width = dims
    go_o, gp_o, gc_o, g_in = refs[3:7]
    gv, pad, conv, nv, iv, upv, downv, sv, gpv, acc, scaled, gcv, yv, sems = refs[7:]
    positions, channels = gv.shape
    reach = (side - 1) // 2

    @pl.when(sc[0] > 0)
    def _():
        slot = sc[2]
        down_in = pltpu.make_async_copy(down, downv, sems.at[0])
        up_in = pltpu.make_async_copy(up, upv, sems.at[1])
        s_in = pltpu.make_async_copy(slope_i.at[slot], sv, sems.at[3])
        n_in = pltpu.make_async_copy(n_i.at[slot], nv, sems.at[4])
        i_in = pltpu.make_async_copy(istd_i.at[slot], iv, sems.at[5])

        def begin(source):
            cp = pltpu.make_async_copy(source, gv, sems.at[2])
            cp.start()
            down_in.start()
            s_in.start()
            up_in.start()
            n_in.start()
            i_in.start()
            cp.wait()

        @pl.when(sc[1] > 0)
        def _():
            begin(cotangent.at[slot])

        @pl.when(sc[1] == 0)
        def _():
            begin(gr)

        go_out = pltpu.make_async_copy(gv, go_o.at[slot], sems.at[6])
        go_out.start()
        scaled[...] = (gv[...].astype(F32) * scale[...]).astype(BF16)
        down_in.wait()
        s_in.wait()
        up_in.wait()
        step = 512
        across = (((1,), (1,)), ((), ()))
        for k in range(0, width, step):
            grad_hidden = lax.dot_general(
                scaled[...], downv[k : k + step, :], across, preferred_element_type=F32
            )
            grad_pre = (grad_hidden * sv[:, k : k + step].astype(F32)).astype(BF16)
            gpv[:, k : k + step] = grad_pre
            part = lax.dot_general(
                grad_pre, upv[:, k : k + step], across, preferred_element_type=F32
            )
            if k == 0:
                acc[...] = part
            else:
                acc[...] += part
        gp_out = pltpu.make_async_copy(gpv, gp_o.at[slot], sems.at[7])
        gp_out.start()
        n_in.wait()
        i_in.wait()
        block = 64
        for p in range(0, positions, block):
            rows = acc[p : p + block, :]
            normed = nv[p : p + block, :].astype(F32)
            mean = jnp.mean(rows, axis=-1, keepdims=True)
            slant = jnp.mean(rows * normed, axis=-1, keepdims=True)
            gcv[p : p + block, :] = (
                iv[p : p + block, :1] * (rows - mean - normed * slant)
            ).astype(BF16)
        gc_out = pltpu.make_async_copy(gcv, gc_o.at[slot], sems.at[8])
        gc_out.start()

        @pl.when(sc[3] > 0)
        def _():
            pad_map(pad, gcv, reach, height, breadth)
            depthwise(pad, taps, conv, side, height, breadth, True)
            yv[...] = (gv[...].astype(F32) + conv[...]).astype(BF16)
            cp = pltpu.make_async_copy(yv, g_in, sems.at[9])
            cp.start()
            cp.wait()

        for cp in (go_out, gp_out, gc_out):
            cp.wait()


def weight_kernel(
    dims, bounds, owners, scale, x_i, n_i, hid_i, branch_i, go_i, gp_i, gc_i, slots_o, *refs
):
    side, height, breadth, width, real_rows, owner_count, buckets = dims
    (xv, nv, hv, bv, gv, gpv, gcv, scaled, pad, flat, stage, ready, starts, lengths, counts, sems) = refs
    micro, positions, channels = x_i.shape
    reach = (side - 1) // 2
    chunks = channels // LANES
    rows = micro * positions
    tap_rows = side * side * chunks
    up_rows = channels * (width // LANES)
    down_base = tap_rows + up_rows
    scale_base = down_base + up_rows
    copies = []
    for q, (src, dst) in enumerate(
        ((n_i, nv), (gp_i, gpv), (go_i, gv), (hid_i, hv), (x_i, xv), (gc_i, gcv), (branch_i, bv))
    ):
        for m in range(micro):
            cp = pltpu.make_async_copy(
                src.at[m], dst.at[pl.ds(m * positions, positions)], sems.at[q * micro + m]
            )
            cp.start()
            copies.append(cp)
    for d in range(owner_count):
        counts[d] = 0

    @rolled(buckets)
    def _(b):
        d = owners[b]
        at = d * (buckets // owner_count) + counts[d]
        starts[at] = bounds[b]
        lengths[at] = bounds[b + 1] - bounds[b]
        counts[d] = counts[d] + 1

    for cp in copies:
        cp.wait()
    along = (((0,), (0,)), ((), ()))
    scaled[...] = (gv[...].astype(F32) * scale[...]).astype(BF16)
    for j in range(0, width // LANES, 2):
        part = lax.dot_general(
            nv[...], gpv[:, j * LANES : (j + 2) * LANES], along, preferred_element_type=F32
        )
        for q in range(2):
            flat[pl.ds(tap_rows + j + q, channels, stride=width // LANES), :] = part[
                :, q * LANES : (q + 1) * LANES
            ]
    for j in range(0, chunks, 2):
        part = lax.dot_general(
            hv[...], scaled[:, j * LANES : (j + 2) * LANES], along, preferred_element_type=F32
        )
        for q in range(2):
            flat[pl.ds(down_base + j + q, width, stride=chunks), :] = part[
                :, q * LANES : (q + 1) * LANES
            ]
    terms = jnp.sum(gv[...].astype(F32) * bv[...], axis=0, keepdims=True)
    for c in range(chunks):
        flat[pl.ds(scale_base + c, 1), :] = terms[:, c * LANES : (c + 1) * LANES]
    tail = flat.shape[0] - scale_base - chunks
    flat[pl.ds(scale_base + chunks, tail), :] = jnp.zeros((tail, LANES), F32)
    halves = breadth // 8
    for m in range(micro):
        pad_map(pad, xv.at[pl.ds(m * positions, positions)], reach, height, breadth)

        @rolled(chunks)
        def _(c):
            columns = pl.ds(pl.multiple_of(c * LANES, LANES), LANES)
            grads = [
                gcv[pl.ds(m * positions + 16 * i, 16), columns].astype(F32)
                for i in range(positions // 16)
            ]
            for b in range(side):
                sums = [None] * side
                for r in range(reach, height + reach):
                    for w in range(halves):
                        value = pad[c, r, pl.ds(MARGIN - reach + b + 8 * w, 8), :]
                        for a in range(side):
                            i = r - a
                            if 0 <= i < height:
                                p = i * breadth + 8 * w
                                term = value * grads[p // 16][p % 16 : p % 16 + 8]
                                sums[a] = term if sums[a] is None else sums[a] + term
                for a in range(side):
                    total = jnp.sum(sums[a], axis=0, keepdims=True)
                    at = pl.ds((a * side + b) * chunks + c, 1)
                    if m == 0:
                        flat[at, :] = total
                    else:
                        flat[at, :] += total

    share = ready.shape[1]

    def out_copy(d, q):
        return pltpu.make_async_copy(ready.at[q], slots_o.at[d], sems.at[7 * micro + q])

    @rolled(owner_count)
    def _(d):
        q = lax.rem(d, 2)
        offset = 0
        for k in range(buckets // owner_count):
            at = d * (buckets // owner_count) + k
            start, length = starts[at], lengths[at]
            here = offset

            def move(i, c, start=start, here=here):
                stage[pl.ds(here + STEP * i, STEP), :] = flat[pl.ds(start + STEP * i, STEP), :]
                return c

            lax.fori_loop(0, lax.div(length + STEP - 1, STEP), move, 0)
            offset = offset + length

        def clear(i, c):
            stage[pl.ds(offset + STEP * i, STEP), :] = jnp.zeros((STEP, LANES), F32)
            return c

        lax.fori_loop(0, lax.div(share - offset + STEP - 1, STEP), clear, 0)

        @pl.when(d >= 2)
        def _():
            out_copy(d - 2, q).wait()

        ready[q] = stage[:share, :].astype(BF16)
        out_copy(d, q).start()

    for d in range(owner_count - 2, owner_count):
        out_copy(d, d % 2).wait()


def adam_kernel(count, replicas, g_i, m_i, f_i, s_i, m_o, f_o, s_o, grads):
    @pl.when(pl.program_id(0) == 0)
    def _():
        grads[...] = g_i[...].astype(F32) * (1.0 / replicas)

    base = pl.program_id(0) * (4 * count)
    for k in range(count):
        grad = grads[pl.ds(base + 4 * k, 4), :]
        new_first = beta_one * f_i[k] + (1.0 - beta_one) * grad
        new_second = beta_two * s_i[k] + (1.0 - beta_two) * grad * grad
        update = (
            new_first / first_fix / (jnp.sqrt(new_second / second_fix) + adam_eps)
            + decay_rate * m_i[k]
        )
        m_o[k] = m_i[k] - learn_rate * update
        f_o[k] = new_first
        s_o[k] = new_second


def blank(shapes):
    def kernel(*refs):
        pass

    return pl.pallas_call(
        kernel, out_shape=shapes, out_specs=[ANY] * len(shapes), name="blank"
    )()


def body(
    images,
    roster,
    cotangent,
    depth_kernel,
    up_weight,
    down_weight,
    layer_scale,
    master,
    first_moment,
    second_moment,
    bucket_bounds,
    bucket_owner,
):
    sections = lax.axis_size("section")
    replicas = lax.axis_size("dp")
    section = lax.axis_index("section")
    micro, height, breadth, channels = images.shape
    side = depth_kernel.shape[1]
    width = up_weight.shape[2]
    positions = height * breadth
    chunks = channels // LANES
    up, down = up_weight[0], down_weight[0]
    taps = (
        depth_kernel[0].astype(F32).reshape(side * side, chunks, LANES).transpose(1, 0, 2)
    )
    images = images.reshape(micro, positions, channels)
    cotangent = cotangent.reshape(micro, positions, channels)
    sds = jax.ShapeDtypeStruct
    act = sds((micro, positions, channels), BF16)
    wide = sds((micro, positions, width), BF16)
    one = sds((positions, channels), BF16)
    spread = sds((micro, positions, LANES), F32)
    full = sds((micro, positions, channels), F32)
    pad_shape = (chunks, height + side - 1, breadth + 2 * MARGIN, LANES)
    dims = (side, height, breadth, width)

    kept = (act, act, act, spread, wide, wide, full)
    forward_call = pl.pallas_call(
        functools.partial(forward_kernel, dims),
        out_shape=(*kept, one),
        in_specs=[SMEM, ANY, ANY, VMEM, VMEM, ANY, ANY] + [ANY] * len(kept),
        out_specs=[ANY] * (len(kept) + 1),
        input_output_aliases={7 + q: q for q in range(len(kept))},
        scratch_shapes=[
            pltpu.VMEM((positions, channels), BF16),
            pltpu.VMEM(pad_shape, F32),
            pltpu.VMEM((positions, channels), F32),
            pltpu.VMEM((positions, channels), BF16),
            pltpu.VMEM((positions, LANES), F32),
            pltpu.VMEM((channels, width), BF16),
            pltpu.VMEM((width, channels), BF16),
            pltpu.VMEM((positions, width), BF16),
            pltpu.VMEM((positions, width), BF16),
            pltpu.VMEM((positions, channels), F32),
            pltpu.VMEM((positions, channels), BF16),
            pltpu.SemaphoreType.DMA((11,)),
        ],
        compiler_params=PARAMS,
        name="block_forward",
    )
    saved = (act, wide, act)
    backward_call = pl.pallas_call(
        functools.partial(backward_kernel, dims),
        out_shape=(*saved, one),
        in_specs=[SMEM, ANY, ANY, VMEM, VMEM, ANY, ANY, ANY, ANY, ANY] + [ANY] * len(saved),
        out_specs=[ANY] * (len(saved) + 1),
        input_output_aliases={10 + q: q for q in range(len(saved))},
        scratch_shapes=[
            pltpu.VMEM((positions, channels), BF16),
            pltpu.VMEM(pad_shape, F32),
            pltpu.VMEM((positions, channels), F32),
            pltpu.VMEM((positions, channels), BF16),
            pltpu.VMEM((positions, LANES), F32),
            pltpu.VMEM((channels, width), BF16),
            pltpu.VMEM((width, channels), BF16),
            pltpu.VMEM((positions, width), BF16),
            pltpu.VMEM((positions, width), BF16),
            pltpu.VMEM((positions, channels), F32),
            pltpu.VMEM((positions, channels), BF16),
            pltpu.VMEM((positions, channels), BF16),
            pltpu.VMEM((positions, channels), BF16),
            pltpu.SemaphoreType.DMA((10,)),
        ],
        compiler_params=PARAMS,
        name="block_backward",
    )
    made = blank((*kept, one, *saved, one))
    stash, received = tuple(made[: len(kept)]), made[len(kept)]
    grads, returned = tuple(made[len(kept) + 1 : -1]), made[-1]
    route = [(i, i + 1) for i in range(sections - 1)]
    back_route = [(i + 1, i) for i in range(sections - 1)]
    ticks = micro + sections - 1

    def forward_tick(tick, received, stash):
        slot = tick - section
        active = (slot >= 0) & (slot < micro)
        slot = jnp.clip(slot, 0, micro - 1)
        sc = jnp.stack(
            [active.astype(jnp.int32), (section == 0).astype(jnp.int32), slot, roster[0, slot]]
        )
        *stash, y = forward_call(
            sc, received, images, taps, layer_scale, up, down, *stash
        )
        return tuple(stash), y

    def forward_loop(tick, state):
        received, stash = state
        stash, y = forward_tick(tick, received, stash)
        return lax.ppermute(y, "section", route), stash

    received, stash = lax.fori_loop(0, ticks - 1, forward_loop, (received, stash))
    stash, _ = forward_tick(ticks - 1, received, stash)
    outputs, x_s, n_s, istd_s, hid_s, slope_s, branch_s = stash

    def backward_tick(tick, returned, grads):
        slot = tick - (sections - 1 - section)
        active = (slot >= 0) & (slot < micro)
        slot = jnp.clip(slot, 0, micro - 1)
        sc = jnp.stack(
            [
                active.astype(jnp.int32),
                (section == sections - 1).astype(jnp.int32),
                slot,
                (section > 0).astype(jnp.int32),
            ]
        )
        *grads, g = backward_call(
            sc, returned, cotangent, taps, layer_scale, up, down, n_s, istd_s, slope_s, *grads
        )
        return tuple(grads), g

    def backward_loop(tick, state):
        returned, grads = state
        grads, g = backward_tick(tick, returned, grads)
        return lax.ppermute(g, "section", back_route), grads

    returned, grads = lax.fori_loop(0, ticks - 1, backward_loop, (returned, grads))
    grads, _ = backward_tick(ticks - 1, returned, grads)
    go_s, gp_s, gc_s = grads

    real_rows = (side * side * channels + 2 * channels * width + channels) // LANES
    slot_count = master.shape[1]
    share = -(-slot_count // 16) * 16
    buckets = bucket_owner.shape[1]
    slots = pl.pallas_call(
        functools.partial(weight_kernel, (*dims, real_rows, replicas, buckets)),
        out_shape=sds((replicas, share, LANES), BF16),
        in_specs=[SMEM, SMEM, VMEM] + [ANY] * 7,
        out_specs=ANY,
        scratch_shapes=[
            pltpu.VMEM((micro * positions, channels), BF16),
            pltpu.VMEM((micro * positions, channels), BF16),
            pltpu.VMEM((micro * positions, width), BF16),
            pltpu.VMEM((micro * positions, channels), F32),
            pltpu.VMEM((micro * positions, channels), BF16),
            pltpu.VMEM((micro * positions, width), BF16),
            pltpu.VMEM((micro * positions, channels), BF16),
            pltpu.VMEM((micro * positions, channels), BF16),
            pltpu.VMEM(pad_shape, F32),
            pltpu.VMEM((-(-real_rows // replicas) * replicas + STEP, LANES), F32),
            pltpu.VMEM((share + 2 * STEP, LANES), F32),
            pltpu.VMEM((2, share, LANES), BF16),
            pltpu.SMEM((buckets,), jnp.int32),
            pltpu.SMEM((buckets,), jnp.int32),
            pltpu.SMEM((replicas,), jnp.int32),
            pltpu.SemaphoreType.DMA((7 * micro + 2,)),
        ],
        compiler_params=PARAMS,
        name="weight_grads",
    )(
        bucket_bounds[0], bucket_owner[0], layer_scale, x_s, n_s, hid_s, branch_s, go_s, gp_s, gc_s
    )
    summed = lax.psum_scatter(slots, "dp", scatter_dimension=0, tiled=False)
    quads = slot_count // 4
    count = 67 if quads % 67 == 0 else 1
    part = pl.BlockSpec((count, 4, LANES), lambda i: (i, 0, 0))
    quad = sds((quads, 4, LANES), F32)
    new = pl.pallas_call(
        functools.partial(adam_kernel, count, replicas),
        grid=(quads // count,),
        out_shape=(quad, quad, quad),
        in_specs=[pl.BlockSpec((share, LANES), lambda i: (0, 0)), part, part, part],
        out_specs=[part, part, part],
        scratch_shapes=[pltpu.VMEM((share, LANES), F32)],
        compiler_params=PARAMS,
        name="adam",
    )(
        summed,
        master.reshape(quads, 4, LANES),
        first_moment.reshape(quads, 4, LANES),
        second_moment.reshape(quads, 4, LANES),
    )
    new_master, new_first, new_second = (value.reshape(master.shape) for value in new)
    return (
        outputs.reshape(1, micro, height, breadth, channels),
        new_master,
        new_first,
        new_second,
    )


def solution(mesh):
    placed = (
        P("dp", None, None, None),
        P("dp", None),
        P("dp", None, None, None),
        P("section", None, None, None),
        P("section", None, None),
        P("section", None, None),
        P("section", None),
        P("section", "dp", None),
        P("section", "dp", None),
        P("section", "dp", None),
        P("section", None),
        P("section", None),
    )
    return jax.shard_map(
        body,
        mesh=mesh,
        in_specs=placed,
        out_specs=(
            P("section", "dp", None, None, None),
            P("section", "dp", None),
            P("section", "dp", None),
            P("section", "dp", None),
        ),
        check_vma=False,
    )
```

time: 1270 us -> 588 us (0.46)
  waiting for transfers between devices: 764 us -> 370 us
  matrix products: 113 us -> 0 us
  local copies, waits for them, and re-layouts: 112 us -> 14.5 us
  Pallas kernels: 0 us -> 92.7 us
  starting transfers between devices: 166 us -> 78 us
  other arithmetic: 82.5 us -> 16.8 us
    ppermute x18 -> x16, waiting for transfers between devices: 599 us -> 236 us  [the longest x8 192 us: backward_loop(): return (lax.ppermute(g, 'section', back_route), grads)]
    psum x1 -> x0, waiting for transfers between devices: 165 us -> none  [body(): lax.psum(grad_rows[:unit_count].astype(jnp.bfloat16), 'dp')]
    reduce_scatter x0 -> x1, waiting for transfers between devices: none -> 134 us  [body(): summed = lax.psum_scatter(slots, 'dp', scatter_dimension=0, tiled=False)]
    pallas_call x0 -> x21, Pallas kernels: none -> 92.7 us  [the longest x9 29.9 us: forward_tick(): forward_call(sc, received, images, taps, layer_scale, up, down, *stash)]
    ppermute x18 -> x16, starting transfers between devices: 166 us -> 78 us  [the longest x8 67.7 us: forward_loop(): return (lax.ppermute(y, 'section', route), stash)]
    dot_general x12 -> x0, matrix products: 69.5 us -> none  [the longest x2 17.3 us: block_forward(): branch = jnp.dot(hidden, down_matrix, preferred_element_type=jnp.float32)]
    conv_general_dilated x6 -> x0, matrix products: 43.4 us -> none  [the longest x4 28.9 us: depthwise(): lax.conv_general_dilated(inputs, kernel[:, :, None, :], (1, 1), ((reach,...]
    unnamed x10 -> x8, local copies, waits for them, and re-layouts: 39.8 us -> 0.01 us
  transfers between devices with their start and end apart: 19 -> 17, of which waited for: 19 -> 17; matrix products, arithmetic and copies ran while one was open for 0% -> 0% of each run, Pallas kernels for 0% -> 0%
where the time goes in v1:
time: 588 us; the launch traced here: 587 us
  waiting for transfers between devices  370 us (63%)
  Pallas kernels  92.7 us (16%)
  starting transfers between devices  78 us (13%)
  other arithmetic  16.8 us (3%)
  local copies, waits for them, and re-layouts  14.5 us (2%)
  between operations  14.1 us (2%)
    ppermute x8, waiting for transfers between devices, backward_loop(): return (lax.ppermute(g, 'section', back_route), grads)  192 us
    reduce_scatter x1, waiting for transfers between devices, body(): summed = lax.psum_scatter(slots, 'dp', scatter_dimension=0, tiled=False)  134 us
    ppermute x8, starting transfers between devices, forward_loop(): return (lax.ppermute(y, 'section', route), stash)  67.7 us
    ppermute x8, waiting for transfers between devices, forward_loop(): return (lax.ppermute(y, 'section', route), stash)  44.1 us
    pallas_call x9, Pallas kernels, forward_tick(): forward_call(sc, received, images, taps, layer_scale, up, down, *stash)  29.9 us
    pallas_call x9, Pallas kernels, backward_tick(): backward_call(sc, returned, cotangent, taps, layer_scale, up, down, n_s,...  26.6 us
    pallas_call x1, Pallas kernels, body(): pl.pallas_call(functools.partial(weight_kernel, (*dims, real_rows, replic...  25 us
  transfers between devices with their start and end apart: 17, of which 17 were waited for; matrix products, arithmetic and copies ran while one was open for 0% of the time, Pallas kernels for 0%

profile of v1, /device:TPU:0, one launch (start us, length us, event | category | flops | bytes accessed | tf_op | source)
XLA Modules:
  0.0 586.7 jit_solution(12737270954738531711)
XLA Ops:
  7.2 1.7 reshape.58
  8.9 1.6 copy.48
  10.5 1.3 constant_dynamic-slice_fusion.1
  11.8 1.3 pad_add_fusion.2.sc
  13.8 160.5 %while.49 = (s32[]{:T(128)}, bf16[256,768]{1,0:T(8,128)(2,1)}, bf16[2,256,768]{2,1,0:T(8,128)(2,1)}, bf16[2,256,768]{2,1,0:T(8,128)(2,1)}, bf16[2,256,768]{2,1,0...) while((s32[]{:T(128)}, bf16[256,768]{1,0:T(8,128)(2,1)}, ...), condition=%wide.region_1.2_spmd, body=%wide.region_0.1_spmd.sunk | while | flops 22 | bytes 1573196 | solution.py:507
  13.8 1.2 constant_dynamic-slice_fusion.3
  15.0 1.3 pad_add_fusion.6.sc
  16.3 11.2 %block_forward.8 = (bf16[2,256,768]{2,1,0:T(8,128)(2,1)}, bf16[2,256,768]{2,1,0:T(8,128)(2,1)}, bf16[2,256,768]{2,1,0:T(8,128)(2,1)}, f32[2,256,128]{2,1,0:T(8,1...) custom-call(s32[4]{0:T(128)} %pad_add_fusion.6.sc, ...), custom_call_target="tpu_custom_call", output_to_operand_aliasing={{0}: (7, {}), {1}: (8, {}), {2}: (9, {}), {3}: (10, {}), {4... | custom-call | tf_op jit(solution)/shard_map/while/body/eval_jaxpr/block_forward/pallas_call | solution.py:497
  27.5 2.1 collective-permute-start
  29.6 7.5 %collective-permute-done = bf16[256,768]{1,0:T(8,128)(2,1)} collective-permute-done((bf16[256,768]{1,0:T(8,128)(2,1)}, bf16[256,768]{1,0:T(8,128)(2,1)}, u32[]{:S(2)}, u32[]{:S(2)}) %collective-permute-start) | collective-permute-done | bytes 393248 | tf_op jit(solution)/shard_map/while/body/eval_jaxpr/ppermute | solution.py:505
  37.0 1.2 constant_dynamic-slice_fusion.3
  38.3 1.3 pad_add_fusion.6.sc
  39.6 11.2 %block_forward.8 = (bf16[2,256,768]{2,1,0:T(8,128)(2,1)}, bf16[2,256,768]{2,1,0:T(8,128)(2,1)}, bf16[2,256,768]{2,1,0:T(8,128)(2,1)}, f32[2,256,128]{2,1,0:T(8,1...) custom-call(s32[4]{0:T(128)} %pad_add_fusion.6.sc, ...), custom_call_target="tpu_custom_call", output_to_operand_aliasing={{0}: (7, {}), {1}: (8, {}), {2}: (9, {}), {3}: (10, {}), {4... | custom-call | tf_op jit(solution)/shard_map/while/body/eval_jaxpr/block_forward/pallas_call | solution.py:497
  50.8 5.2 collective-permute-start
  56.0 6.6 %collective-permute-done = bf16[256,768]{1,0:T(8,128)(2,1)} collective-permute-done((bf16[256,768]{1,0:T(8,128)(2,1)}, bf16[256,768]{1,0:T(8,128)(2,1)}, u32[]{:S(2)}, u32[]{:S(2)}) %collective-permute-start) | collective-permute-done | bytes 393248 | tf_op jit(solution)/shard_map/while/body/eval_jaxpr/ppermute | solution.py:505
  62.6 1.2 constant_dynamic-slice_fusion.3
  63.8 1.3 pad_add_fusion.6.sc
  65.1 1.0 block_forward.8
  66.1 15.4 %collective-permute-start = (bf16[256,768]{1,0:T(8,128)(2,1)}, bf16[256,768]{1,0:T(8,128)(2,1)}, u32[]{:S(2)}, u32[]{:S(2)}) collective-permute-start(bf16[256,768]{1,0:T(8,128)(2,1)} %get-tuple-element.988), channel_id=1, source_target_pairs={{0,16},{16,32},{32,48},{48,64},{64,80},{80,96},{96,112},{1,17},{17... | collective-permute-start | bytes 1179656 | tf_op jit(solution)/shard_map/while/body/eval_jaxpr/ppermute | solution.py:505
  81.5 5.8 collective-permute-done
  87.2 1.2 constant_dynamic-slice_fusion.3
  88.5 1.3 pad_add_fusion.6.sc
  89.7 1.0 block_forward.8
  90.8 5.2 collective-permute-start
  96.0 4.9 collective-permute-done
  100.9 1.2 constant_dynamic-slice_fusion.3
  102.1 1.3 pad_add_fusion.6.sc
  104.4 15.5 %collective-permute-start = (bf16[256,768]{1,0:T(8,128)(2,1)}, bf16[256,768]{1,0:T(8,128)(2,1)}, u32[]{:S(2)}, u32[]{:S(2)}) collective-permute-start(bf16[256,768]{1,0:T(8,128)(2,1)} %get-tuple-element.988), channel_id=1, source_target_pairs={{0,16},{16,32},{32,48},{48,64},{64,80},{80,96},{96,112},{1,17},{17... | collective-permute-start | bytes 1179656 | tf_op jit(solution)/shard_map/while/body/eval_jaxpr/ppermute | solution.py:505
  119.9 4.8 collective-permute-done
  124.8 1.2 constant_dynamic-slice_fusion.3
  126.0 1.3 pad_add_fusion.6.sc
  128.3 6.1 %collective-permute-start = (bf16[256,768]{1,0:T(8,128)(2,1)}, bf16[256,768]{1,0:T(8,128)(2,1)}, u32[]{:S(2)}, u32[]{:S(2)}) collective-permute-start(bf16[256,768]{1,0:T(8,128)(2,1)} %get-tuple-element.988), channel_id=1, source_target_pairs={{0,16},{16,32},{32,48},{48,64},{64,80},{80,96},{96,112},{1,17},{17... | collective-permute-start | bytes 1179656 | tf_op jit(solution)/shard_map/while/body/eval_jaxpr/ppermute | solution.py:505
  134.4 4.8 collective-permute-done
  139.2 1.2 constant_dynamic-slice_fusion.3
  140.4 1.3 pad_add_fusion.6.sc
  142.7 12.3 %collective-permute-start = (bf16[256,768]{1,0:T(8,128)(2,1)}, bf16[256,768]{1,0:T(8,128)(2,1)}, u32[]{:S(2)}, u32[]{:S(2)}) collective-permute-start(bf16[256,768]{1,0:T(8,128)(2,1)} %get-tuple-element.988), channel_id=1, source_target_pairs={{0,16},{16,32},{32,48},{48,64},{64,80},{80,96},{96,112},{1,17},{17... | collective-permute-start | bytes 1179656 | tf_op jit(solution)/shard_map/while/body/eval_jaxpr/ppermute | solution.py:505
  155.0 4.8 collective-permute-done
  159.8 1.2 constant_dynamic-slice_fusion.3
  161.1 1.3 pad_add_fusion.6.sc
  163.4 6.1 %collective-permute-start = (bf16[256,768]{1,0:T(8,128)(2,1)}, bf16[256,768]{1,0:T(8,128)(2,1)}, u32[]{:S(2)}, u32[]{:S(2)}) collective-permute-start(bf16[256,768]{1,0:T(8,128)(2,1)} %get-tuple-element.988), channel_id=1, source_target_pairs={{0,16},{16,32},{32,48},{48,64},{64,80},{80,96},{96,112},{1,17},{17... | collective-permute-start | bytes 1179656 | tf_op jit(solution)/shard_map/while/body/eval_jaxpr/ppermute | solution.py:505
  169.4 4.8 collective-permute-done
  174.3 1.2 block_forward.7
  175.5 223.9 %while.50 = (s32[]{:T(128)}, bf16[256,768]{1,0:T(8,128)(2,1)}, bf16[2,256,768]{2,1,0:T(8,128)(2,1)}, bf16[2,256,3072]{2,1,0:T(8,128)(2,1)}, bf16[2,256,768]{2,1,...) while((s32[]{:T(128)}, bf16[256,768]{1,0:T(8,128)(2,1)}, ...), condition=%wide.region_3.4_spmd, body=%wide.region_2.3_spmd.sunk | while | flops 23 | bytes 1573181 | solution.py:533
  177.2 1.3 collective-permute-start.1
  178.5 17.5 %collective-permute-done.1 = bf16[256,768]{1,0:T(8,128)(2,1)} collective-permute-done((bf16[256,768]{1,0:T(8,128)(2,1)}, bf16[256,768]{1,0:T(8,128)(2,1)}, u32[]{:S(2)}, u32[]{:S(2)}) %collective-permute-start.1) | collective-permute-done | bytes 393248 | tf_op jit(solution)/shard_map/while/body/eval_jaxpr/ppermute | solution.py:531
  197.6 1.3 collective-permute-start.1
  198.9 10.1 %collective-permute-done.1 = bf16[256,768]{1,0:T(8,128)(2,1)} collective-permute-done((bf16[256,768]{1,0:T(8,128)(2,1)}, bf16[256,768]{1,0:T(8,128)(2,1)}, u32[]{:S(2)}, u32[]{:S(2)}) %collective-permute-start.1) | collective-permute-done | bytes 393248 | tf_op jit(solution)/shard_map/while/body/eval_jaxpr/ppermute | solution.py:531
  210.6 1.3 collective-permute-start.1
  211.9 18.0 %collective-permute-done.1 = bf16[256,768]{1,0:T(8,128)(2,1)} collective-permute-done((bf16[256,768]{1,0:T(8,128)(2,1)}, bf16[256,768]{1,0:T(8,128)(2,1)}, u32[]{:S(2)}, u32[]{:S(2)}) %collective-permute-start.1) | collective-permute-done | bytes 393248 | tf_op jit(solution)/shard_map/while/body/eval_jaxpr/ppermute | solution.py:531
  231.5 1.3 collective-permute-start.1
  232.8 8.7 %collective-permute-done.1 = bf16[256,768]{1,0:T(8,128)(2,1)} collective-permute-done((bf16[256,768]{1,0:T(8,128)(2,1)}, bf16[256,768]{1,0:T(8,128)(2,1)}, u32[]{:S(2)}, u32[]{:S(2)}) %collective-permute-start.1) | collective-permute-done | bytes 393248 | tf_op jit(solution)/shard_map/while/body/eval_jaxpr/ppermute | solution.py:531
  243.1 1.3 collective-permute-start.1
  244.4 24.0 %collective-permute-done.1 = bf16[256,768]{1,0:T(8,128)(2,1)} collective-permute-done((bf16[256,768]{1,0:T(8,128)(2,1)}, bf16[256,768]{1,0:T(8,128)(2,1)}, u32[]{:S(2)}, u32[]{:S(2)}) %collective-permute-start.1) | collective-permute-done | bytes 393248 | tf_op jit(solution)/shard_map/while/body/eval_jaxpr/ppermute | solution.py:531
  270.0 1.3 collective-permute-start.1
  271.3 8.7 %collective-permute-done.1 = bf16[256,768]{1,0:T(8,128)(2,1)} collective-permute-done((bf16[256,768]{1,0:T(8,128)(2,1)}, bf16[256,768]{1,0:T(8,128)(2,1)}, u32[]{:S(2)}, u32[]{:S(2)}) %collective-permute-start.1) | collective-permute-done | bytes 393248 | tf_op jit(solution)/shard_map/while/body/eval_jaxpr/ppermute | solution.py:531
  281.6 1.3 collective-permute-start.1
  282.9 92.0 %collective-permute-done.1 = bf16[256,768]{1,0:T(8,128)(2,1)} collective-permute-done((bf16[256,768]{1,0:T(8,128)(2,1)}, bf16[256,768]{1,0:T(8,128)(2,1)}, u32[]{:S(2)}, u32[]{:S(2)}) %collective-permute-start.1) | collective-permute-done | bytes 393248 | tf_op jit(solution)/shard_map/while/body/eval_jaxpr/ppermute | solution.py:531
  375.6 9.4 %block_backward.9 = (bf16[2,256,768]{2,1,0:T(8,128)(2,1)}, bf16[2,256,3072]{2,1,0:T(8,128)(2,1)}, bf16[2,256,768]{2,1,0:T(8,128)(2,1)}, bf16[256,768]{1,0:T(8,128)(2,1)}) custom-call(s32[4]{0:T(128)} %pad_add_fusion.7.sc, bf16[256,768]{1,0:T(8,128)(2,1)} %get-tuple-element.1096.gr, ...), custom_call_target="tpu_custom_call", output_to_operand_aliasing={{0}: (10, {}), {1}: (11, {}), {2}: (12, {})} | custom-call | tf_op jit(solution)/shard_map/while/body/eval_jaxpr/block_backward/pallas_call | solution.py:523
  385.0 1.3 collective-permute-start.1
  386.3 13.0 %collective-permute-done.1 = bf16[256,768]{1,0:T(8,128)(2,1)} collective-permute-done((bf16[256,768]{1,0:T(8,128)(2,1)}, bf16[256,768]{1,0:T(8,128)(2,1)}, u32[]{:S(2)}, u32[]{:S(2)}) %collective-permute-start.1) | collective-permute-done | bytes 393248 | tf_op jit(solution)/shard_map/while/body/eval_jaxpr/ppermute | solution.py:531
  399.4 10.0 %block_backward.8 = (bf16[2,256,768]{2,1,0:T(8,128)(2,1)}, bf16[2,256,3072]{2,1,0:T(8,128)(2,1)}, bf16[2,256,768]{2,1,0:T(8,128)(2,1)}, bf16[256,768]{1,0:T(8,128)(2,1)}) custom-call(s32[4]{0:T(128)} %pad_add_fusion.3.sc, bf16[256,768]{1,0:T(8,128)(2,1)} %get-tuple-element.704.gr, ...), custom_call_target="tpu_custom_call", output_to_operand_aliasing={{0}: (10, {}), {1}: (11, {}), {2}: (12, {})} | custom-call | tf_op jit(solution)/shard_map/block_backward/pallas_call | solution.py:523
  409.4 25.0 %weight_grads.1 = bf16[16,3488,128]{2,1,0:T(8,128)(2,1)} custom-call(s32[49]{0:T(128)} %bitcast.59, s32[48]{0:T(128)} %bitcast.60, f32[1,768]{1,0:T(1,128)S(1)} %get-tuple-element.1149, bf16[2,256,768]{2,1,0:T(8,128)(2,1)S(1)} %copy-done.2, bf16[2,256,768]{2,1,0:T(8,128)(2,1)S(1)} %copy-done.1, bf16[2,256,3072]{2,1,0:T(8,128)(2,1)S(1)} %copy-done, ...), custom_call_target="tpu_custom_call" | custom-call | tf_op jit(solution)/shard_map/weight_grads/pallas_call | solution.py:541
  434.4 134.2 %reduce-scatter.2.cloned.1.call-done = bf16[1,3488,128]{2,1,0:T(8,128)(2,1)} async-done(((bf16[16,3488,128]{2,1,0:T(8,128)(2,1)}), bf16[1,3488,128]{2,1,0:T(8,128)(2,1)}) %reduce-scatter.2.cloned.1.call-update) | async-done | bytes 892944 | tf_op jit(solution)/shard_map/reduce_scatter | solution.py:569
  568.6 11.3 %adam.1 = (f32[871,4,128]{2,1,0:T(4,128)}, f32[871,4,128]{2,1,0:T(4,128)}, f32[871,4,128]{2,1,0:T(4,128)}) custom-call(bf16[3488,128]{1,0:T(8,128)(2,1)} %bitcast.58, f32[871,4,128]{2,1,0:T(4,128)} %bitcast.55, f32[871,4,128]{2,1,0:T(4,128)} %bitcast.56, f32[871,4,128]{2,1,0:T(4,128)} %bitcast.57), custom_call_target="tpu_custom_call" | custom-call | tf_op jit(solution)/shard_map/adam/pallas_call | solution.py:574
  (31 shorter events, 16.7 us)
Async XLA Ops:
  7.2 561.4 %reduce-scatter.2.cloned.1.call-start = ((), (), s32[]{:S(2)}) async-start(), calls=%async_computation.1 | async-start | bytes 15179776 | tf_op jit(solution)/shard_map/reduce_scatter | solution.py:569
  27.5 9.5 %collective-permute-start = (bf16[256,768]{1,0:T(8,128)(2,1)}, bf16[256,768]{1,0:T(8,128)(2,1)}, u32[]{:S(2)}, u32[]{:S(2)}) collective-permute-start(bf16[256,768]{1,0:T(8,128)(2,1)} %get-tuple-element.988), channel_id=1, source_target_pairs={{0,16},{16,32},{32,48},{48,64},{64,80},{80,96},{96,112},{1,17},{17... | collective-permute-start | bytes 1179656 | tf_op jit(solution)/shard_map/while/body/eval_jaxpr/ppermute | solution.py:505
  50.8 11.8 %collective-permute-start = (bf16[256,768]{1,0:T(8,128)(2,1)}, bf16[256,768]{1,0:T(8,128)(2,1)}, u32[]{:S(2)}, u32[]{:S(2)}) collective-permute-start(bf16[256,768]{1,0:T(8,128)(2,1)} %get-tuple-element.988), channel_id=1, source_target_pairs={{0,16},{16,32},{32,48},{48,64},{64,80},{80,96},{96,112},{1,17},{17... | collective-permute-start | bytes 1179656 | tf_op jit(solution)/shard_map/while/body/eval_jaxpr/ppermute | solution.py:505
  66.1 21.1 %collective-permute-start = (bf16[256,768]{1,0:T(8,128)(2,1)}, bf16[256,768]{1,0:T(8,128)(2,1)}, u32[]{:S(2)}, u32[]{:S(2)}) collective-permute-start(bf16[256,768]{1,0:T(8,128)(2,1)} %get-tuple-element.988), channel_id=1, source_target_pairs={{0,16},{16,32},{32,48},{48,64},{64,80},{80,96},{96,112},{1,17},{17... | collective-permute-start | bytes 1179656 | tf_op jit(solution)/shard_map/while/body/eval_jaxpr/ppermute | solution.py:505
  90.8 10.1 %collective-permute-start = (bf16[256,768]{1,0:T(8,128)(2,1)}, bf16[256,768]{1,0:T(8,128)(2,1)}, u32[]{:S(2)}, u32[]{:S(2)}) collective-permute-start(bf16[256,768]{1,0:T(8,128)(2,1)} %get-tuple-element.988), channel_id=1, source_target_pairs={{0,16},{16,32},{32,48},{48,64},{64,80},{80,96},{96,112},{1,17},{17... | collective-permute-start | bytes 1179656 | tf_op jit(solution)/shard_map/while/body/eval_jaxpr/ppermute | solution.py:505
  104.4 20.3 %collective-permute-start = (bf16[256,768]{1,0:T(8,128)(2,1)}, bf16[256,768]{1,0:T(8,128)(2,1)}, u32[]{:S(2)}, u32[]{:S(2)}) collective-permute-start(bf16[256,768]{1,0:T(8,128)(2,1)} %get-tuple-element.988), channel_id=1, source_target_pairs={{0,16},{16,32},{32,48},{48,64},{64,80},{80,96},{96,112},{1,17},{17... | collective-permute-start | bytes 1179656 | tf_op jit(solution)/shard_map/while/body/eval_jaxpr/ppermute | solution.py:505
  128.3 10.9 %collective-permute-start = (bf16[256,768]{1,0:T(8,128)(2,1)}, bf16[256,768]{1,0:T(8,128)(2,1)}, u32[]{:S(2)}, u32[]{:S(2)}) collective-permute-start(bf16[256,768]{1,0:T(8,128)(2,1)} %get-tuple-element.988), channel_id=1, source_target_pairs={{0,16},{16,32},{32,48},{48,64},{64,80},{80,96},{96,112},{1,17},{17... | collective-permute-start | bytes 1179656 | tf_op jit(solution)/shard_map/while/body/eval_jaxpr/ppermute | solution.py:505
  142.7 17.1 %collective-permute-start = (bf16[256,768]{1,0:T(8,128)(2,1)}, bf16[256,768]{1,0:T(8,128)(2,1)}, u32[]{:S(2)}, u32[]{:S(2)}) collective-permute-start(bf16[256,768]{1,0:T(8,128)(2,1)} %get-tuple-element.988), channel_id=1, source_target_pairs={{0,16},{16,32},{32,48},{48,64},{64,80},{80,96},{96,112},{1,17},{17... | collective-permute-start | bytes 1179656 | tf_op jit(solution)/shard_map/while/body/eval_jaxpr/ppermute | solution.py:505
  163.4 10.9 %collective-permute-start = (bf16[256,768]{1,0:T(8,128)(2,1)}, bf16[256,768]{1,0:T(8,128)(2,1)}, u32[]{:S(2)}, u32[]{:S(2)}) collective-permute-start(bf16[256,768]{1,0:T(8,128)(2,1)} %get-tuple-element.988), channel_id=1, source_target_pairs={{0,16},{16,32},{32,48},{48,64},{64,80},{80,96},{96,112},{1,17},{17... | collective-permute-start | bytes 1179656 | tf_op jit(solution)/shard_map/while/body/eval_jaxpr/ppermute | solution.py:505
  174.3 1.2 copy-start.3
  177.2 18.8 %collective-permute-start.1 = (bf16[256,768]{1,0:T(8,128)(2,1)}, bf16[256,768]{1,0:T(8,128)(2,1)}, u32[]{:S(2)}, u32[]{:S(2)}) collective-permute-start(bf16[256,768]{1,0:T(8,128)(2,1)} %get-tuple-element.1012), channel_id=1, source_target_pairs={{16,0},{32,16},{48,32},{64,48},{80,64},{96,80},{112,96},{17,1},{33... | collective-permute-start | bytes 1179656 | tf_op jit(solution)/shard_map/while/body/eval_jaxpr/ppermute | solution.py:531
  197.6 11.4 %collective-permute-start.1 = (bf16[256,768]{1,0:T(8,128)(2,1)}, bf16[256,768]{1,0:T(8,128)(2,1)}, u32[]{:S(2)}, u32[]{:S(2)}) collective-permute-start(bf16[256,768]{1,0:T(8,128)(2,1)} %get-tuple-element.1012), channel_id=1, source_target_pairs={{16,0},{32,16},{48,32},{64,48},{80,64},{96,80},{112,96},{17,1},{33... | collective-permute-start | bytes 1179656 | tf_op jit(solution)/shard_map/while/body/eval_jaxpr/ppermute | solution.py:531
  210.6 19.3 %collective-permute-start.1 = (bf16[256,768]{1,0:T(8,128)(2,1)}, bf16[256,768]{1,0:T(8,128)(2,1)}, u32[]{:S(2)}, u32[]{:S(2)}) collective-permute-start(bf16[256,768]{1,0:T(8,128)(2,1)} %get-tuple-element.1012), channel_id=1, source_target_pairs={{16,0},{32,16},{48,32},{64,48},{80,64},{96,80},{112,96},{17,1},{33... | collective-permute-start | bytes 1179656 | tf_op jit(solution)/shard_map/while/body/eval_jaxpr/ppermute | solution.py:531
  231.5 10.0 %collective-permute-start.1 = (bf16[256,768]{1,0:T(8,128)(2,1)}, bf16[256,768]{1,0:T(8,128)(2,1)}, u32[]{:S(2)}, u32[]{:S(2)}) collective-permute-start(bf16[256,768]{1,0:T(8,128)(2,1)} %get-tuple-element.1012), channel_id=1, source_target_pairs={{16,0},{32,16},{48,32},{64,48},{80,64},{96,80},{112,96},{17,1},{33... | collective-permute-start | bytes 1179656 | tf_op jit(solution)/shard_map/while/body/eval_jaxpr/ppermute | solution.py:531
  243.1 25.3 %collective-permute-start.1 = (bf16[256,768]{1,0:T(8,128)(2,1)}, bf16[256,768]{1,0:T(8,128)(2,1)}, u32[]{:S(2)}, u32[]{:S(2)}) collective-permute-start(bf16[256,768]{1,0:T(8,128)(2,1)} %get-tuple-element.1012), channel_id=1, source_target_pairs={{16,0},{32,16},{48,32},{64,48},{80,64},{96,80},{112,96},{17,1},{33... | collective-permute-start | bytes 1179656 | tf_op jit(solution)/shard_map/while/body/eval_jaxpr/ppermute | solution.py:531
  270.0 10.0 %collective-permute-start.1 = (bf16[256,768]{1,0:T(8,128)(2,1)}, bf16[256,768]{1,0:T(8,128)(2,1)}, u32[]{:S(2)}, u32[]{:S(2)}) collective-permute-start(bf16[256,768]{1,0:T(8,128)(2,1)} %get-tuple-element.1012), channel_id=1, source_target_pairs={{16,0},{32,16},{48,32},{64,48},{80,64},{96,80},{112,96},{17,1},{33... | collective-permute-start | bytes 1179656 | tf_op jit(solution)/shard_map/while/body/eval_jaxpr/ppermute | solution.py:531
  281.6 93.3 %collective-permute-start.1 = (bf16[256,768]{1,0:T(8,128)(2,1)}, bf16[256,768]{1,0:T(8,128)(2,1)}, u32[]{:S(2)}, u32[]{:S(2)}) collective-permute-start(bf16[256,768]{1,0:T(8,128)(2,1)} %get-tuple-element.1012), channel_id=1, source_target_pairs={{16,0},{32,16},{48,32},{64,48},{80,64},{96,80},{112,96},{17,1},{33... | collective-permute-start | bytes 1179656 | tf_op jit(solution)/shard_map/while/body/eval_jaxpr/ppermute | solution.py:531
  385.0 14.3 %collective-permute-start.1 = (bf16[256,768]{1,0:T(8,128)(2,1)}, bf16[256,768]{1,0:T(8,128)(2,1)}, u32[]{:S(2)}, u32[]{:S(2)}) collective-permute-start(bf16[256,768]{1,0:T(8,128)(2,1)} %get-tuple-element.1012), channel_id=1, source_target_pairs={{16,0},{32,16},{48,32},{64,48},{80,64},{96,80},{112,96},{17,1},{33... | collective-permute-start | bytes 1179656 | tf_op jit(solution)/shard_map/while/body/eval_jaxpr/ppermute | solution.py:531
  399.4 10.0 %copy-start = (bf16[2,256,3072]{2,1,0:T(8,128)(2,1)S(1)}, bf16[2,256,3072]{2,1,0:T(8,128)(2,1)}, u32[]{:S(2)}) copy-start(bf16[2,256,3072]{2,1,0:T(8,128)(2,1)} %get-tuple-element.696.hid_i) | copy-start | bytes 9437188
  399.4 10.0 %copy-start.1 = (bf16[2,256,768]{2,1,0:T(8,128)(2,1)S(1)}, bf16[2,256,768]{2,1,0:T(8,128)(2,1)}, u32[]{:S(2)}) copy-start(bf16[2,256,768]{2,1,0:T(8,128)(2,1)} %get-tuple-element.1139) | copy-start | bytes 2359300
  399.4 10.0 %copy-start.2 = (bf16[2,256,768]{2,1,0:T(8,128)(2,1)S(1)}, bf16[2,256,768]{2,1,0:T(8,128)(2,1)}, u32[]{:S(2)}) copy-start(bf16[2,256,768]{2,1,0:T(8,128)(2,1)} %get-tuple-element.694.x_i) | copy-start | bytes 2359300
Sparse Core Ops, SparseCore 0:
  434.5 134.0 reduce-scatter.1

commit v2 on v1

--- a/solution.py
+++ b/solution.py
@@ -77,29 +77,30 @@
 
 
 def forward_kernel(
-    dims, sc, xr, images, taps, scale, up, down, *refs
+    dims, tick, place, roster, xr, images, taps, scale, up, down, *refs
 ):
     side, height, breadth, width = dims
     out_o, x_o, n_o, istd_o, hid_o, slope_o, branch_o, y = refs[7:15]
     xv, pad, conv, nv, iv, upv, downv, hv, sv, acc, yv, sems = refs[15:]
     positions, channels = xv.shape
+    micro = images.shape[0]
     reach = (side - 1) // 2
-
-    @pl.when(sc[0] > 0)
+    slot = tick[0] - place[0]
+
+    @pl.when((slot >= 0) & (slot < micro))
     def _():
-        slot = sc[2]
         up_in = pltpu.make_async_copy(up, upv, sems.at[0])
         down_in = pltpu.make_async_copy(down, downv, sems.at[1])
 
-        @pl.when(sc[1] > 0)
+        @pl.when(place[0] == 0)
         def _():
-            cp = pltpu.make_async_copy(images.at[sc[3]], xv, sems.at[2])
+            cp = pltpu.make_async_copy(images.at[roster[0, slot]], xv, sems.at[2])
             cp.start()
             up_in.start()
             down_in.start()
             cp.wait()
 
-        @pl.when(sc[1] == 0)
+        @pl.when(place[0] > 0)
         def _():
             cp = pltpu.make_async_copy(xr, xv, sems.at[2])
             cp.start()
@@ -153,17 +154,18 @@
 
 
 def backward_kernel(
-    dims, sc, gr, cotangent, taps, scale, up, down, n_i, istd_i, slope_i, *refs
+    dims, tick, place, gr, cotangent, taps, scale, up, down, n_i, istd_i, slope_i, *refs
 ):
     side, height, breadth, width = dims
     go_o, gp_o, gc_o, g_in = refs[3:7]
     gv, pad, conv, nv, iv, upv, downv, sv, gpv, acc, scaled, gcv, yv, sems = refs[7:]
     positions, channels = gv.shape
+    micro = cotangent.shape[0]
     reach = (side - 1) // 2
-
-    @pl.when(sc[0] > 0)
+    slot = tick[0] - place[1]
+
+    @pl.when((slot >= 0) & (slot < micro))
     def _():
-        slot = sc[2]
         down_in = pltpu.make_async_copy(down, downv, sems.at[0])
         up_in = pltpu.make_async_copy(up, upv, sems.at[1])
         s_in = pltpu.make_async_copy(slope_i.at[slot], sv, sems.at[3])
@@ -180,11 +182,11 @@
             i_in.start()
             cp.wait()
 
-        @pl.when(sc[1] > 0)
+        @pl.when(place[1] == 0)
         def _():
             begin(cotangent.at[slot])
 
-        @pl.when(sc[1] == 0)
+        @pl.when(place[1] > 0)
         def _():
             begin(gr)
 
@@ -225,7 +227,7 @@
         gc_out = pltpu.make_async_copy(gcv, gc_o.at[slot], sems.at[8])
         gc_out.start()
 
-        @pl.when(sc[3] > 0)
+        @pl.when(place[0] > 0)
         def _():
             pad_map(pad, gcv, reach, height, breadth)
             depthwise(pad, taps, conv, side, height, breadth, True)
@@ -239,9 +241,10 @@
 
 
 def weight_kernel(
-    dims, bounds, owners, scale, x_i, n_i, hid_i, branch_i, go_i, gp_i, gc_i, slots_o, *refs
+    dims, bounds, owners, order, scale, x_i, n_i, hid_i, branch_i, go_i, gp_i, gc_i, *refs
 ):
-    side, height, breadth, width, real_rows, owner_count, buckets = dims
+    side, height, breadth, width, real_rows, owner_count, buckets, share, cut = dims
+    pieces, refs = refs[:PIECES], refs[PIECES:]
     (xv, nv, hv, bv, gv, gpv, gcv, scaled, pad, flat, stage, ready, starts, lengths, counts, sems) = refs
     micro, positions, channels = x_i.shape
     reach = (side - 1) // 2
@@ -327,14 +330,26 @@
                     else:
                         flat[at, :] += total
 
-    share = ready.shape[1]
-
-    def out_copy(d, q):
-        return pltpu.make_async_copy(ready.at[q], slots_o.at[d], sems.at[7 * micro + q])
-
-    @rolled(owner_count)
-    def _(d):
-        q = lax.rem(d, 2)
+    half = (share - cut) // 2
+    spans = ((0, cut), (cut, half), (cut + half, half))
+
+    def out_copies(target, q, n):
+        result = []
+        for part, (first, size) in enumerate(spans):
+            piece, at = target[part]
+            result.append(
+                pltpu.make_async_copy(
+                    ready.at[q, pl.ds(first, size)],
+                    pieces[piece].at[at],
+                    sems.at[7 * micro + 3 * q + part],
+                )
+            )
+        return result
+
+    waiting = [None, None]
+    for n, target in enumerate(relay_targets()):
+        q = n % 2
+        d = order[n]
         offset = 0
         for k in range(buckets // owner_count):
             at = d * (buckets // owner_count) + k
@@ -348,21 +363,110 @@
             lax.fori_loop(0, lax.div(length + STEP - 1, STEP), move, 0)
             offset = offset + length
 
-        def clear(i, c):
+        def clear(i, c, offset=offset):
             stage[pl.ds(offset + STEP * i, STEP), :] = jnp.zeros((STEP, LANES), F32)
             return c
 
         lax.fori_loop(0, lax.div(share - offset + STEP - 1, STEP), clear, 0)
-
-        @pl.when(d >= 2)
-        def _():
-            out_copy(d - 2, q).wait()
-
+        if waiting[q] is not None:
+            for cp in waiting[q]:
+                cp.wait()
         ready[q] = stage[:share, :].astype(BF16)
-        out_copy(d, q).start()
-
-    for d in range(owner_count - 2, owner_count):
-        out_copy(d, d % 2).wait()
+        waiting[q] = out_copies(target, q, n)
+        for cp in waiting[q]:
+            cp.start()
+    for q in range(2):
+        for cp in waiting[q]:
+            cp.wait()
+
+
+ORBIT = 4
+PIECES = 12
+
+
+def relay_order():
+    order = []
+    for core in (1, 0):
+        for z, x in ((0, 3), (1, 1), (0, 2), (1, 2), (0, 1), (1, 3), (0, 0), (1, 0)):
+            order.append((core, z, x))
+    return order
+
+
+def relay_targets():
+    turn = {(0, 3): 0, (1, 1): 0, (0, 2): 1, (1, 2): 1, (0, 1): 2, (1, 3): 2, (0, 0): 3, (1, 0): 3}
+    result = []
+    for core, z, x in relay_order():
+        base = 6 * (1 - core)
+        q = base + 4 + (1 - z)
+        result.append(((base + turn[z, x], z), (q, x), (q, ORBIT + x)))
+    return result
+
+
+def piece_shapes(share, cut):
+    half = (share - cut) // 2
+    one = [(2, cut, LANES)] * 4 + [(2 * ORBIT, half, LANES)] * 2
+    return one + one
+
+
+def owner_order(me):
+    z, x, core = me // 8, (me // 2) % 4, me % 2
+    return jnp.stack(
+        [((z + dz) % 2) * 8 + ((x + dx) % 4) * 2 + (core + dc) % 2 for dc, dz, dx in relay_order()]
+    ).astype(jnp.int32)
+
+
+def routes():
+    def route(to):
+        pairs = []
+        for me in range(16):
+            z, x, core = me // 8, (me // 2) % 4, me % 2
+            z, x, core = to(z, x, core)
+            pairs.append((me, z * 8 + x * 2 + core))
+        return pairs
+
+    return (
+        route(lambda z, x, c: (z, x, 1 - c)),
+        route(lambda z, x, c: (z, (x + 1) % 4, c)),
+        route(lambda z, x, c: (z, (x + 3) % 4, c)),
+        route(lambda z, x, c: (1 - z, x, c)),
+    )
+
+
+def plus(*values):
+    total = values[0].astype(F32)
+    for value in values[1:]:
+        total = total + value.astype(F32)
+    return total.astype(BF16)
+
+
+def relay_sum(pieces):
+    across, right, left, over = routes()
+    sent, kept = pieces[:6], pieces[6:]
+    half = sent[4].shape[1]
+
+    def hop(value, route):
+        return lax.ppermute(value, "dp", route)
+
+    came = [None] * 6
+    for q in (0, 4, 1, 2, 5, 3):
+        came[q] = hop(sent[q], across)
+    r = hop(plus(kept[0][0], came[0][0]), right)
+    l = hop(plus(kept[0][1], came[0][1]), left)
+    far = hop(plus(kept[4][:ORBIT], came[4][:ORBIT]), over)
+    farther = hop(plus(kept[4][ORBIT:], came[4][ORBIT:]), over)
+    for q in (1, 2):
+        r = hop(plus(kept[q][0], came[q][0], r), right)
+        l = hop(plus(kept[q][1], came[q][1], l), left)
+    z_sent = hop(plus(kept[3][1], came[3][1], l), over)
+    near = (kept[5][:ORBIT], came[5][:ORBIT], far)
+    nearer = (kept[5][ORBIT:], came[5][ORBIT:], farther)
+    a = hop(plus(*(v[3] for v in near)), right)
+    b = hop(plus(*(v[1] for v in nearer)), left)
+    for step in (2, 1):
+        a = hop(plus(*(v[step] for v in near), a), right)
+        b = hop(plus(*(v[4 - step] for v in nearer), b), left)
+    first = (kept[3][0], came[3][0], r, z_sent)
+    return first, tuple(v[0] for v in near) + (a,), tuple(v[0] for v in nearer) + (b,)
 
 
 def adam_kernel(count, replicas, g_i, m_i, f_i, s_i, m_o, f_o, s_o, grads):
@@ -434,9 +538,9 @@
     forward_call = pl.pallas_call(
         functools.partial(forward_kernel, dims),
         out_shape=(*kept, one),
-        in_specs=[SMEM, ANY, ANY, VMEM, VMEM, ANY, ANY] + [ANY] * len(kept),
+        in_specs=[SMEM, SMEM, SMEM, ANY, ANY, VMEM, VMEM, ANY, ANY] + [ANY] * len(kept),
         out_specs=[ANY] * (len(kept) + 1),
-        input_output_aliases={7 + q: q for q in range(len(kept))},
+        input_output_aliases={9 + q: q for q in range(len(kept))},
         scratch_shapes=[
             pltpu.VMEM((positions, channels), BF16),
             pltpu.VMEM(pad_shape, F32),
@@ -458,9 +562,9 @@
     backward_call = pl.pallas_call(
         functools.partial(backward_kernel, dims),
         out_shape=(*saved, one),
-        in_specs=[SMEM, ANY, ANY, VMEM, VMEM, ANY, ANY, ANY, ANY, ANY] + [ANY] * len(saved),
+        in_specs=[SMEM, SMEM, ANY, ANY, VMEM, VMEM, ANY, ANY, ANY, ANY, ANY] + [ANY] * len(saved),
         out_specs=[ANY] * (len(saved) + 1),
-        input_output_aliases={10 + q: q for q in range(len(saved))},
+        input_output_aliases={11 + q: q for q in range(len(saved))},
         scratch_shapes=[
             pltpu.VMEM((positions, channels), BF16),
             pltpu.VMEM(pad_shape, F32),
@@ -486,16 +590,12 @@
     route = [(i, i + 1) for i in range(sections - 1)]
     back_route = [(i + 1, i) for i in range(sections - 1)]
     ticks = micro + sections - 1
+    order = owner_order(lax.axis_index("dp"))
+    place = jnp.stack([section, sections - 1 - section]).astype(jnp.int32)
 
     def forward_tick(tick, received, stash):
-        slot = tick - section
-        active = (slot >= 0) & (slot < micro)
-        slot = jnp.clip(slot, 0, micro - 1)
-        sc = jnp.stack(
-            [active.astype(jnp.int32), (section == 0).astype(jnp.int32), slot, roster[0, slot]]
-        )
         *stash, y = forward_call(
-            sc, received, images, taps, layer_scale, up, down, *stash
+            tick.reshape(1), place, roster, received, images, taps, layer_scale, up, down, *stash
         )
         return tuple(stash), y
 
@@ -505,23 +605,12 @@
         return lax.ppermute(y, "section", route), stash
 
     received, stash = lax.fori_loop(0, ticks - 1, forward_loop, (received, stash))
-    stash, _ = forward_tick(ticks - 1, received, stash)
+    stash, _ = forward_tick(jnp.int32(ticks - 1), received, stash)
     outputs, x_s, n_s, istd_s, hid_s, slope_s, branch_s = stash
 
     def backward_tick(tick, returned, grads):
-        slot = tick - (sections - 1 - section)
-        active = (slot >= 0) & (slot < micro)
-        slot = jnp.clip(slot, 0, micro - 1)
-        sc = jnp.stack(
-            [
-                active.astype(jnp.int32),
-                (section == sections - 1).astype(jnp.int32),
-                slot,
-                (section > 0).astype(jnp.int32),
-            ]
-        )
         *grads, g = backward_call(
-            sc, returned, cotangent, taps, layer_scale, up, down, n_s, istd_s, slope_s, *grads
+            tick.reshape(1), place, returned, cotangent, taps, layer_scale, up, down, n_s, istd_s, slope_s, *grads
         )
         return tuple(grads), g
 
@@ -531,18 +620,21 @@
         return lax.ppermute(g, "section", back_route), grads
 
     returned, grads = lax.fori_loop(0, ticks - 1, backward_loop, (returned, grads))
-    grads, _ = backward_tick(ticks - 1, returned, grads)
+    grads, _ = backward_tick(jnp.int32(ticks - 1), returned, grads)
     go_s, gp_s, gc_s = grads
 
     real_rows = (side * side * channels + 2 * channels * width + channels) // LANES
     slot_count = master.shape[1]
     share = -(-slot_count // 16) * 16
     buckets = bucket_owner.shape[1]
-    slots = pl.pallas_call(
-        functools.partial(weight_kernel, (*dims, real_rows, replicas, buckets)),
-        out_shape=sds((replicas, share, LANES), BF16),
-        in_specs=[SMEM, SMEM, VMEM] + [ANY] * 7,
-        out_specs=ANY,
+    cut = share * 4 // 7 // 32 * 32 + share % 32
+    pieces = pl.pallas_call(
+        functools.partial(
+            weight_kernel, (*dims, real_rows, replicas, buckets, share, cut)
+        ),
+        out_shape=tuple(sds(shape, BF16) for shape in piece_shapes(share, cut)),
+        in_specs=[SMEM, SMEM, SMEM, VMEM] + [ANY] * 7,
+        out_specs=[ANY] * PIECES,
         scratch_shapes=[
             pltpu.VMEM((micro * positions, channels), BF16),
             pltpu.VMEM((micro * positions, channels), BF16),
@@ -559,14 +651,14 @@
             pltpu.SMEM((buckets,), jnp.int32),
             pltpu.SMEM((buckets,), jnp.int32),
             pltpu.SMEM((replicas,), jnp.int32),
-            pltpu.SemaphoreType.DMA((7 * micro + 2,)),
+            pltpu.SemaphoreType.DMA((7 * micro + 6,)),
         ],
         compiler_params=PARAMS,
         name="weight_grads",
     )(
-        bucket_bounds[0], bucket_owner[0], layer_scale, x_s, n_s, hid_s, branch_s, go_s, gp_s, gc_s
-    )
-    summed = lax.psum_scatter(slots, "dp", scatter_dimension=0, tiled=False)
+        bucket_bounds[0], bucket_owner[0], order, layer_scale, x_s, n_s, hid_s, branch_s, go_s, gp_s, gc_s
+    )
+    summed = jnp.concatenate([plus(*values) for values in relay_sum(pieces)])
     quads = slot_count // 4
     count = 67 if quads % 67 == 0 else 1
     part = pl.BlockSpec((count, 4, LANES), lambda i: (i, 0, 0))

time: 588 us -> 507 us (0.86)
  waiting for transfers between devices: 370 us -> 295 us
  starting transfers between devices: 78 us -> 107 us
  between operations: 14.1 us -> 1.04 us
  other arithmetic: 16.8 us -> 4.98 us
  local copies, waits for them, and re-layouts: 14.5 us -> 4 us
    reduce_scatter x1 -> x0, waiting for transfers between devices: 134 us -> none  [body(): summed = lax.psum_scatter(slots, 'dp', scatter_dimension=0, tiled=False)]
    ppermute x0 -> x21, waiting for transfers between devices: none -> 58.9 us  [hop(): return lax.ppermute(value, 'dp', route)]
    ppermute x0 -> x21, starting transfers between devices: none -> 29.7 us  [hop(): return lax.ppermute(value, 'dp', route)]
    another operation x18 -> x1, other arithmetic: 16.8 us -> 0.07 us  [body(): place = jnp.stack([section, sections - 1 - section]).astype(jnp.int32)]
    dynamic_slice x9 -> x0, local copies, waits for them, and re-layouts: 11.2 us -> none  [forward_tick(): roster[0, slot]]
  transfers between devices with their start and end apart: 17 -> 37, of which waited for: 17 -> 25; matrix products, arithmetic and copies ran while one was open for 0% -> 1% of each run, Pallas kernels for 0% -> 0%
where the time goes in v2:
time: 507 us; the launch traced here: 506 us
  waiting for transfers between devices  295 us (58%)
  starting transfers between devices  107 us (21%)
  Pallas kernels  92.8 us (18%)
    ppermute x8, waiting for transfers between devices, backward_loop(): return (lax.ppermute(g, 'section', back_route), grads)  192 us
    ppermute x8, starting transfers between devices, forward_loop(): return (lax.ppermute(y, 'section', route), stash)  67.4 us
    ppermute x21, waiting for transfers between devices, hop(): return lax.ppermute(value, 'dp', route)  58.9 us
    ppermute x8, waiting for transfers between devices, forward_loop(): return (lax.ppermute(y, 'section', route), stash)  44.3 us
    pallas_call x9, Pallas kernels, forward_tick(): forward_call(tick.reshape(1), place, roster, received, images, taps, laye...  29.9 us
    ppermute x21, starting transfers between devices, hop(): return lax.ppermute(value, 'dp', route)  29.7 us
    pallas_call x9, Pallas kernels, backward_tick(): backward_call(tick.reshape(1), place, returned, cotangent, taps, layer_sc...  26.1 us
    pallas_call x1, Pallas kernels, body(): pl.pallas_call(functools.partial(weight_kernel, (*dims, real_rows, replic...  25.4 us
  transfers between devices with their start and end apart: 37, of which 25 were waited for; matrix products, arithmetic and copies ran while one was open for 1% of the time, Pallas kernels for 0%

profile of v2, /device:TPU:0, one launch (start us, length us, event | category | flops | bytes accessed | tf_op | source)
XLA Modules:
  0.0 505.6 jit_solution(7141964383129197228)
XLA Ops:
  0.8 1.7 reshape.122
  2.5 1.6 copy.44
  4.2 140.5 %while.46 = (s32[]{:T(128)}, bf16[256,768]{1,0:T(8,128)(2,1)}, bf16[2,256,768]{2,1,0:T(8,128)(2,1)}, bf16[2,256,768]{2,1,0:T(8,128)(2,1)}, bf16[2,256,768]{2,1,0...) while((s32[]{:T(128)}, bf16[256,768]{1,0:T(8,128)(2,1)}, ...), condition=%wide.region_1.2_spmd, body=%wide.region_0.1_spmd.sunk | while | flops 2 | bytes 1573061 | solution.py:607
  4.2 11.2 %block_forward.7 = (bf16[2,256,768]{2,1,0:T(8,128)(2,1)}, bf16[2,256,768]{2,1,0:T(8,128)(2,1)}, bf16[2,256,768]{2,1,0:T(8,128)(2,1)}, f32[2,256,128]{2,1,0:T(8,1...) custom-call(s32[1]{0:T(128)} %bitcast.96.tick, ...), custom_call_target="tpu_custom_call", output_to_operand_aliasing={{0}: (9, {}), {1}: (10, {}), {2}: (11, {}), {3}: (12, {}), ... | custom-call | tf_op jit(solution)/shard_map/while/body/eval_jaxpr/block_forward/pallas_call | solution.py:597
  15.4 2.0 collective-permute-start
  17.4 7.5 %collective-permute-done = bf16[256,768]{1,0:T(8,128)(2,1)} collective-permute-done((bf16[256,768]{1,0:T(8,128)(2,1)}, bf16[256,768]{1,0:T(8,128)(2,1)}, u32[]{:S(2)}, u32[]{:S(2)}) %collective-permute-start) | collective-permute-done | bytes 393248 | tf_op jit(solution)/shard_map/while/body/eval_jaxpr/ppermute | solution.py:605
  25.0 11.2 %block_forward.7 = (bf16[2,256,768]{2,1,0:T(8,128)(2,1)}, bf16[2,256,768]{2,1,0:T(8,128)(2,1)}, bf16[2,256,768]{2,1,0:T(8,128)(2,1)}, f32[2,256,128]{2,1,0:T(8,1...) custom-call(s32[1]{0:T(128)} %bitcast.96.tick, ...), custom_call_target="tpu_custom_call", output_to_operand_aliasing={{0}: (9, {}), {1}: (10, {}), {2}: (11, {}), {3}: (12, {}), ... | custom-call | tf_op jit(solution)/shard_map/while/body/eval_jaxpr/block_forward/pallas_call | solution.py:597
  36.2 5.1 %collective-permute-start = (bf16[256,768]{1,0:T(8,128)(2,1)}, bf16[256,768]{1,0:T(8,128)(2,1)}, u32[]{:S(2)}, u32[]{:S(2)}) collective-permute-start(bf16[256,768]{1,0:T(8,128)(2,1)} %get-tuple-element.812), channel_id=1, source_target_pairs={{0,16},{16,32},{32,48},{48,64},{64,80},{80,96},{96,112},{1,17},{17... | collective-permute-start | bytes 1179656 | tf_op jit(solution)/shard_map/while/body/eval_jaxpr/ppermute | solution.py:605
  41.3 6.7 %collective-permute-done = bf16[256,768]{1,0:T(8,128)(2,1)} collective-permute-done((bf16[256,768]{1,0:T(8,128)(2,1)}, bf16[256,768]{1,0:T(8,128)(2,1)}, u32[]{:S(2)}, u32[]{:S(2)}) %collective-permute-start) | collective-permute-done | bytes 393248 | tf_op jit(solution)/shard_map/while/body/eval_jaxpr/ppermute | solution.py:605
  48.0 1.0 block_forward.7
  49.0 15.3 %collective-permute-start = (bf16[256,768]{1,0:T(8,128)(2,1)}, bf16[256,768]{1,0:T(8,128)(2,1)}, u32[]{:S(2)}, u32[]{:S(2)}) collective-permute-start(bf16[256,768]{1,0:T(8,128)(2,1)} %get-tuple-element.812), channel_id=1, source_target_pairs={{0,16},{16,32},{32,48},{48,64},{64,80},{80,96},{96,112},{1,17},{17... | collective-permute-start | bytes 1179656 | tf_op jit(solution)/shard_map/while/body/eval_jaxpr/ppermute | solution.py:605
  64.3 5.8 %collective-permute-done = bf16[256,768]{1,0:T(8,128)(2,1)} collective-permute-done((bf16[256,768]{1,0:T(8,128)(2,1)}, bf16[256,768]{1,0:T(8,128)(2,1)}, u32[]{:S(2)}, u32[]{:S(2)}) %collective-permute-start) | collective-permute-done | bytes 393248 | tf_op jit(solution)/shard_map/while/body/eval_jaxpr/ppermute | solution.py:605
  70.1 1.0 block_forward.7
  71.2 5.1 %collective-permute-start = (bf16[256,768]{1,0:T(8,128)(2,1)}, bf16[256,768]{1,0:T(8,128)(2,1)}, u32[]{:S(2)}, u32[]{:S(2)}) collective-permute-start(bf16[256,768]{1,0:T(8,128)(2,1)} %get-tuple-element.812), channel_id=1, source_target_pairs={{0,16},{16,32},{32,48},{48,64},{64,80},{80,96},{96,112},{1,17},{17... | collective-permute-start | bytes 1179656 | tf_op jit(solution)/shard_map/while/body/eval_jaxpr/ppermute | solution.py:605
  76.3 4.9 collective-permute-done
  82.3 15.5 %collective-permute-start = (bf16[256,768]{1,0:T(8,128)(2,1)}, bf16[256,768]{1,0:T(8,128)(2,1)}, u32[]{:S(2)}, u32[]{:S(2)}) collective-permute-start(bf16[256,768]{1,0:T(8,128)(2,1)} %get-tuple-element.812), channel_id=1, source_target_pairs={{0,16},{16,32},{32,48},{48,64},{64,80},{80,96},{96,112},{1,17},{17... | collective-permute-start | bytes 1179656 | tf_op jit(solution)/shard_map/while/body/eval_jaxpr/ppermute | solution.py:605
  97.8 4.9 collective-permute-done
  103.7 6.0 %collective-permute-start = (bf16[256,768]{1,0:T(8,128)(2,1)}, bf16[256,768]{1,0:T(8,128)(2,1)}, u32[]{:S(2)}, u32[]{:S(2)}) collective-permute-start(bf16[256,768]{1,0:T(8,128)(2,1)} %get-tuple-element.812), channel_id=1, source_target_pairs={{0,16},{16,32},{32,48},{48,64},{64,80},{80,96},{96,112},{1,17},{17... | collective-permute-start | bytes 1179656 | tf_op jit(solution)/shard_map/while/body/eval_jaxpr/ppermute | solution.py:605
  109.7 4.9 collective-permute-done
  115.6 12.2 %collective-permute-start = (bf16[256,768]{1,0:T(8,128)(2,1)}, bf16[256,768]{1,0:T(8,128)(2,1)}, u32[]{:S(2)}, u32[]{:S(2)}) collective-permute-start(bf16[256,768]{1,0:T(8,128)(2,1)} %get-tuple-element.812), channel_id=1, source_target_pairs={{0,16},{16,32},{32,48},{48,64},{64,80},{80,96},{96,112},{1,17},{17... | collective-permute-start | bytes 1179656 | tf_op jit(solution)/shard_map/while/body/eval_jaxpr/ppermute | solution.py:605
  127.9 4.9 collective-permute-done
  133.8 6.0 %collective-permute-start = (bf16[256,768]{1,0:T(8,128)(2,1)}, bf16[256,768]{1,0:T(8,128)(2,1)}, u32[]{:S(2)}, u32[]{:S(2)}) collective-permute-start(bf16[256,768]{1,0:T(8,128)(2,1)} %get-tuple-element.812), channel_id=1, source_target_pairs={{0,16},{16,32},{32,48},{48,64},{64,80},{80,96},{96,112},{1,17},{17... | collective-permute-start | bytes 1179656 | tf_op jit(solution)/shard_map/while/body/eval_jaxpr/ppermute | solution.py:605
  139.8 4.9 collective-permute-done
  144.7 1.2 block_forward.6
  145.9 219.0 %while.47 = (s32[]{:T(128)}, bf16[256,768]{1,0:T(8,128)(2,1)}, bf16[2,256,768]{2,1,0:T(8,128)(2,1)}, bf16[2,256,3072]{2,1,0:T(8,128)(2,1)}, bf16[2,256,768]{2,1,...) while((s32[]{:T(128)}, bf16[256,768]{1,0:T(8,128)(2,1)}, ...), condition=%wide.region_3.4_spmd, body=%wide.region_2.3_spmd.sunk | while | flops 2 | bytes 1573045 | solution.py:622
  147.0 1.3 collective-permute-start.1
  148.3 17.8 %collective-permute-done.1 = bf16[256,768]{1,0:T(8,128)(2,1)} collective-permute-done((bf16[256,768]{1,0:T(8,128)(2,1)}, bf16[256,768]{1,0:T(8,128)(2,1)}, u32[]{:S(2)}, u32[]{:S(2)}) %collective-permute-start.1) | collective-permute-done | bytes 393248 | tf_op jit(solution)/shard_map/while/body/eval_jaxpr/ppermute | solution.py:620
  167.1 1.3 collective-permute-start.1
  168.4 9.8 %collective-permute-done.1 = bf16[256,768]{1,0:T(8,128)(2,1)} collective-permute-done((bf16[256,768]{1,0:T(8,128)(2,1)}, bf16[256,768]{1,0:T(8,128)(2,1)}, u32[]{:S(2)}, u32[]{:S(2)}) %collective-permute-start.1) | collective-permute-done | bytes 393248 | tf_op jit(solution)/shard_map/while/body/eval_jaxpr/ppermute | solution.py:620
  179.2 1.3 collective-permute-start.1
  180.5 20.2 %collective-permute-done.1 = bf16[256,768]{1,0:T(8,128)(2,1)} collective-permute-done((bf16[256,768]{1,0:T(8,128)(2,1)}, bf16[256,768]{1,0:T(8,128)(2,1)}, u32[]{:S(2)}, u32[]{:S(2)}) %collective-permute-start.1) | collective-permute-done | bytes 393248 | tf_op jit(solution)/shard_map/while/body/eval_jaxpr/ppermute | solution.py:620
  201.8 1.3 collective-permute-start.1
  203.1 8.7 %collective-permute-done.1 = bf16[256,768]{1,0:T(8,128)(2,1)} collective-permute-done((bf16[256,768]{1,0:T(8,128)(2,1)}, bf16[256,768]{1,0:T(8,128)(2,1)}, u32[]{:S(2)}, u32[]{:S(2)}) %collective-permute-start.1) | collective-permute-done | bytes 393248 | tf_op jit(solution)/shard_map/while/body/eval_jaxpr/ppermute | solution.py:620
  212.8 1.3 collective-permute-start.1
  214.1 24.5 %collective-permute-done.1 = bf16[256,768]{1,0:T(8,128)(2,1)} collective-permute-done((bf16[256,768]{1,0:T(8,128)(2,1)}, bf16[256,768]{1,0:T(8,128)(2,1)}, u32[]{:S(2)}, u32[]{:S(2)}) %collective-permute-start.1) | collective-permute-done | bytes 393248 | tf_op jit(solution)/shard_map/while/body/eval_jaxpr/ppermute | solution.py:620
  239.6 1.3 collective-permute-start.1
  240.9 8.7 %collective-permute-done.1 = bf16[256,768]{1,0:T(8,128)(2,1)} collective-permute-done((bf16[256,768]{1,0:T(8,128)(2,1)}, bf16[256,768]{1,0:T(8,128)(2,1)}, u32[]{:S(2)}, u32[]{:S(2)}) %collective-permute-start.1) | collective-permute-done | bytes 393248 | tf_op jit(solution)/shard_map/while/body/eval_jaxpr/ppermute | solution.py:620
  250.6 1.3 collective-permute-start.1
  251.9 89.2 %collective-permute-done.1 = bf16[256,768]{1,0:T(8,128)(2,1)} collective-permute-done((bf16[256,768]{1,0:T(8,128)(2,1)}, bf16[256,768]{1,0:T(8,128)(2,1)}, u32[]{:S(2)}, u32[]{:S(2)}) %collective-permute-start.1) | collective-permute-done | bytes 393248 | tf_op jit(solution)/shard_map/while/body/eval_jaxpr/ppermute | solution.py:620
  341.1 9.5 %block_backward.7 = (bf16[2,256,768]{2,1,0:T(8,128)(2,1)}, bf16[2,256,3072]{2,1,0:T(8,128)(2,1)}, bf16[2,256,768]{2,1,0:T(8,128)(2,1)}, bf16[256,768]{1,0:T(8,128)(2,1)}) custom-call(s32[1]{0:T(128)} %bitcast.97.tick, s32[2]{0:T(128)S(1)} %get-tuple-element.924.place, ...), custom_call_target="tpu_custom_call", output_to_operand_aliasing={{0}: (11, {}), {1}: (12, {}), {2}: (13, {})} | custom-call | tf_op jit(solution)/shard_map/while/body/eval_jaxpr/block_backward/pallas_call | solution.py:612
  350.6 1.3 collective-permute-start.1
  351.9 13.0 %collective-permute-done.1 = bf16[256,768]{1,0:T(8,128)(2,1)} collective-permute-done((bf16[256,768]{1,0:T(8,128)(2,1)}, bf16[256,768]{1,0:T(8,128)(2,1)}, u32[]{:S(2)}, u32[]{:S(2)}) %collective-permute-start.1) | collective-permute-done | bytes 393248 | tf_op jit(solution)/shard_map/while/body/eval_jaxpr/ppermute | solution.py:620
  364.9 9.5 %block_backward.6 = (bf16[2,256,768]{2,1,0:T(8,128)(2,1)}, bf16[2,256,3072]{2,1,0:T(8,128)(2,1)}, bf16[2,256,768]{2,1,0:T(8,128)(2,1)}, bf16[256,768]{1,0:T(8,128)(2,1)}) custom-call(s32[1]{0:T(128)} %constant.180.clone.1.tick, s32[2]{0:T(128)S(1)} %get-tuple-element.984, ...), custom_call_target="tpu_custom_call", output_to_operand_aliasing={{0}: (11, {}), {1}: (12, {}), {2}: (13, {})} | custom-call | tf_op jit(solution)/shard_map/block_backward/pallas_call | solution.py:612
  375.1 25.4 %weight_grads.1 = (bf16[2,1984,128]{2,1,0:T(8,128)(2,1)}, bf16[2,1984,128]{2,1,0:T(8,128)(2,1)}, bf16[2,1984,128]{2,1,0:T(8,128)(2,1)}, bf16[2,1984,128]{2,1,0:T...) custom-call(s32[49]{0:T(128)} %bitcast.107, ...), custom_call_target="tpu_custom_call" | custom-call | tf_op jit(solution)/shard_map/weight_grads/pallas_call | solution.py:631
  401.6 1.8 collective-permute-done.5
  403.4 1.5 fusion.7
  404.9 5.6 %collective-permute-start.6 = (bf16[1984,128]{1,0:T(8,128)(2,1)S(1)}, bf16[1984,128]{1,0:T(8,128)(2,1)S(1)}, u32[]{:S(2)}, u32[]{:S(2)}) collective-permute-start(bf16[1984,128]{1,0:T(8,128)(2,1)S(1)} %get-tuple-element.630), channel_id=1, source_target_pairs={{0,2},{1,3},{2,4},{3,5},{4,6},{5,7},{6,0},{7,1},{8,10},{9,11},{10,... | collective-permute-start | bytes 1523720 | tf_op jit(solution)/shard_map/ppermute | solution.py:448
  410.5 1.4 collective-permute-start.9
  412.4 4.4 collective-permute-start.15
  416.7 7.0 %collective-permute-done.6 = bf16[1984,128]{1,0:T(8,128)(2,1)S(1)} collective-permute-done((bf16[1984,128]{1,0:T(8,128)(2,1)S(1)}, bf16[1984,128]{1,0:T(8,128)(2,1)S(1)}, u32[]{:S(2)}, u32[]{:S(2)}) %collective-permute-start.6) | collective-permute-done | bytes 507936 | tf_op jit(solution)/shard_map/ppermute | solution.py:448
  423.7 4.1 collective-permute-start.19
  428.2 1.6 collective-permute-start.10
  430.3 4.5 collective-permute-done.15
  434.8 16.3 %collective-permute-done.19 = bf16[4,752,128]{2,1,0:T(8,128)(2,1)S(1)} collective-permute-done((bf16[4,752,128]{2,1,0:T(8,128)(2,1)S(1)}, bf16[4,752,128]{2,1,0:T(8,128)(2,1)S(1)}, u32[]{:S(2)}, u32[]{:S(2)}) %collective-permute-start.19) | collective-permute-done | bytes 770080 | tf_op jit(solution)/shard_map/ppermute | solution.py:448
  451.9 3.1 collective-permute-start.11
  455.0 4.1 collective-permute-done.16
  459.8 2.8 collective-permute-start.20
  462.6 5.6 %collective-permute-done.17 = bf16[752,128]{1,0:T(8,128)(2,1)S(1)} collective-permute-done((bf16[752,128]{1,0:T(8,128)(2,1)S(1)}, bf16[752,128]{1,0:T(8,128)(2,1)S(1)}, u32[]{:S(2)}, u32[]{:S(2)}) %collective-permute-start.17) | collective-permute-done | bytes 192544 | tf_op jit(solution)/shard_map/ppermute | solution.py:448
  468.6 3.0 collective-permute-start.12
  471.7 9.6 %collective-permute-done.18 = bf16[752,128]{1,0:T(8,128)(2,1)S(1)} collective-permute-done((bf16[752,128]{1,0:T(8,128)(2,1)S(1)}, bf16[752,128]{1,0:T(8,128)(2,1)S(1)}, u32[]{:S(2)}, u32[]{:S(2)}) %collective-permute-start.18) | collective-permute-done | bytes 192544 | tf_op jit(solution)/shard_map/ppermute | solution.py:448
  481.6 5.8 %collective-permute-done.21 = bf16[752,128]{1,0:T(8,128)(2,1)S(1)} collective-permute-done((bf16[752,128]{1,0:T(8,128)(2,1)S(1)}, bf16[752,128]{1,0:T(8,128)(2,1)S(1)}, u32[]{:S(2)}, u32[]{:S(2)}) %collective-permute-start.21) | collective-permute-done | bytes 192544 | tf_op jit(solution)/shard_map/ppermute | solution.py:448
  487.5 1.1 collective-permute-start.22
  488.9 4.3 collective-permute-done.22
  494.3 11.3 %adam.1 = (f32[871,4,128]{2,1,0:T(4,128)}, f32[871,4,128]{2,1,0:T(4,128)}, f32[871,4,128]{2,1,0:T(4,128)}) custom-call(bf16[3488,128]{1,0:T(8,128)(2,1)} %pad_maximum_fusion.g_i, f32[871,4,128]{2,1,0:T(4,128)} %bitcast.104, f32[871,4,128]{2,1,0:T(4,128)} %bitcast.105, f32[871,4,128]{2,1,0:T(4,128)} %bitcast.106), custom_call_target="tpu_custom_call" | custom-call | tf_op jit(solution)/shard_map/adam/pallas_call | solution.py:666
  (66 shorter events, 18.1 us)
Async XLA Ops:
  15.4 9.5 %collective-permute-start = (bf16[256,768]{1,0:T(8,128)(2,1)}, bf16[256,768]{1,0:T(8,128)(2,1)}, u32[]{:S(2)}, u32[]{:S(2)}) collective-permute-start(bf16[256,768]{1,0:T(8,128)(2,1)} %get-tuple-element.812), channel_id=1, source_target_pairs={{0,16},{16,32},{32,48},{48,64},{64,80},{80,96},{96,112},{1,17},{17... | collective-permute-start | bytes 1179656 | tf_op jit(solution)/shard_map/while/body/eval_jaxpr/ppermute | solution.py:605
  36.2 11.8 %collective-permute-start = (bf16[256,768]{1,0:T(8,128)(2,1)}, bf16[256,768]{1,0:T(8,128)(2,1)}, u32[]{:S(2)}, u32[]{:S(2)}) collective-permute-start(bf16[256,768]{1,0:T(8,128)(2,1)} %get-tuple-element.812), channel_id=1, source_target_pairs={{0,16},{16,32},{32,48},{48,64},{64,80},{80,96},{96,112},{1,17},{17... | collective-permute-start | bytes 1179656 | tf_op jit(solution)/shard_map/while/body/eval_jaxpr/ppermute | solution.py:605
  49.0 21.1 %collective-permute-start = (bf16[256,768]{1,0:T(8,128)(2,1)}, bf16[256,768]{1,0:T(8,128)(2,1)}, u32[]{:S(2)}, u32[]{:S(2)}) collective-permute-start(bf16[256,768]{1,0:T(8,128)(2,1)} %get-tuple-element.812), channel_id=1, source_target_pairs={{0,16},{16,32},{32,48},{48,64},{64,80},{80,96},{96,112},{1,17},{17... | collective-permute-start | bytes 1179656 | tf_op jit(solution)/shard_map/while/body/eval_jaxpr/ppermute | solution.py:605
  71.2 10.1 %collective-permute-start = (bf16[256,768]{1,0:T(8,128)(2,1)}, bf16[256,768]{1,0:T(8,128)(2,1)}, u32[]{:S(2)}, u32[]{:S(2)}) collective-permute-start(bf16[256,768]{1,0:T(8,128)(2,1)} %get-tuple-element.812), channel_id=1, source_target_pairs={{0,16},{16,32},{32,48},{48,64},{64,80},{80,96},{96,112},{1,17},{17... | collective-permute-start | bytes 1179656 | tf_op jit(solution)/shard_map/while/body/eval_jaxpr/ppermute | solution.py:605
  82.3 20.3 %collective-permute-start = (bf16[256,768]{1,0:T(8,128)(2,1)}, bf16[256,768]{1,0:T(8,128)(2,1)}, u32[]{:S(2)}, u32[]{:S(2)}) collective-permute-start(bf16[256,768]{1,0:T(8,128)(2,1)} %get-tuple-element.812), channel_id=1, source_target_pairs={{0,16},{16,32},{32,48},{48,64},{64,80},{80,96},{96,112},{1,17},{17... | collective-permute-start | bytes 1179656 | tf_op jit(solution)/shard_map/while/body/eval_jaxpr/ppermute | solution.py:605
  103.7 10.9 %collective-permute-start = (bf16[256,768]{1,0:T(8,128)(2,1)}, bf16[256,768]{1,0:T(8,128)(2,1)}, u32[]{:S(2)}, u32[]{:S(2)}) collective-permute-start(bf16[256,768]{1,0:T(8,128)(2,1)} %get-tuple-element.812), channel_id=1, source_target_pairs={{0,16},{16,32},{32,48},{48,64},{64,80},{80,96},{96,112},{1,17},{17... | collective-permute-start | bytes 1179656 | tf_op jit(solution)/shard_map/while/body/eval_jaxpr/ppermute | solution.py:605
  115.6 17.1 %collective-permute-start = (bf16[256,768]{1,0:T(8,128)(2,1)}, bf16[256,768]{1,0:T(8,128)(2,1)}, u32[]{:S(2)}, u32[]{:S(2)}) collective-permute-start(bf16[256,768]{1,0:T(8,128)(2,1)} %get-tuple-element.812), channel_id=1, source_target_pairs={{0,16},{16,32},{32,48},{48,64},{64,80},{80,96},{96,112},{1,17},{17... | collective-permute-start | bytes 1179656 | tf_op jit(solution)/shard_map/while/body/eval_jaxpr/ppermute | solution.py:605
  133.8 10.9 %collective-permute-start = (bf16[256,768]{1,0:T(8,128)(2,1)}, bf16[256,768]{1,0:T(8,128)(2,1)}, u32[]{:S(2)}, u32[]{:S(2)}) collective-permute-start(bf16[256,768]{1,0:T(8,128)(2,1)} %get-tuple-element.812), channel_id=1, source_target_pairs={{0,16},{16,32},{32,48},{48,64},{64,80},{80,96},{96,112},{1,17},{17... | collective-permute-start | bytes 1179656 | tf_op jit(solution)/shard_map/while/body/eval_jaxpr/ppermute | solution.py:605
  144.7 1.2 copy-start.5
  147.0 19.1 %collective-permute-start.1 = (bf16[256,768]{1,0:T(8,128)(2,1)}, bf16[256,768]{1,0:T(8,128)(2,1)}, u32[]{:S(2)}, u32[]{:S(2)}) collective-permute-start(bf16[256,768]{1,0:T(8,128)(2,1)} %get-tuple-element.834), channel_id=1, source_target_pairs={{16,0},{32,16},{48,32},{64,48},{80,64},{96,80},{112,96},{17,1},{33... | collective-permute-start | bytes 1179656 | tf_op jit(solution)/shard_map/while/body/eval_jaxpr/ppermute | solution.py:620
  167.1 11.1 %collective-permute-start.1 = (bf16[256,768]{1,0:T(8,128)(2,1)}, bf16[256,768]{1,0:T(8,128)(2,1)}, u32[]{:S(2)}, u32[]{:S(2)}) collective-permute-start(bf16[256,768]{1,0:T(8,128)(2,1)} %get-tuple-element.834), channel_id=1, source_target_pairs={{16,0},{32,16},{48,32},{64,48},{80,64},{96,80},{112,96},{17,1},{33... | collective-permute-start | bytes 1179656 | tf_op jit(solution)/shard_map/while/body/eval_jaxpr/ppermute | solution.py:620
  179.2 21.5 %collective-permute-start.1 = (bf16[256,768]{1,0:T(8,128)(2,1)}, bf16[256,768]{1,0:T(8,128)(2,1)}, u32[]{:S(2)}, u32[]{:S(2)}) collective-permute-start(bf16[256,768]{1,0:T(8,128)(2,1)} %get-tuple-element.834), channel_id=1, source_target_pairs={{16,0},{32,16},{48,32},{64,48},{80,64},{96,80},{112,96},{17,1},{33... | collective-permute-start | bytes 1179656 | tf_op jit(solution)/shard_map/while/body/eval_jaxpr/ppermute | solution.py:620
  201.8 10.0 %collective-permute-start.1 = (bf16[256,768]{1,0:T(8,128)(2,1)}, bf16[256,768]{1,0:T(8,128)(2,1)}, u32[]{:S(2)}, u32[]{:S(2)}) collective-permute-start(bf16[256,768]{1,0:T(8,128)(2,1)} %get-tuple-element.834), channel_id=1, source_target_pairs={{16,0},{32,16},{48,32},{64,48},{80,64},{96,80},{112,96},{17,1},{33... | collective-permute-start | bytes 1179656 | tf_op jit(solution)/shard_map/while/body/eval_jaxpr/ppermute | solution.py:620
  212.8 25.8 %collective-permute-start.1 = (bf16[256,768]{1,0:T(8,128)(2,1)}, bf16[256,768]{1,0:T(8,128)(2,1)}, u32[]{:S(2)}, u32[]{:S(2)}) collective-permute-start(bf16[256,768]{1,0:T(8,128)(2,1)} %get-tuple-element.834), channel_id=1, source_target_pairs={{16,0},{32,16},{48,32},{64,48},{80,64},{96,80},{112,96},{17,1},{33... | collective-permute-start | bytes 1179656 | tf_op jit(solution)/shard_map/while/body/eval_jaxpr/ppermute | solution.py:620
  239.6 10.0 %collective-permute-start.1 = (bf16[256,768]{1,0:T(8,128)(2,1)}, bf16[256,768]{1,0:T(8,128)(2,1)}, u32[]{:S(2)}, u32[]{:S(2)}) collective-permute-start(bf16[256,768]{1,0:T(8,128)(2,1)} %get-tuple-element.834), channel_id=1, source_target_pairs={{16,0},{32,16},{48,32},{64,48},{80,64},{96,80},{112,96},{17,1},{33... | collective-permute-start | bytes 1179656 | tf_op jit(solution)/shard_map/while/body/eval_jaxpr/ppermute | solution.py:620
  250.6 90.5 %collective-permute-start.1 = (bf16[256,768]{1,0:T(8,128)(2,1)}, bf16[256,768]{1,0:T(8,128)(2,1)}, u32[]{:S(2)}, u32[]{:S(2)}) collective-permute-start(bf16[256,768]{1,0:T(8,128)(2,1)} %get-tuple-element.834), channel_id=1, source_target_pairs={{16,0},{32,16},{48,32},{64,48},{80,64},{96,80},{112,96},{17,1},{33... | collective-permute-start | bytes 1179656 | tf_op jit(solution)/shard_map/while/body/eval_jaxpr/ppermute | solution.py:620
  350.6 14.3 %collective-permute-start.1 = (bf16[256,768]{1,0:T(8,128)(2,1)}, bf16[256,768]{1,0:T(8,128)(2,1)}, u32[]{:S(2)}, u32[]{:S(2)}) collective-permute-start(bf16[256,768]{1,0:T(8,128)(2,1)} %get-tuple-element.834), channel_id=1, source_target_pairs={{16,0},{32,16},{48,32},{64,48},{80,64},{96,80},{112,96},{17,1},{33... | collective-permute-start | bytes 1179656 | tf_op jit(solution)/shard_map/while/body/eval_jaxpr/ppermute | solution.py:620
  400.5 11.4 %copy-start.7 = (bf16[2,1984,128]{2,1,0:T(8,128)(2,1)S(1)}, bf16[2,1984,128]{2,1,0:T(8,128)(2,1)}, u32[]{:S(2)}) copy-start(bf16[2,1984,128]{2,1,0:T(8,128)(2,1)} %get-tuple-element.540) | copy-start | bytes 3047428
  400.5 11.4 %copy-start = (bf16[8,752,128]{2,1,0:T(8,128)(2,1)S(1)}, bf16[8,752,128]{2,1,0:T(8,128)(2,1)}, u32[]{:S(2)}) copy-start(bf16[8,752,128]{2,1,0:T(8,128)(2,1)} %get-tuple-element.547) | copy-start | bytes 4620292
  400.5 2.9 collective-permute-start.5
  400.6 11.3 %collective-permute-start.14 = (bf16[8,752,128]{2,1,0:T(8,128)(2,1)}, bf16[8,752,128]{2,1,0:T(8,128)(2,1)S(1)}, u32[]{:S(2)}, u32[]{:S(2)}) collective-permute-start(bf16[8,752,128]{2,1,0:T(8,128)(2,1)} %get-tuple-element.548), channel_id=1, source_target_pairs={{0,1},{1,0},{2,3},{3,2},{4,5},{5,4},{6,7},{7,6},{8,9},{9,8},{10,11... | collective-permute-start | bytes 4620296 | tf_op jit(solution)/shard_map/ppermute | solution.py:448
  401.1 11.3 %collective-permute-start.4 = (bf16[2,1984,128]{2,1,0:T(8,128)(2,1)}, bf16[2,1984,128]{2,1,0:T(8,128)(2,1)S(1)}, u32[]{:S(2)}, u32[]{:S(2)}) collective-permute-start(bf16[2,1984,128]{2,1,0:T(8,128)(2,1)} %get-tuple-element.542), channel_id=1, source_target_pairs={{0,1},{1,0},{2,3},{3,2},{4,5},{5,4},{6,7},{7,6},{8,9},{9,8},{10,11... | collective-permute-start | bytes 3047432 | tf_op jit(solution)/shard_map/ppermute | solution.py:448
  401.2 28.6 %collective-permute-start.13 = (bf16[8,752,128]{2,1,0:T(8,128)(2,1)}, bf16[8,752,128]{2,1,0:T(8,128)(2,1)S(1)}, u32[]{:S(2)}, u32[]{:S(2)}) collective-permute-start(bf16[8,752,128]{2,1,0:T(8,128)(2,1)} %get-tuple-element.546), channel_id=1, source_target_pairs={{0,1},{1,0},{2,3},{3,2},{4,5},{5,4},{6,7},{7,6},{8,9},{9,8},{10,11... | collective-permute-start | bytes 4620296 | tf_op jit(solution)/shard_map/ppermute | solution.py:448
  404.9 18.8 %collective-permute-start.6 = (bf16[1984,128]{1,0:T(8,128)(2,1)S(1)}, bf16[1984,128]{1,0:T(8,128)(2,1)S(1)}, u32[]{:S(2)}, u32[]{:S(2)}) collective-permute-start(bf16[1984,128]{1,0:T(8,128)(2,1)S(1)} %get-tuple-element.630), channel_id=1, source_target_pairs={{0,2},{1,3},{2,4},{3,5},{4,6},{5,7},{6,0},{7,1},{8,10},{9,11},{10,... | collective-permute-start | bytes 1523720 | tf_op jit(solution)/shard_map/ppermute | solution.py:448
  410.5 17.3 %collective-permute-start.9 = (bf16[1984,128]{1,0:T(8,128)(2,1)S(1)}, bf16[1984,128]{1,0:T(8,128)(2,1)S(1)}, u32[]{:S(2)}, u32[]{:S(2)}) collective-permute-start(bf16[1984,128]{1,0:T(8,128)(2,1)S(1)} %get-tuple-element.631), channel_id=1, source_target_pairs={{0,6},{1,7},{2,0},{3,1},{4,2},{5,3},{6,4},{7,5},{8,14},{9,15},{10,... | collective-permute-start | bytes 1523720 | tf_op jit(solution)/shard_map/ppermute | solution.py:448
  411.9 39.6 %collective-permute-start.3 = (bf16[2,1984,128]{2,1,0:T(8,128)(2,1)S(1)}, bf16[2,1984,128]{2,1,0:T(8,128)(2,1)S(1)}, u32[]{:S(2)}, u32[]{:S(2)}) collective-permute-start(bf16[2,1984,128]{2,1,0:T(8,128)(2,1)S(1)} %copy-done.7), channel_id=1, source_target_pairs={{0,1},{1,0},{2,3},{3,2},{4,5},{5,4},{6,7},{7,6},{8,9},{9,8},{10,11... | collective-permute-start | bytes 3047432 | tf_op jit(solution)/shard_map/ppermute | solution.py:448
  411.9 15.9 %copy-start.4 = (bf16[2,1984,128]{2,1,0:T(8,128)(2,1)S(1)}, bf16[2,1984,128]{2,1,0:T(8,128)(2,1)}, u32[]{:S(2)}) copy-start(bf16[2,1984,128]{2,1,0:T(8,128)(2,1)} %get-tuple-element.541) | copy-start | bytes 3047428
  412.4 22.4 %collective-permute-start.15 = (bf16[4,752,128]{2,1,0:T(8,128)(2,1)S(1)}, bf16[4,752,128]{2,1,0:T(8,128)(2,1)S(1)}, u32[]{:S(2)}, u32[]{:S(2)}) collective-permute-start(bf16[4,752,128]{2,1,0:T(8,128)(2,1)S(1)} %get-tuple-element.624), channel_id=1, source_target_pairs={{0,8},{1,9},{2,10},{3,11},{4,12},{5,13},{6,14},{7,15},{8,0},{9,1},... | collective-permute-start | bytes 2310152 | tf_op jit(solution)/shard_map/ppermute | solution.py:448
  423.7 27.4 %collective-permute-start.19 = (bf16[4,752,128]{2,1,0:T(8,128)(2,1)S(1)}, bf16[4,752,128]{2,1,0:T(8,128)(2,1)S(1)}, u32[]{:S(2)}, u32[]{:S(2)}) collective-permute-start(bf16[4,752,128]{2,1,0:T(8,128)(2,1)S(1)} %get-tuple-element.625), channel_id=1, source_target_pairs={{0,8},{1,9},{2,10},{3,11},{4,12},{5,13},{6,14},{7,15},{8,0},{9,1},... | collective-permute-start | bytes 2310152 | tf_op jit(solution)/shard_map/ppermute | solution.py:448
  427.8 7.0 %copy-start.6 = (bf16[2,1984,128]{2,1,0:T(8,128)(2,1)S(1)}, bf16[2,1984,128]{2,1,0:T(8,128)(2,1)}, u32[]{:S(2)}) copy-start(bf16[2,1984,128]{2,1,0:T(8,128)(2,1)} %get-tuple-element.538) | copy-start | bytes 3047428
  427.8 23.3 %copy-start.1 = (bf16[8,752,128]{2,1,0:T(8,128)(2,1)S(1)}, bf16[8,752,128]{2,1,0:T(8,128)(2,1)}, u32[]{:S(2)}) copy-start(bf16[8,752,128]{2,1,0:T(8,128)(2,1)} %get-tuple-element.545) | copy-start | bytes 4620292
  428.2 23.3 %copy-start.3 = (bf16[2,1984,128]{2,1,0:T(8,128)(2,1)S(1)}, bf16[2,1984,128]{2,1,0:T(8,128)(2,1)}, u32[]{:S(2)}) copy-start(bf16[2,1984,128]{2,1,0:T(8,128)(2,1)} %get-tuple-element.539) | copy-start | bytes 3047428
  428.2 23.3 %collective-permute-start.10 = (bf16[1984,128]{1,0:T(8,128)(2,1)S(1)}, bf16[1984,128]{1,0:T(8,128)(2,1)S(1)}, u32[]{:S(2)}, u32[]{:S(2)}) collective-permute-start(bf16[1984,128]{1,0:T(8,128)(2,1)S(1)} %get-tuple-element.629), channel_id=1, source_target_pairs={{0,6},{1,7},{2,0},{3,1},{4,2},{5,3},{6,4},{7,5},{8,14},{9,15},{10,... | collective-permute-start | bytes 1523720 | tf_op jit(solution)/shard_map/ppermute | solution.py:448
  429.8 21.7 %collective-permute-start.7 = (bf16[1984,128]{1,0:T(8,128)(2,1)S(1)}, bf16[1984,128]{1,0:T(8,128)(2,1)S(1)}, u32[]{:S(2)}, u32[]{:S(2)}) collective-permute-start(bf16[1984,128]{1,0:T(8,128)(2,1)S(1)} %get-tuple-element.628), channel_id=1, source_target_pairs={{0,2},{1,3},{2,4},{3,5},{4,6},{5,7},{6,0},{7,1},{8,10},{9,11},{10,... | collective-permute-start | bytes 1523720 | tf_op jit(solution)/shard_map/ppermute | solution.py:448
  434.8 33.6 %collective-permute-start.2 = (bf16[2,1984,128]{2,1,0:T(8,128)(2,1)S(1)}, bf16[2,1984,128]{2,1,0:T(8,128)(2,1)S(1)}, u32[]{:S(2)}, u32[]{:S(2)}) collective-permute-start(bf16[2,1984,128]{2,1,0:T(8,128)(2,1)S(1)} %copy-done.6), channel_id=1, source_target_pairs={{0,1},{1,0},{2,3},{3,2},{4,5},{5,4},{6,7},{7,6},{8,9},{9,8},{10,11... | collective-permute-start | bytes 3047432 | tf_op jit(solution)/shard_map/ppermute | solution.py:448
  451.2 7.9 %collective-permute-start.16 = (bf16[752,128]{1,0:T(8,128)(2,1)S(1)}, bf16[752,128]{1,0:T(8,128)(2,1)S(1)}, u32[]{:S(2)}, u32[]{:S(2)}) collective-permute-start(bf16[752,128]{1,0:T(8,128)(2,1)S(1)} %get-tuple-element.622), channel_id=1, source_target_pairs={{0,2},{1,3},{2,4},{3,5},{4,6},{5,7},{6,0},{7,1},{8,10},{9,11},{10,... | collective-permute-start | bytes 577544 | tf_op jit(solution)/shard_map/ppermute | solution.py:448
  451.9 16.5 %copy-start.2 = (bf16[2,1984,128]{2,1,0:T(8,128)(2,1)S(1)}, bf16[2,1984,128]{2,1,0:T(8,128)(2,1)}, u32[]{:S(2)}) copy-start(bf16[2,1984,128]{2,1,0:T(8,128)(2,1)} %get-tuple-element.537) | copy-start | bytes 3047428
  451.9 16.5 %collective-permute-start.11 = (bf16[1984,128]{1,0:T(8,128)(2,1)S(1)}, bf16[1984,128]{1,0:T(8,128)(2,1)S(1)}, u32[]{:S(2)}, u32[]{:S(2)}) collective-permute-start(bf16[1984,128]{1,0:T(8,128)(2,1)S(1)} %get-tuple-element.627), channel_id=1, source_target_pairs={{0,6},{1,7},{2,0},{3,1},{4,2},{5,3},{6,4},{7,5},{8,14},{9,15},{10,... | collective-permute-start | bytes 1523720 | tf_op jit(solution)/shard_map/ppermute | solution.py:448
  459.2 9.0 %collective-permute-start.17 = (bf16[752,128]{1,0:T(8,128)(2,1)S(1)}, bf16[752,128]{1,0:T(8,128)(2,1)S(1)}, u32[]{:S(2)}, u32[]{:S(2)}) collective-permute-start(bf16[752,128]{1,0:T(8,128)(2,1)S(1)} %fusion.12), channel_id=1, source_target_pairs={{0,2},{1,3},{2,4},{3,5},{4,6},{5,7},{6,0},{7,1},{8,10},{9,11},{10,... | collective-permute-start | bytes 577544 | tf_op jit(solution)/shard_map/ppermute | solution.py:448
  459.3 29.3 %collective-permute-start.8 = (bf16[1984,128]{1,0:T(8,128)(2,1)S(1)}, bf16[1984,128]{1,0:T(8,128)(2,1)S(1)}, u32[]{:S(2)}, u32[]{:S(2)}) collective-permute-start(bf16[1984,128]{1,0:T(8,128)(2,1)S(1)} %get-tuple-element.626), channel_id=1, source_target_pairs={{0,2},{1,3},{2,4},{3,5},{4,6},{5,7},{6,0},{7,1},{8,10},{9,11},{10,... | collective-permute-start | bytes 1523720 | tf_op jit(solution)/shard_map/ppermute | solution.py:448
  459.8 11.9 %collective-permute-start.20 = (bf16[752,128]{1,0:T(8,128)(2,1)S(1)}, bf16[752,128]{1,0:T(8,128)(2,1)S(1)}, u32[]{:S(2)}, u32[]{:S(2)}) collective-permute-start(bf16[752,128]{1,0:T(8,128)(2,1)S(1)} %get-tuple-element.623), channel_id=1, source_target_pairs={{0,6},{1,7},{2,0},{3,1},{4,2},{5,3},{6,4},{7,5},{8,14},{9,15},{10,... | collective-permute-start | bytes 577544 | tf_op jit(solution)/shard_map/ppermute | solution.py:448
  468.3 13.0 %collective-permute-start.18 = (bf16[752,128]{1,0:T(8,128)(2,1)S(1)}, bf16[752,128]{1,0:T(8,128)(2,1)S(1)}, u32[]{:S(2)}, u32[]{:S(2)}) collective-permute-start(bf16[752,128]{1,0:T(8,128)(2,1)S(1)} %fusion.13), channel_id=1, source_target_pairs={{0,2},{1,3},{2,4},{3,5},{4,6},{5,7},{6,0},{7,1},{8,10},{9,11},{10,... | collective-permute-start | bytes 577544 | tf_op jit(solution)/shard_map/ppermute | solution.py:448
  468.6 20.0 %collective-permute-start.12 = (bf16[1984,128]{1,0:T(8,128)(2,1)S(1)}, bf16[1984,128]{1,0:T(8,128)(2,1)S(1)}, u32[]{:S(2)}, u32[]{:S(2)}) collective-permute-start(bf16[1984,128]{1,0:T(8,128)(2,1)S(1)} %fusion.2), channel_id=1, source_target_pairs={{0,8},{1,9},{2,10},{3,11},{4,12},{5,13},{6,14},{7,15},{8,0},{9,1},... | collective-permute-start | bytes 1523720 | tf_op jit(solution)/shard_map/ppermute | solution.py:448
  481.5 5.9 %collective-permute-start.21 = (bf16[752,128]{1,0:T(8,128)(2,1)S(1)}, bf16[752,128]{1,0:T(8,128)(2,1)S(1)}, u32[]{:S(2)}, u32[]{:S(2)}) collective-permute-start(bf16[752,128]{1,0:T(8,128)(2,1)S(1)} %get-tuple-element.621), channel_id=1, source_target_pairs={{0,6},{1,7},{2,0},{3,1},{4,2},{5,3},{6,4},{7,5},{8,14},{9,15},{10,... | collective-permute-start | bytes 577544 | tf_op jit(solution)/shard_map/ppermute | solution.py:448
  487.5 5.7 %collective-permute-start.22 = (bf16[752,128]{1,0:T(8,128)(2,1)S(1)}, bf16[752,128]{1,0:T(8,128)(2,1)S(1)}, u32[]{:S(2)}, u32[]{:S(2)}) collective-permute-start(bf16[752,128]{1,0:T(8,128)(2,1)S(1)} %fusion.10), channel_id=1, source_target_pairs={{0,6},{1,7},{2,0},{3,1},{4,2},{5,3},{6,4},{7,5},{8,14},{9,15},{10,... | collective-permute-start | bytes 577544 | tf_op jit(solution)/shard_map/ppermute | solution.py:448

commit v3 on v2

--- a/solution.py
+++ b/solution.py
@@ -19,6 +19,7 @@
 LANES = 128
 MARGIN = 8
 STEP = 64
+SLICE = 512
 F32 = jnp.float32
 BF16 = jnp.bfloat16
 ANY = pl.BlockSpec(memory_space=pl.ANY)
@@ -76,12 +77,36 @@
                 result[pl.ds(i * breadth + 8 * w, 8), columns] = sums[i][w]
 
 
+class Streamed:
+    def __init__(self, up, upv, down, downv, slope, slopev, sems):
+        half = up.shape[1] // 2
+        self.parts = []
+        for q in range(2):
+            cut = pl.ds(q * half, half)
+            self.parts.append(
+                (
+                    pltpu.make_async_copy(down.at[cut], downv.at[cut], sems.at[3 * q]),
+                    pltpu.make_async_copy(slope.at[:, cut], slopev.at[:, cut], sems.at[3 * q + 1]),
+                    pltpu.make_async_copy(up.at[:, cut], upv.at[:, cut], sems.at[3 * q + 2]),
+                )
+            )
+
+    def start(self):
+        for part in self.parts:
+            for cp in part:
+                cp.start()
+
+    def wait(self, q):
+        for cp in self.parts[q]:
+            cp.wait()
+
+
 def forward_kernel(
     dims, tick, place, roster, xr, images, taps, scale, up, down, *refs
 ):
     side, height, breadth, width = dims
     out_o, x_o, n_o, istd_o, hid_o, slope_o, branch_o, y = refs[7:15]
-    xv, pad, conv, nv, iv, upv, downv, hv, sv, acc, yv, sems = refs[15:]
+    xv, pad, conv, nv, iv, upv, downv, hv, sv, acc, bv, yv, sems = refs[15:]
     positions, channels = xv.shape
     micro = images.shape[0]
     reach = (side - 1) // 2
@@ -147,7 +172,8 @@
         h_out.start()
         s_out = pltpu.make_async_copy(sv, slope_o.at[slot], sems.at[9])
         s_out.start()
-        b_out = pltpu.make_async_copy(acc, branch_o.at[slot], sems.at[10])
+        bv[...] = acc[...].astype(BF16)
+        b_out = pltpu.make_async_copy(bv, branch_o.at[slot], sems.at[10])
         b_out.start()
         for cp in (x_out, n_out, i_out, y_out, o_out, h_out, s_out, b_out):
             cp.wait()
@@ -158,7 +184,7 @@
 ):
     side, height, breadth, width = dims
     go_o, gp_o, gc_o, g_in = refs[3:7]
-    gv, pad, conv, nv, iv, upv, downv, sv, gpv, acc, scaled, gcv, yv, sems = refs[7:]
+    gv, pad, conv, nv, iv, upv, downv, sv, gpv, acc, scaled, gcv, yv, sems, weight_sems = refs[7:]
     positions, channels = gv.shape
     micro = cotangent.shape[0]
     reach = (side - 1) // 2
@@ -166,18 +192,14 @@
 
     @pl.when((slot >= 0) & (slot < micro))
     def _():
-        down_in = pltpu.make_async_copy(down, downv, sems.at[0])
-        up_in = pltpu.make_async_copy(up, upv, sems.at[1])
-        s_in = pltpu.make_async_copy(slope_i.at[slot], sv, sems.at[3])
+        weights = Streamed(up, upv, down, downv, slope_i.at[slot], sv, weight_sems)
         n_in = pltpu.make_async_copy(n_i.at[slot], nv, sems.at[4])
         i_in = pltpu.make_async_copy(istd_i.at[slot], iv, sems.at[5])
 
         def begin(source):
             cp = pltpu.make_async_copy(source, gv, sems.at[2])
             cp.start()
-            down_in.start()
-            s_in.start()
-            up_in.start()
+            weights.start()
             n_in.start()
             i_in.start()
             cp.wait()
@@ -193,12 +215,11 @@
         go_out = pltpu.make_async_copy(gv, go_o.at[slot], sems.at[6])
         go_out.start()
         scaled[...] = (gv[...].astype(F32) * scale[...]).astype(BF16)
-        down_in.wait()
-        s_in.wait()
-        up_in.wait()
-        step = 512
+        step = SLICE
         across = (((1,), (1,)), ((), ()))
         for k in range(0, width, step):
+            if k % (width // 2) == 0:
+                weights.wait(k // (width // 2))
             grad_hidden = lax.dot_general(
                 scaled[...], downv[k : k + step, :], across, preferred_element_type=F32
             )
@@ -256,7 +277,7 @@
     scale_base = down_base + up_rows
     copies = []
     for q, (src, dst) in enumerate(
-        ((n_i, nv), (gp_i, gpv), (go_i, gv), (hid_i, hv), (x_i, xv), (gc_i, gcv), (branch_i, bv))
+        ((x_i, xv), (gc_i, gcv), (n_i, nv), (gp_i, gpv), (go_i, gv), (hid_i, hv), (branch_i, bv))
     ):
         for m in range(micro):
             cp = pltpu.make_async_copy(
@@ -275,7 +296,41 @@
         lengths[at] = bounds[b + 1] - bounds[b]
         counts[d] = counts[d] + 1
 
-    for cp in copies:
+    early = 2 * micro
+    for cp in copies[:early]:
+        cp.wait()
+    halves = breadth // 8
+    flat[:tap_rows, :] = jnp.zeros((tap_rows, LANES), F32)
+
+    @rolled(micro)
+    def _(m):
+        base = pl.multiple_of(m * positions, positions)
+        pad_map(pad, xv.at[pl.ds(base, positions)], reach, height, breadth)
+
+        @rolled(chunks)
+        def _(c):
+            columns = pl.ds(pl.multiple_of(c * LANES, LANES), LANES)
+            grads = [
+                gcv[pl.ds(base + 16 * i, 16), columns].astype(F32)
+                for i in range(positions // 16)
+            ]
+            for b in range(side):
+                sums = [None] * side
+                for r in range(reach, height + reach):
+                    for w in range(halves):
+                        value = pad[c, r, pl.ds(MARGIN - reach + b + 8 * w, 8), :]
+                        for a in range(side):
+                            i = r - a
+                            if 0 <= i < height:
+                                p = i * breadth + 8 * w
+                                term = value * grads[p // 16][p % 16 : p % 16 + 8]
+                                sums[a] = term if sums[a] is None else sums[a] + term
+                for a in range(side):
+                    total = jnp.sum(sums[a], axis=0, keepdims=True)
+                    at = pl.ds((a * side + b) * chunks + c, 1)
+                    flat[at, :] += total
+
+    for cp in copies[early:]:
         cp.wait()
     along = (((0,), (0,)), ((), ()))
     scaled[...] = (gv[...].astype(F32) * scale[...]).astype(BF16)
@@ -295,41 +350,11 @@
             flat[pl.ds(down_base + j + q, width, stride=chunks), :] = part[
                 :, q * LANES : (q + 1) * LANES
             ]
-    terms = jnp.sum(gv[...].astype(F32) * bv[...], axis=0, keepdims=True)
+    terms = jnp.sum(gv[...].astype(F32) * bv[...].astype(F32), axis=0, keepdims=True)
     for c in range(chunks):
         flat[pl.ds(scale_base + c, 1), :] = terms[:, c * LANES : (c + 1) * LANES]
     tail = flat.shape[0] - scale_base - chunks
     flat[pl.ds(scale_base + chunks, tail), :] = jnp.zeros((tail, LANES), F32)
-    halves = breadth // 8
-    for m in range(micro):
-        pad_map(pad, xv.at[pl.ds(m * positions, positions)], reach, height, breadth)
-
-        @rolled(chunks)
-        def _(c):
-            columns = pl.ds(pl.multiple_of(c * LANES, LANES), LANES)
-            grads = [
-                gcv[pl.ds(m * positions + 16 * i, 16), columns].astype(F32)
-                for i in range(positions // 16)
-            ]
-            for b in range(side):
-                sums = [None] * side
-                for r in range(reach, height + reach):
-                    for w in range(halves):
-                        value = pad[c, r, pl.ds(MARGIN - reach + b + 8 * w, 8), :]
-                        for a in range(side):
-                            i = r - a
-                            if 0 <= i < height:
-                                p = i * breadth + 8 * w
-                                term = value * grads[p // 16][p % 16 : p % 16 + 8]
-                                sums[a] = term if sums[a] is None else sums[a] + term
-                for a in range(side):
-                    total = jnp.sum(sums[a], axis=0, keepdims=True)
-                    at = pl.ds((a * side + b) * chunks + c, 1)
-                    if m == 0:
-                        flat[at, :] = total
-                    else:
-                        flat[at, :] += total
-
     half = (share - cut) // 2
     spans = ((0, cut), (cut, half), (cut + half, half))
 
@@ -530,7 +555,7 @@
     wide = sds((micro, positions, width), BF16)
     one = sds((positions, channels), BF16)
     spread = sds((micro, positions, LANES), F32)
-    full = sds((micro, positions, channels), F32)
+    full = sds((micro, positions, channels), BF16)
     pad_shape = (chunks, height + side - 1, breadth + 2 * MARGIN, LANES)
     dims = (side, height, breadth, width)
 
@@ -553,6 +578,7 @@
             pltpu.VMEM((positions, width), BF16),
             pltpu.VMEM((positions, channels), F32),
             pltpu.VMEM((positions, channels), BF16),
+            pltpu.VMEM((positions, channels), BF16),
             pltpu.SemaphoreType.DMA((11,)),
         ],
         compiler_params=PARAMS,
@@ -580,6 +606,7 @@
             pltpu.VMEM((positions, channels), BF16),
             pltpu.VMEM((positions, channels), BF16),
             pltpu.SemaphoreType.DMA((10,)),
+            pltpu.SemaphoreType.DMA((6,)),
         ],
         compiler_params=PARAMS,
         name="block_backward",
@@ -639,7 +666,7 @@
             pltpu.VMEM((micro * positions, channels), BF16),
             pltpu.VMEM((micro * positions, channels), BF16),
             pltpu.VMEM((micro * positions, width), BF16),
-            pltpu.VMEM((micro * positions, channels), F32),
+            pltpu.VMEM((micro * positions, channels), BF16),
             pltpu.VMEM((micro * positions, channels), BF16),
             pltpu.VMEM((micro * positions, width), BF16),
             pltpu.VMEM((micro * positions, channels), BF16),
@@ -670,7 +697,7 @@
         in_specs=[pl.BlockSpec((share, LANES), lambda i: (0, 0)), part, part, part],
         out_specs=[part, part, part],
         scratch_shapes=[pltpu.VMEM((share, LANES), F32)],
-        compiler_params=PARAMS,
+        compiler_params=pltpu.CompilerParams(vmem_limit_bytes=16 * 1024 * 1024),
         name="adam",
     )(
         summed,

time: 507 us -> 486 us (0.959)
  waiting for transfers between devices: 295 us -> 285 us
  Pallas kernels: 92.8 us -> 83.1 us
    ppermute x8, waiting for transfers between devices: 192 us -> 182 us  [backward_loop(): return (lax.ppermute(g, 'section', back_route), grads)]
where the time goes in v3:
time: 486 us; the launch traced here: 485 us
  waiting for transfers between devices  285 us (59%)
  starting transfers between devices  107 us (22%)
  Pallas kernels  83.1 us (17%)
    ppermute x8, waiting for transfers between devices, backward_loop(): return (lax.ppermute(g, 'section', back_route), grads)  182 us
    ppermute x8, starting transfers between devices, forward_loop(): return (lax.ppermute(y, 'section', route), stash)  67.1 us
    ppermute x21, waiting for transfers between devices, hop(): return lax.ppermute(value, 'dp', route)  58.9 us
    ppermute x8, waiting for transfers between devices, forward_loop(): return (lax.ppermute(y, 'section', route), stash)  44.3 us
    pallas_call x9, Pallas kernels, forward_tick(): forward_call(tick.reshape(1), place, roster, received, images, taps, laye...  29.7 us
    ppermute x21, starting transfers between devices, hop(): return lax.ppermute(value, 'dp', route)  29.6 us
    pallas_call x9, Pallas kernels, backward_tick(): backward_call(tick.reshape(1), place, returned, cotangent, taps, layer_sc...  24 us
    pallas_call x1, Pallas kernels, body(): pl.pallas_call(functools.partial(weight_kernel, (*dims, real_rows, replic...  22.4 us
  transfers between devices with their start and end apart: 37, of which 25 were waited for; matrix products, arithmetic and copies ran while one was open for 1% of the time, Pallas kernels for 0%

profile of v3, /device:TPU:0, one launch (start us, length us, event | category | flops | bytes accessed | tf_op | source)
XLA Modules:
  0.0 485.0 jit_solution(7907873426195803024)
XLA Ops:
  0.8 1.7 reshape.122
  2.5 1.6 copy.44
  4.2 139.8 %while.46 = (s32[]{:T(128)}, bf16[256,768]{1,0:T(8,128)(2,1)}, bf16[2,256,768]{2,1,0:T(8,128)(2,1)}, bf16[2,256,768]{2,1,0:T(8,128)(2,1)}, bf16[2,256,768]{2,1,0...) while((s32[]{:T(128)}, bf16[256,768]{1,0:T(8,128)(2,1)}, ...), condition=%wide.region_1.2_spmd, body=%wide.region_0.1_spmd.sunk | while | flops 2 | bytes 1573061 | solution.py:634
  4.2 11.1 %block_forward.7 = (bf16[2,256,768]{2,1,0:T(8,128)(2,1)}, bf16[2,256,768]{2,1,0:T(8,128)(2,1)}, bf16[2,256,768]{2,1,0:T(8,128)(2,1)}, f32[2,256,128]{2,1,0:T(8,1...) custom-call(s32[1]{0:T(128)} %bitcast.96.tick, ...), custom_call_target="tpu_custom_call", output_to_operand_aliasing={{0}: (9, {}), {1}: (10, {}), {2}: (11, {}), {3}: (12, {}), ... | custom-call | tf_op jit(solution)/shard_map/while/body/eval_jaxpr/block_forward/pallas_call | solution.py:624
  15.3 2.0 collective-permute-start
  17.3 7.5 %collective-permute-done = bf16[256,768]{1,0:T(8,128)(2,1)} collective-permute-done((bf16[256,768]{1,0:T(8,128)(2,1)}, bf16[256,768]{1,0:T(8,128)(2,1)}, u32[]{:S(2)}, u32[]{:S(2)}) %collective-permute-start) | collective-permute-done | bytes 393248 | tf_op jit(solution)/shard_map/while/body/eval_jaxpr/ppermute | solution.py:632
  24.8 11.1 %block_forward.7 = (bf16[2,256,768]{2,1,0:T(8,128)(2,1)}, bf16[2,256,768]{2,1,0:T(8,128)(2,1)}, bf16[2,256,768]{2,1,0:T(8,128)(2,1)}, f32[2,256,128]{2,1,0:T(8,1...) custom-call(s32[1]{0:T(128)} %bitcast.96.tick, ...), custom_call_target="tpu_custom_call", output_to_operand_aliasing={{0}: (9, {}), {1}: (10, {}), {2}: (11, {}), {3}: (12, {}), ... | custom-call | tf_op jit(solution)/shard_map/while/body/eval_jaxpr/block_forward/pallas_call | solution.py:624
  35.9 5.1 %collective-permute-start = (bf16[256,768]{1,0:T(8,128)(2,1)}, bf16[256,768]{1,0:T(8,128)(2,1)}, u32[]{:S(2)}, u32[]{:S(2)}) collective-permute-start(bf16[256,768]{1,0:T(8,128)(2,1)} %get-tuple-element.812), channel_id=1, source_target_pairs={{0,16},{16,32},{32,48},{48,64},{64,80},{80,96},{96,112},{1,17},{17... | collective-permute-start | bytes 1179656 | tf_op jit(solution)/shard_map/while/body/eval_jaxpr/ppermute | solution.py:632
  41.0 6.6 %collective-permute-done = bf16[256,768]{1,0:T(8,128)(2,1)} collective-permute-done((bf16[256,768]{1,0:T(8,128)(2,1)}, bf16[256,768]{1,0:T(8,128)(2,1)}, u32[]{:S(2)}, u32[]{:S(2)}) %collective-permute-start) | collective-permute-done | bytes 393248 | tf_op jit(solution)/shard_map/while/body/eval_jaxpr/ppermute | solution.py:632
  48.7 15.2 %collective-permute-start = (bf16[256,768]{1,0:T(8,128)(2,1)}, bf16[256,768]{1,0:T(8,128)(2,1)}, u32[]{:S(2)}, u32[]{:S(2)}) collective-permute-start(bf16[256,768]{1,0:T(8,128)(2,1)} %get-tuple-element.812), channel_id=1, source_target_pairs={{0,16},{16,32},{32,48},{48,64},{64,80},{80,96},{96,112},{1,17},{17... | collective-permute-start | bytes 1179656 | tf_op jit(solution)/shard_map/while/body/eval_jaxpr/ppermute | solution.py:632
  63.9 5.8 %collective-permute-done = bf16[256,768]{1,0:T(8,128)(2,1)} collective-permute-done((bf16[256,768]{1,0:T(8,128)(2,1)}, bf16[256,768]{1,0:T(8,128)(2,1)}, u32[]{:S(2)}, u32[]{:S(2)}) %collective-permute-start) | collective-permute-done | bytes 393248 | tf_op jit(solution)/shard_map/while/body/eval_jaxpr/ppermute | solution.py:632
  70.8 5.1 %collective-permute-start = (bf16[256,768]{1,0:T(8,128)(2,1)}, bf16[256,768]{1,0:T(8,128)(2,1)}, u32[]{:S(2)}, u32[]{:S(2)}) collective-permute-start(bf16[256,768]{1,0:T(8,128)(2,1)} %get-tuple-element.812), channel_id=1, source_target_pairs={{0,16},{16,32},{32,48},{48,64},{64,80},{80,96},{96,112},{1,17},{17... | collective-permute-start | bytes 1179656 | tf_op jit(solution)/shard_map/while/body/eval_jaxpr/ppermute | solution.py:632
  75.9 4.9 %collective-permute-done = bf16[256,768]{1,0:T(8,128)(2,1)} collective-permute-done((bf16[256,768]{1,0:T(8,128)(2,1)}, bf16[256,768]{1,0:T(8,128)(2,1)}, u32[]{:S(2)}, u32[]{:S(2)}) %collective-permute-start) | collective-permute-done | bytes 393248 | tf_op jit(solution)/shard_map/while/body/eval_jaxpr/ppermute | solution.py:632
  81.9 15.4 %collective-permute-start = (bf16[256,768]{1,0:T(8,128)(2,1)}, bf16[256,768]{1,0:T(8,128)(2,1)}, u32[]{:S(2)}, u32[]{:S(2)}) collective-permute-start(bf16[256,768]{1,0:T(8,128)(2,1)} %get-tuple-element.812), channel_id=1, source_target_pairs={{0,16},{16,32},{32,48},{48,64},{64,80},{80,96},{96,112},{1,17},{17... | collective-permute-start | bytes 1179656 | tf_op jit(solution)/shard_map/while/body/eval_jaxpr/ppermute | solution.py:632
  97.3 4.8 %collective-permute-done = bf16[256,768]{1,0:T(8,128)(2,1)} collective-permute-done((bf16[256,768]{1,0:T(8,128)(2,1)}, bf16[256,768]{1,0:T(8,128)(2,1)}, u32[]{:S(2)}, u32[]{:S(2)}) %collective-permute-start) | collective-permute-done | bytes 393248 | tf_op jit(solution)/shard_map/while/body/eval_jaxpr/ppermute | solution.py:632
  103.1 6.0 %collective-permute-start = (bf16[256,768]{1,0:T(8,128)(2,1)}, bf16[256,768]{1,0:T(8,128)(2,1)}, u32[]{:S(2)}, u32[]{:S(2)}) collective-permute-start(bf16[256,768]{1,0:T(8,128)(2,1)} %get-tuple-element.812), channel_id=1, source_target_pairs={{0,16},{16,32},{32,48},{48,64},{64,80},{80,96},{96,112},{1,17},{17... | collective-permute-start | bytes 1179656 | tf_op jit(solution)/shard_map/while/body/eval_jaxpr/ppermute | solution.py:632
  109.2 4.8 %collective-permute-done = bf16[256,768]{1,0:T(8,128)(2,1)} collective-permute-done((bf16[256,768]{1,0:T(8,128)(2,1)}, bf16[256,768]{1,0:T(8,128)(2,1)}, u32[]{:S(2)}, u32[]{:S(2)}) %collective-permute-start) | collective-permute-done | bytes 393248 | tf_op jit(solution)/shard_map/while/body/eval_jaxpr/ppermute | solution.py:632
  115.1 12.1 %collective-permute-start = (bf16[256,768]{1,0:T(8,128)(2,1)}, bf16[256,768]{1,0:T(8,128)(2,1)}, u32[]{:S(2)}, u32[]{:S(2)}) collective-permute-start(bf16[256,768]{1,0:T(8,128)(2,1)} %get-tuple-element.812), channel_id=1, source_target_pairs={{0,16},{16,32},{32,48},{48,64},{64,80},{80,96},{96,112},{1,17},{17... | collective-permute-start | bytes 1179656 | tf_op jit(solution)/shard_map/while/body/eval_jaxpr/ppermute | solution.py:632
  127.2 4.8 %collective-permute-done = bf16[256,768]{1,0:T(8,128)(2,1)} collective-permute-done((bf16[256,768]{1,0:T(8,128)(2,1)}, bf16[256,768]{1,0:T(8,128)(2,1)}, u32[]{:S(2)}, u32[]{:S(2)}) %collective-permute-start) | collective-permute-done | bytes 393248 | tf_op jit(solution)/shard_map/while/body/eval_jaxpr/ppermute | solution.py:632
  133.1 6.0 %collective-permute-start = (bf16[256,768]{1,0:T(8,128)(2,1)}, bf16[256,768]{1,0:T(8,128)(2,1)}, u32[]{:S(2)}, u32[]{:S(2)}) collective-permute-start(bf16[256,768]{1,0:T(8,128)(2,1)} %get-tuple-element.812), channel_id=1, source_target_pairs={{0,16},{16,32},{32,48},{48,64},{64,80},{80,96},{96,112},{1,17},{17... | collective-permute-start | bytes 1179656 | tf_op jit(solution)/shard_map/while/body/eval_jaxpr/ppermute | solution.py:632
  139.1 4.8 %collective-permute-done = bf16[256,768]{1,0:T(8,128)(2,1)} collective-permute-done((bf16[256,768]{1,0:T(8,128)(2,1)}, bf16[256,768]{1,0:T(8,128)(2,1)}, u32[]{:S(2)}, u32[]{:S(2)}) %collective-permute-start) | collective-permute-done | bytes 393248 | tf_op jit(solution)/shard_map/while/body/eval_jaxpr/ppermute | solution.py:632
  144.0 1.2 block_forward.6
  145.2 208.5 %while.47 = (s32[]{:T(128)}, bf16[256,768]{1,0:T(8,128)(2,1)}, bf16[2,256,768]{2,1,0:T(8,128)(2,1)}, bf16[2,256,3072]{2,1,0:T(8,128)(2,1)}, bf16[2,256,768]{2,1,...) while((s32[]{:T(128)}, bf16[256,768]{1,0:T(8,128)(2,1)}, ...), condition=%wide.region_3.4_spmd, body=%wide.region_2.3_spmd.sunk | while | flops 2 | bytes 1573045 | solution.py:649
  145.3 1.1 block_backward.7
  146.4 1.3 collective-permute-start.1
  147.7 17.6 %collective-permute-done.1 = bf16[256,768]{1,0:T(8,128)(2,1)} collective-permute-done((bf16[256,768]{1,0:T(8,128)(2,1)}, bf16[256,768]{1,0:T(8,128)(2,1)}, u32[]{:S(2)}, u32[]{:S(2)}) %collective-permute-start.1) | collective-permute-done | bytes 393248 | tf_op jit(solution)/shard_map/while/body/eval_jaxpr/ppermute | solution.py:647
  165.2 1.1 block_backward.7
  166.3 1.3 collective-permute-start.1
  167.6 9.8 %collective-permute-done.1 = bf16[256,768]{1,0:T(8,128)(2,1)} collective-permute-done((bf16[256,768]{1,0:T(8,128)(2,1)}, bf16[256,768]{1,0:T(8,128)(2,1)}, u32[]{:S(2)}, u32[]{:S(2)}) %collective-permute-start.1) | collective-permute-done | bytes 393248 | tf_op jit(solution)/shard_map/while/body/eval_jaxpr/ppermute | solution.py:647
  178.5 1.3 collective-permute-start.1
  179.8 20.0 %collective-permute-done.1 = bf16[256,768]{1,0:T(8,128)(2,1)} collective-permute-done((bf16[256,768]{1,0:T(8,128)(2,1)}, bf16[256,768]{1,0:T(8,128)(2,1)}, u32[]{:S(2)}, u32[]{:S(2)}) %collective-permute-start.1) | collective-permute-done | bytes 393248 | tf_op jit(solution)/shard_map/while/body/eval_jaxpr/ppermute | solution.py:647
  200.9 1.3 collective-permute-start.1
  202.2 8.7 %collective-permute-done.1 = bf16[256,768]{1,0:T(8,128)(2,1)} collective-permute-done((bf16[256,768]{1,0:T(8,128)(2,1)}, bf16[256,768]{1,0:T(8,128)(2,1)}, u32[]{:S(2)}, u32[]{:S(2)}) %collective-permute-start.1) | collective-permute-done | bytes 393248 | tf_op jit(solution)/shard_map/while/body/eval_jaxpr/ppermute | solution.py:647
  212.0 1.3 collective-permute-start.1
  213.3 24.2 %collective-permute-done.1 = bf16[256,768]{1,0:T(8,128)(2,1)} collective-permute-done((bf16[256,768]{1,0:T(8,128)(2,1)}, bf16[256,768]{1,0:T(8,128)(2,1)}, u32[]{:S(2)}, u32[]{:S(2)}) %collective-permute-start.1) | collective-permute-done | bytes 393248 | tf_op jit(solution)/shard_map/while/body/eval_jaxpr/ppermute | solution.py:647
  238.6 1.3 collective-permute-start.1
  239.9 8.7 %collective-permute-done.1 = bf16[256,768]{1,0:T(8,128)(2,1)} collective-permute-done((bf16[256,768]{1,0:T(8,128)(2,1)}, bf16[256,768]{1,0:T(8,128)(2,1)}, u32[]{:S(2)}, u32[]{:S(2)}) %collective-permute-start.1) | collective-permute-done | bytes 393248 | tf_op jit(solution)/shard_map/while/body/eval_jaxpr/ppermute | solution.py:647
  249.7 1.3 collective-permute-start.1
  251.0 80.3 %collective-permute-done.1 = bf16[256,768]{1,0:T(8,128)(2,1)} collective-permute-done((bf16[256,768]{1,0:T(8,128)(2,1)}, bf16[256,768]{1,0:T(8,128)(2,1)}, u32[]{:S(2)}, u32[]{:S(2)}) %collective-permute-start.1) | collective-permute-done | bytes 393248 | tf_op jit(solution)/shard_map/while/body/eval_jaxpr/ppermute | solution.py:647
  331.2 8.2 %block_backward.7 = (bf16[2,256,768]{2,1,0:T(8,128)(2,1)}, bf16[2,256,3072]{2,1,0:T(8,128)(2,1)}, bf16[2,256,768]{2,1,0:T(8,128)(2,1)}, bf16[256,768]{1,0:T(8,128)(2,1)}) custom-call(s32[1]{0:T(128)} %bitcast.97.tick, s32[2]{0:T(128)S(1)} %get-tuple-element.924.place, ...), custom_call_target="tpu_custom_call", output_to_operand_aliasing={{0}: (11, {}), {1}: (12, {}), {2}: (13, {})} | custom-call | tf_op jit(solution)/shard_map/while/body/eval_jaxpr/block_backward/pallas_call | solution.py:639
  339.4 1.3 collective-permute-start.1
  340.7 13.0 %collective-permute-done.1 = bf16[256,768]{1,0:T(8,128)(2,1)} collective-permute-done((bf16[256,768]{1,0:T(8,128)(2,1)}, bf16[256,768]{1,0:T(8,128)(2,1)}, u32[]{:S(2)}, u32[]{:S(2)}) %collective-permute-start.1) | collective-permute-done | bytes 393248 | tf_op jit(solution)/shard_map/while/body/eval_jaxpr/ppermute | solution.py:647
  353.8 8.2 %block_backward.6 = (bf16[2,256,768]{2,1,0:T(8,128)(2,1)}, bf16[2,256,3072]{2,1,0:T(8,128)(2,1)}, bf16[2,256,768]{2,1,0:T(8,128)(2,1)}, bf16[256,768]{1,0:T(8,128)(2,1)}) custom-call(s32[1]{0:T(128)} %constant.180.clone.1.tick, s32[2]{0:T(128)S(1)} %get-tuple-element.984, ...), custom_call_target="tpu_custom_call", output_to_operand_aliasing={{0}: (11, {}), {1}: (12, {}), {2}: (13, {})} | custom-call | tf_op jit(solution)/shard_map/block_backward/pallas_call | solution.py:639
  362.7 22.4 %weight_grads.1 = (bf16[2,1984,128]{2,1,0:T(8,128)(2,1)}, bf16[2,1984,128]{2,1,0:T(8,128)(2,1)}, bf16[2,1984,128]{2,1,0:T(8,128)(2,1)}, bf16[2,1984,128]{2,1,0:T...) custom-call(s32[49]{0:T(128)} %bitcast.107, ...), custom_call_target="tpu_custom_call" | custom-call | tf_op jit(solution)/shard_map/weight_grads/pallas_call | solution.py:658
  386.2 1.8 collective-permute-done.5
  388.0 1.5 fusion.7
  389.5 5.7 %collective-permute-start.6 = (bf16[1984,128]{1,0:T(8,128)(2,1)S(1)}, bf16[1984,128]{1,0:T(8,128)(2,1)S(1)}, u32[]{:S(2)}, u32[]{:S(2)}) collective-permute-start(bf16[1984,128]{1,0:T(8,128)(2,1)S(1)} %get-tuple-element.630), channel_id=1, source_target_pairs={{0,2},{1,3},{2,4},{3,5},{4,6},{5,7},{6,0},{7,1},{8,10},{9,11},{10,... | collective-permute-start | bytes 1523720 | tf_op jit(solution)/shard_map/ppermute | solution.py:473
  395.1 1.3 collective-permute-start.9
  396.9 4.3 collective-permute-start.15
  401.2 7.0 %collective-permute-done.6 = bf16[1984,128]{1,0:T(8,128)(2,1)S(1)} collective-permute-done((bf16[1984,128]{1,0:T(8,128)(2,1)S(1)}, bf16[1984,128]{1,0:T(8,128)(2,1)S(1)}, u32[]{:S(2)}, u32[]{:S(2)}) %collective-permute-start.6) | collective-permute-done | bytes 507936 | tf_op jit(solution)/shard_map/ppermute | solution.py:473
  408.3 4.0 collective-permute-start.19
  412.7 1.6 collective-permute-start.10
  414.8 4.5 collective-permute-done.15
  419.3 16.3 %collective-permute-done.19 = bf16[4,752,128]{2,1,0:T(8,128)(2,1)S(1)} collective-permute-done((bf16[4,752,128]{2,1,0:T(8,128)(2,1)S(1)}, bf16[4,752,128]{2,1,0:T(8,128)(2,1)S(1)}, u32[]{:S(2)}, u32[]{:S(2)}) %collective-permute-start.19) | collective-permute-done | bytes 770080 | tf_op jit(solution)/shard_map/ppermute | solution.py:473
  436.6 3.0 collective-permute-start.11
  439.6 4.1 collective-permute-done.16
  444.5 2.7 collective-permute-start.20
  447.2 5.6 %collective-permute-done.17 = bf16[752,128]{1,0:T(8,128)(2,1)S(1)} collective-permute-done((bf16[752,128]{1,0:T(8,128)(2,1)S(1)}, bf16[752,128]{1,0:T(8,128)(2,1)S(1)}, u32[]{:S(2)}, u32[]{:S(2)}) %collective-permute-start.17) | collective-permute-done | bytes 192544 | tf_op jit(solution)/shard_map/ppermute | solution.py:473
  453.2 3.0 collective-permute-start.12
  456.2 9.6 %collective-permute-done.18 = bf16[752,128]{1,0:T(8,128)(2,1)S(1)} collective-permute-done((bf16[752,128]{1,0:T(8,128)(2,1)S(1)}, bf16[752,128]{1,0:T(8,128)(2,1)S(1)}, u32[]{:S(2)}, u32[]{:S(2)}) %collective-permute-start.18) | collective-permute-done | bytes 192544 | tf_op jit(solution)/shard_map/ppermute | solution.py:473
  466.2 5.8 %collective-permute-done.21 = bf16[752,128]{1,0:T(8,128)(2,1)S(1)} collective-permute-done((bf16[752,128]{1,0:T(8,128)(2,1)S(1)}, bf16[752,128]{1,0:T(8,128)(2,1)S(1)}, u32[]{:S(2)}, u32[]{:S(2)}) %collective-permute-start.21) | collective-permute-done | bytes 192544 | tf_op jit(solution)/shard_map/ppermute | solution.py:473
  472.1 1.1 collective-permute-start.22
  473.5 4.3 collective-permute-done.22
  478.0 7.0 %adam.1 = (f32[871,4,128]{2,1,0:T(4,128)}, f32[871,4,128]{2,1,0:T(4,128)}, f32[871,4,128]{2,1,0:T(4,128)}) custom-call(bf16[3488,128]{1,0:T(8,128)(2,1)S(1)} %pad_maximum_fusion.g_i, f32[871,4,128]{2,1,0:T(4,128)S(1)} %bitcast.98, f32[871,4,128]{2,1,0:T(4,128)S(1)} %bitcast.99, f32[871,4,128]{2,1,0:T(4,128)S(1)} %bitcast.100), custom_call_target="tpu_custom_call" | custom-call | tf_op jit(solution)/shard_map/adam/pallas_call | solution.py:693
  (72 shorter events, 17.8 us)
Async XLA Ops:
  15.3 9.5 %collective-permute-start = (bf16[256,768]{1,0:T(8,128)(2,1)}, bf16[256,768]{1,0:T(8,128)(2,1)}, u32[]{:S(2)}, u32[]{:S(2)}) collective-permute-start(bf16[256,768]{1,0:T(8,128)(2,1)} %get-tuple-element.812), channel_id=1, source_target_pairs={{0,16},{16,32},{32,48},{48,64},{64,80},{80,96},{96,112},{1,17},{17... | collective-permute-start | bytes 1179656 | tf_op jit(solution)/shard_map/while/body/eval_jaxpr/ppermute | solution.py:632
  35.9 11.8 %collective-permute-start = (bf16[256,768]{1,0:T(8,128)(2,1)}, bf16[256,768]{1,0:T(8,128)(2,1)}, u32[]{:S(2)}, u32[]{:S(2)}) collective-permute-start(bf16[256,768]{1,0:T(8,128)(2,1)} %get-tuple-element.812), channel_id=1, source_target_pairs={{0,16},{16,32},{32,48},{48,64},{64,80},{80,96},{96,112},{1,17},{17... | collective-permute-start | bytes 1179656 | tf_op jit(solution)/shard_map/while/body/eval_jaxpr/ppermute | solution.py:632
  48.7 21.0 %collective-permute-start = (bf16[256,768]{1,0:T(8,128)(2,1)}, bf16[256,768]{1,0:T(8,128)(2,1)}, u32[]{:S(2)}, u32[]{:S(2)}) collective-permute-start(bf16[256,768]{1,0:T(8,128)(2,1)} %get-tuple-element.812), channel_id=1, source_target_pairs={{0,16},{16,32},{32,48},{48,64},{64,80},{80,96},{96,112},{1,17},{17... | collective-permute-start | bytes 1179656 | tf_op jit(solution)/shard_map/while/body/eval_jaxpr/ppermute | solution.py:632
  70.8 10.1 %collective-permute-start = (bf16[256,768]{1,0:T(8,128)(2,1)}, bf16[256,768]{1,0:T(8,128)(2,1)}, u32[]{:S(2)}, u32[]{:S(2)}) collective-permute-start(bf16[256,768]{1,0:T(8,128)(2,1)} %get-tuple-element.812), channel_id=1, source_target_pairs={{0,16},{16,32},{32,48},{48,64},{64,80},{80,96},{96,112},{1,17},{17... | collective-permute-start | bytes 1179656 | tf_op jit(solution)/shard_map/while/body/eval_jaxpr/ppermute | solution.py:632
  81.9 20.2 %collective-permute-start = (bf16[256,768]{1,0:T(8,128)(2,1)}, bf16[256,768]{1,0:T(8,128)(2,1)}, u32[]{:S(2)}, u32[]{:S(2)}) collective-permute-start(bf16[256,768]{1,0:T(8,128)(2,1)} %get-tuple-element.812), channel_id=1, source_target_pairs={{0,16},{16,32},{32,48},{48,64},{64,80},{80,96},{96,112},{1,17},{17... | collective-permute-start | bytes 1179656 | tf_op jit(solution)/shard_map/while/body/eval_jaxpr/ppermute | solution.py:632
  103.1 10.9 %collective-permute-start = (bf16[256,768]{1,0:T(8,128)(2,1)}, bf16[256,768]{1,0:T(8,128)(2,1)}, u32[]{:S(2)}, u32[]{:S(2)}) collective-permute-start(bf16[256,768]{1,0:T(8,128)(2,1)} %get-tuple-element.812), channel_id=1, source_target_pairs={{0,16},{16,32},{32,48},{48,64},{64,80},{80,96},{96,112},{1,17},{17... | collective-permute-start | bytes 1179656 | tf_op jit(solution)/shard_map/while/body/eval_jaxpr/ppermute | solution.py:632
  115.1 17.0 %collective-permute-start = (bf16[256,768]{1,0:T(8,128)(2,1)}, bf16[256,768]{1,0:T(8,128)(2,1)}, u32[]{:S(2)}, u32[]{:S(2)}) collective-permute-start(bf16[256,768]{1,0:T(8,128)(2,1)} %get-tuple-element.812), channel_id=1, source_target_pairs={{0,16},{16,32},{32,48},{48,64},{64,80},{80,96},{96,112},{1,17},{17... | collective-permute-start | bytes 1179656 | tf_op jit(solution)/shard_map/while/body/eval_jaxpr/ppermute | solution.py:632
  133.1 10.9 %collective-permute-start = (bf16[256,768]{1,0:T(8,128)(2,1)}, bf16[256,768]{1,0:T(8,128)(2,1)}, u32[]{:S(2)}, u32[]{:S(2)}) collective-permute-start(bf16[256,768]{1,0:T(8,128)(2,1)} %get-tuple-element.812), channel_id=1, source_target_pairs={{0,16},{16,32},{32,48},{48,64},{64,80},{80,96},{96,112},{1,17},{17... | collective-permute-start | bytes 1179656 | tf_op jit(solution)/shard_map/while/body/eval_jaxpr/ppermute | solution.py:632
  144.0 1.2 copy-start.8
  146.4 18.9 %collective-permute-start.1 = (bf16[256,768]{1,0:T(8,128)(2,1)}, bf16[256,768]{1,0:T(8,128)(2,1)}, u32[]{:S(2)}, u32[]{:S(2)}) collective-permute-start(bf16[256,768]{1,0:T(8,128)(2,1)} %get-tuple-element.834), channel_id=1, source_target_pairs={{16,0},{32,16},{48,32},{64,48},{80,64},{96,80},{112,96},{17,1},{33... | collective-permute-start | bytes 1179656 | tf_op jit(solution)/shard_map/while/body/eval_jaxpr/ppermute | solution.py:647
  166.3 11.1 %collective-permute-start.1 = (bf16[256,768]{1,0:T(8,128)(2,1)}, bf16[256,768]{1,0:T(8,128)(2,1)}, u32[]{:S(2)}, u32[]{:S(2)}) collective-permute-start(bf16[256,768]{1,0:T(8,128)(2,1)} %get-tuple-element.834), channel_id=1, source_target_pairs={{16,0},{32,16},{48,32},{64,48},{80,64},{96,80},{112,96},{17,1},{33... | collective-permute-start | bytes 1179656 | tf_op jit(solution)/shard_map/while/body/eval_jaxpr/ppermute | solution.py:647
  178.5 21.3 %collective-permute-start.1 = (bf16[256,768]{1,0:T(8,128)(2,1)}, bf16[256,768]{1,0:T(8,128)(2,1)}, u32[]{:S(2)}, u32[]{:S(2)}) collective-permute-start(bf16[256,768]{1,0:T(8,128)(2,1)} %get-tuple-element.834), channel_id=1, source_target_pairs={{16,0},{32,16},{48,32},{64,48},{80,64},{96,80},{112,96},{17,1},{33... | collective-permute-start | bytes 1179656 | tf_op jit(solution)/shard_map/while/body/eval_jaxpr/ppermute | solution.py:647
  200.9 10.0 %collective-permute-start.1 = (bf16[256,768]{1,0:T(8,128)(2,1)}, bf16[256,768]{1,0:T(8,128)(2,1)}, u32[]{:S(2)}, u32[]{:S(2)}) collective-permute-start(bf16[256,768]{1,0:T(8,128)(2,1)} %get-tuple-element.834), channel_id=1, source_target_pairs={{16,0},{32,16},{48,32},{64,48},{80,64},{96,80},{112,96},{17,1},{33... | collective-permute-start | bytes 1179656 | tf_op jit(solution)/shard_map/while/body/eval_jaxpr/ppermute | solution.py:647
  212.0 25.5 %collective-permute-start.1 = (bf16[256,768]{1,0:T(8,128)(2,1)}, bf16[256,768]{1,0:T(8,128)(2,1)}, u32[]{:S(2)}, u32[]{:S(2)}) collective-permute-start(bf16[256,768]{1,0:T(8,128)(2,1)} %get-tuple-element.834), channel_id=1, source_target_pairs={{16,0},{32,16},{48,32},{64,48},{80,64},{96,80},{112,96},{17,1},{33... | collective-permute-start | bytes 1179656 | tf_op jit(solution)/shard_map/while/body/eval_jaxpr/ppermute | solution.py:647
  238.6 10.0 %collective-permute-start.1 = (bf16[256,768]{1,0:T(8,128)(2,1)}, bf16[256,768]{1,0:T(8,128)(2,1)}, u32[]{:S(2)}, u32[]{:S(2)}) collective-permute-start(bf16[256,768]{1,0:T(8,128)(2,1)} %get-tuple-element.834), channel_id=1, source_target_pairs={{16,0},{32,16},{48,32},{64,48},{80,64},{96,80},{112,96},{17,1},{33... | collective-permute-start | bytes 1179656 | tf_op jit(solution)/shard_map/while/body/eval_jaxpr/ppermute | solution.py:647
  249.7 81.6 %collective-permute-start.1 = (bf16[256,768]{1,0:T(8,128)(2,1)}, bf16[256,768]{1,0:T(8,128)(2,1)}, u32[]{:S(2)}, u32[]{:S(2)}) collective-permute-start(bf16[256,768]{1,0:T(8,128)(2,1)} %get-tuple-element.834), channel_id=1, source_target_pairs={{16,0},{32,16},{48,32},{64,48},{80,64},{96,80},{112,96},{17,1},{33... | collective-permute-start | bytes 1179656 | tf_op jit(solution)/shard_map/while/body/eval_jaxpr/ppermute | solution.py:647
  339.4 14.3 %collective-permute-start.1 = (bf16[256,768]{1,0:T(8,128)(2,1)}, bf16[256,768]{1,0:T(8,128)(2,1)}, u32[]{:S(2)}, u32[]{:S(2)}) collective-permute-start(bf16[256,768]{1,0:T(8,128)(2,1)} %get-tuple-element.834), channel_id=1, source_target_pairs={{16,0},{32,16},{48,32},{64,48},{80,64},{96,80},{112,96},{17,1},{33... | collective-permute-start | bytes 1179656 | tf_op jit(solution)/shard_map/while/body/eval_jaxpr/ppermute | solution.py:647
  385.1 11.4 %copy-start.10 = (bf16[2,1984,128]{2,1,0:T(8,128)(2,1)S(1)}, bf16[2,1984,128]{2,1,0:T(8,128)(2,1)}, u32[]{:S(2)}) copy-start(bf16[2,1984,128]{2,1,0:T(8,128)(2,1)} %get-tuple-element.540) | copy-start | bytes 3047428
  385.1 11.4 %copy-start.3 = (bf16[8,752,128]{2,1,0:T(8,128)(2,1)S(1)}, bf16[8,752,128]{2,1,0:T(8,128)(2,1)}, u32[]{:S(2)}) copy-start(bf16[8,752,128]{2,1,0:T(8,128)(2,1)} %get-tuple-element.547) | copy-start | bytes 4620292
  385.1 2.9 collective-permute-start.5
  385.2 11.3 %collective-permute-start.14 = (bf16[8,752,128]{2,1,0:T(8,128)(2,1)}, bf16[8,752,128]{2,1,0:T(8,128)(2,1)S(1)}, u32[]{:S(2)}, u32[]{:S(2)}) collective-permute-start(bf16[8,752,128]{2,1,0:T(8,128)(2,1)} %get-tuple-element.548), channel_id=1, source_target_pairs={{0,1},{1,0},{2,3},{3,2},{4,5},{5,4},{6,7},{7,6},{8,9},{9,8},{10,11... | collective-permute-start | bytes 4620296 | tf_op jit(solution)/shard_map/ppermute | solution.py:473
  385.7 11.2 %collective-permute-start.4 = (bf16[2,1984,128]{2,1,0:T(8,128)(2,1)}, bf16[2,1984,128]{2,1,0:T(8,128)(2,1)S(1)}, u32[]{:S(2)}, u32[]{:S(2)}) collective-permute-start(bf16[2,1984,128]{2,1,0:T(8,128)(2,1)} %get-tuple-element.542), channel_id=1, source_target_pairs={{0,1},{1,0},{2,3},{3,2},{4,5},{5,4},{6,7},{7,6},{8,9},{9,8},{10,11... | collective-permute-start | bytes 3047432 | tf_op jit(solution)/shard_map/ppermute | solution.py:473
  385.8 28.6 %collective-permute-start.13 = (bf16[8,752,128]{2,1,0:T(8,128)(2,1)}, bf16[8,752,128]{2,1,0:T(8,128)(2,1)S(1)}, u32[]{:S(2)}, u32[]{:S(2)}) collective-permute-start(bf16[8,752,128]{2,1,0:T(8,128)(2,1)} %get-tuple-element.546), channel_id=1, source_target_pairs={{0,1},{1,0},{2,3},{3,2},{4,5},{5,4},{6,7},{7,6},{8,9},{9,8},{10,11... | collective-permute-start | bytes 4620296 | tf_op jit(solution)/shard_map/ppermute | solution.py:473
  389.5 18.8 %collective-permute-start.6 = (bf16[1984,128]{1,0:T(8,128)(2,1)S(1)}, bf16[1984,128]{1,0:T(8,128)(2,1)S(1)}, u32[]{:S(2)}, u32[]{:S(2)}) collective-permute-start(bf16[1984,128]{1,0:T(8,128)(2,1)S(1)} %get-tuple-element.630), channel_id=1, source_target_pairs={{0,2},{1,3},{2,4},{3,5},{4,6},{5,7},{6,0},{7,1},{8,10},{9,11},{10,... | collective-permute-start | bytes 1523720 | tf_op jit(solution)/shard_map/ppermute | solution.py:473
  395.1 17.2 %collective-permute-start.9 = (bf16[1984,128]{1,0:T(8,128)(2,1)S(1)}, bf16[1984,128]{1,0:T(8,128)(2,1)S(1)}, u32[]{:S(2)}, u32[]{:S(2)}) collective-permute-start(bf16[1984,128]{1,0:T(8,128)(2,1)S(1)} %get-tuple-element.631), channel_id=1, source_target_pairs={{0,6},{1,7},{2,0},{3,1},{4,2},{5,3},{6,4},{7,5},{8,14},{9,15},{10,... | collective-permute-start | bytes 1523720 | tf_op jit(solution)/shard_map/ppermute | solution.py:473
  396.5 39.7 %collective-permute-start.3 = (bf16[2,1984,128]{2,1,0:T(8,128)(2,1)S(1)}, bf16[2,1984,128]{2,1,0:T(8,128)(2,1)S(1)}, u32[]{:S(2)}, u32[]{:S(2)}) collective-permute-start(bf16[2,1984,128]{2,1,0:T(8,128)(2,1)S(1)} %copy-done.10), channel_id=1, source_target_pairs={{0,1},{1,0},{2,3},{3,2},{4,5},{5,4},{6,7},{7,6},{8,9},{9,8},{10,11... | collective-permute-start | bytes 3047432 | tf_op jit(solution)/shard_map/ppermute | solution.py:473
  396.5 15.8 %copy-start.7 = (bf16[2,1984,128]{2,1,0:T(8,128)(2,1)S(1)}, bf16[2,1984,128]{2,1,0:T(8,128)(2,1)}, u32[]{:S(2)}) copy-start(bf16[2,1984,128]{2,1,0:T(8,128)(2,1)} %get-tuple-element.541) | copy-start | bytes 3047428
  396.9 22.4 %collective-permute-start.15 = (bf16[4,752,128]{2,1,0:T(8,128)(2,1)S(1)}, bf16[4,752,128]{2,1,0:T(8,128)(2,1)S(1)}, u32[]{:S(2)}, u32[]{:S(2)}) collective-permute-start(bf16[4,752,128]{2,1,0:T(8,128)(2,1)S(1)} %get-tuple-element.624), channel_id=1, source_target_pairs={{0,8},{1,9},{2,10},{3,11},{4,12},{5,13},{6,14},{7,15},{8,0},{9,1},... | collective-permute-start | bytes 2310152 | tf_op jit(solution)/shard_map/ppermute | solution.py:473
  408.3 27.3 %collective-permute-start.19 = (bf16[4,752,128]{2,1,0:T(8,128)(2,1)S(1)}, bf16[4,752,128]{2,1,0:T(8,128)(2,1)S(1)}, u32[]{:S(2)}, u32[]{:S(2)}) collective-permute-start(bf16[4,752,128]{2,1,0:T(8,128)(2,1)S(1)} %get-tuple-element.625), channel_id=1, source_target_pairs={{0,8},{1,9},{2,10},{3,11},{4,12},{5,13},{6,14},{7,15},{8,0},{9,1},... | collective-permute-start | bytes 2310152 | tf_op jit(solution)/shard_map/ppermute | solution.py:473
  412.3 7.0 %copy-start.9 = (bf16[2,1984,128]{2,1,0:T(8,128)(2,1)S(1)}, bf16[2,1984,128]{2,1,0:T(8,128)(2,1)}, u32[]{:S(2)}) copy-start(bf16[2,1984,128]{2,1,0:T(8,128)(2,1)} %get-tuple-element.538) | copy-start | bytes 3047428
  412.3 23.3 %copy-start.4 = (bf16[8,752,128]{2,1,0:T(8,128)(2,1)S(1)}, bf16[8,752,128]{2,1,0:T(8,128)(2,1)}, u32[]{:S(2)}) copy-start(bf16[8,752,128]{2,1,0:T(8,128)(2,1)} %get-tuple-element.545) | copy-start | bytes 4620292
  412.7 23.4 %copy-start.6 = (bf16[2,1984,128]{2,1,0:T(8,128)(2,1)S(1)}, bf16[2,1984,128]{2,1,0:T(8,128)(2,1)}, u32[]{:S(2)}) copy-start(bf16[2,1984,128]{2,1,0:T(8,128)(2,1)} %get-tuple-element.539) | copy-start | bytes 3047428
  412.7 23.4 %collective-permute-start.10 = (bf16[1984,128]{1,0:T(8,128)(2,1)S(1)}, bf16[1984,128]{1,0:T(8,128)(2,1)S(1)}, u32[]{:S(2)}, u32[]{:S(2)}) collective-permute-start(bf16[1984,128]{1,0:T(8,128)(2,1)S(1)} %get-tuple-element.629), channel_id=1, source_target_pairs={{0,6},{1,7},{2,0},{3,1},{4,2},{5,3},{6,4},{7,5},{8,14},{9,15},{10,... | collective-permute-start | bytes 1523720 | tf_op jit(solution)/shard_map/ppermute | solution.py:473
  414.4 21.8 %collective-permute-start.7 = (bf16[1984,128]{1,0:T(8,128)(2,1)S(1)}, bf16[1984,128]{1,0:T(8,128)(2,1)S(1)}, u32[]{:S(2)}, u32[]{:S(2)}) collective-permute-start(bf16[1984,128]{1,0:T(8,128)(2,1)S(1)} %get-tuple-element.628), channel_id=1, source_target_pairs={{0,2},{1,3},{2,4},{3,5},{4,6},{5,7},{6,0},{7,1},{8,10},{9,11},{10,... | collective-permute-start | bytes 1523720 | tf_op jit(solution)/shard_map/ppermute | solution.py:473
  419.3 33.7 %collective-permute-start.2 = (bf16[2,1984,128]{2,1,0:T(8,128)(2,1)S(1)}, bf16[2,1984,128]{2,1,0:T(8,128)(2,1)S(1)}, u32[]{:S(2)}, u32[]{:S(2)}) collective-permute-start(bf16[2,1984,128]{2,1,0:T(8,128)(2,1)S(1)} %copy-done.9), channel_id=1, source_target_pairs={{0,1},{1,0},{2,3},{3,2},{4,5},{5,4},{6,7},{7,6},{8,9},{9,8},{10,11... | collective-permute-start | bytes 3047432 | tf_op jit(solution)/shard_map/ppermute | solution.py:473
  435.8 7.9 %collective-permute-start.16 = (bf16[752,128]{1,0:T(8,128)(2,1)S(1)}, bf16[752,128]{1,0:T(8,128)(2,1)S(1)}, u32[]{:S(2)}, u32[]{:S(2)}) collective-permute-start(bf16[752,128]{1,0:T(8,128)(2,1)S(1)} %get-tuple-element.622), channel_id=1, source_target_pairs={{0,2},{1,3},{2,4},{3,5},{4,6},{5,7},{6,0},{7,1},{8,10},{9,11},{10,... | collective-permute-start | bytes 577544 | tf_op jit(solution)/shard_map/ppermute | solution.py:473
  436.6 16.4 %copy-start.5 = (bf16[2,1984,128]{2,1,0:T(8,128)(2,1)S(1)}, bf16[2,1984,128]{2,1,0:T(8,128)(2,1)}, u32[]{:S(2)}) copy-start(bf16[2,1984,128]{2,1,0:T(8,128)(2,1)} %get-tuple-element.537) | copy-start | bytes 3047428
  436.6 16.4 %collective-permute-start.11 = (bf16[1984,128]{1,0:T(8,128)(2,1)S(1)}, bf16[1984,128]{1,0:T(8,128)(2,1)S(1)}, u32[]{:S(2)}, u32[]{:S(2)}) collective-permute-start(bf16[1984,128]{1,0:T(8,128)(2,1)S(1)} %get-tuple-element.627), channel_id=1, source_target_pairs={{0,6},{1,7},{2,0},{3,1},{4,2},{5,3},{6,4},{7,5},{8,14},{9,15},{10,... | collective-permute-start | bytes 1523720 | tf_op jit(solution)/shard_map/ppermute | solution.py:473
  443.8 9.0 %collective-permute-start.17 = (bf16[752,128]{1,0:T(8,128)(2,1)S(1)}, bf16[752,128]{1,0:T(8,128)(2,1)S(1)}, u32[]{:S(2)}, u32[]{:S(2)}) collective-permute-start(bf16[752,128]{1,0:T(8,128)(2,1)S(1)} %fusion.12), channel_id=1, source_target_pairs={{0,2},{1,3},{2,4},{3,5},{4,6},{5,7},{6,0},{7,1},{8,10},{9,11},{10,... | collective-permute-start | bytes 577544 | tf_op jit(solution)/shard_map/ppermute | solution.py:473
  443.9 29.3 %collective-permute-start.8 = (bf16[1984,128]{1,0:T(8,128)(2,1)S(1)}, bf16[1984,128]{1,0:T(8,128)(2,1)S(1)}, u32[]{:S(2)}, u32[]{:S(2)}) collective-permute-start(bf16[1984,128]{1,0:T(8,128)(2,1)S(1)} %get-tuple-element.626), channel_id=1, source_target_pairs={{0,2},{1,3},{2,4},{3,5},{4,6},{5,7},{6,0},{7,1},{8,10},{9,11},{10,... | collective-permute-start | bytes 1523720 | tf_op jit(solution)/shard_map/ppermute | solution.py:473
  444.5 11.8 %collective-permute-start.20 = (bf16[752,128]{1,0:T(8,128)(2,1)S(1)}, bf16[752,128]{1,0:T(8,128)(2,1)S(1)}, u32[]{:S(2)}, u32[]{:S(2)}) collective-permute-start(bf16[752,128]{1,0:T(8,128)(2,1)S(1)} %get-tuple-element.623), channel_id=1, source_target_pairs={{0,6},{1,7},{2,0},{3,1},{4,2},{5,3},{6,4},{7,5},{8,14},{9,15},{10,... | collective-permute-start | bytes 577544 | tf_op jit(solution)/shard_map/ppermute | solution.py:473
  452.9 13.0 %collective-permute-start.18 = (bf16[752,128]{1,0:T(8,128)(2,1)S(1)}, bf16[752,128]{1,0:T(8,128)(2,1)S(1)}, u32[]{:S(2)}, u32[]{:S(2)}) collective-permute-start(bf16[752,128]{1,0:T(8,128)(2,1)S(1)} %fusion.13), channel_id=1, source_target_pairs={{0,2},{1,3},{2,4},{3,5},{4,6},{5,7},{6,0},{7,1},{8,10},{9,11},{10,... | collective-permute-start | bytes 577544 | tf_op jit(solution)/shard_map/ppermute | solution.py:473
  453.2 20.0 %collective-permute-start.12 = (bf16[1984,128]{1,0:T(8,128)(2,1)S(1)}, bf16[1984,128]{1,0:T(8,128)(2,1)S(1)}, u32[]{:S(2)}, u32[]{:S(2)}) collective-permute-start(bf16[1984,128]{1,0:T(8,128)(2,1)S(1)} %fusion.2), channel_id=1, source_target_pairs={{0,8},{1,9},{2,10},{3,11},{4,12},{5,13},{6,14},{7,15},{8,0},{9,1},... | collective-permute-start | bytes 1523720 | tf_op jit(solution)/shard_map/ppermute | solution.py:473
  465.9 12.1 %copy-start.2 = (f32[1,3484,128]{2,0,1:T(1,128)S(1)}, f32[1,3484,128]{2,0,1:T(1,128)}, u32[]{:S(2)}) copy-start(f32[1,3484,128]{2,0,1:T(1,128)} %param.25) | copy-start | bytes 5351428
  466.1 5.9 %collective-permute-start.21 = (bf16[752,128]{1,0:T(8,128)(2,1)S(1)}, bf16[752,128]{1,0:T(8,128)(2,1)S(1)}, u32[]{:S(2)}, u32[]{:S(2)}) collective-permute-start(bf16[752,128]{1,0:T(8,128)(2,1)S(1)} %get-tuple-element.621), channel_id=1, source_target_pairs={{0,6},{1,7},{2,0},{3,1},{4,2},{5,3},{6,4},{7,5},{8,14},{9,15},{10,... | collective-permute-start | bytes 577544 | tf_op jit(solution)/shard_map/ppermute | solution.py:473
  472.1 5.7 %collective-permute-start.22 = (bf16[752,128]{1,0:T(8,128)(2,1)S(1)}, bf16[752,128]{1,0:T(8,128)(2,1)S(1)}, u32[]{:S(2)}, u32[]{:S(2)}) collective-permute-start(bf16[752,128]{1,0:T(8,128)(2,1)S(1)} %fusion.10), channel_id=1, source_target_pairs={{0,6},{1,7},{2,0},{3,1},{4,2},{5,3},{6,4},{7,5},{8,14},{9,15},{10,... | collective-permute-start | bytes 577544 | tf_op jit(solution)/shard_map/ppermute | solution.py:473
  473.2 4.8 copy-start.1
  473.5 4.5 copy-start

commit v4 on v3

--- a/solution.py
+++ b/solution.py
@@ -654,7 +654,7 @@
     slot_count = master.shape[1]
     share = -(-slot_count // 16) * 16
     buckets = bucket_owner.shape[1]
-    cut = share * 4 // 7 // 32 * 32 + share % 32
+    cut = share - share * 3 // 10 // 32 * 32
     pieces = pl.pallas_call(
         functools.partial(
             weight_kernel, (*dims, real_rows, replicas, buckets, share, cut)

time: 486 us -> 483 us (level)
  waiting for transfers between devices: 285 us -> 279 us
    ppermute x21, waiting for transfers between devices: 58.9 us -> 52.3 us  [hop(): return lax.ppermute(value, 'dp', route)]
  transfers between devices with their start and end apart: 37 -> 37, of which waited for: 25 -> 26; matrix products, arithmetic and copies ran while one was open for 1% -> 1% of each run, Pallas kernels for 0% -> 0%
where the time goes in v4:
time: 483 us; the launch traced here: 482 us
  waiting for transfers between devices  279 us (58%)
  starting transfers between devices  109 us (23%)
  Pallas kernels  83 us (17%)
  local copies, waits for them, and re-layouts  5.7 us (1%)
    ppermute x8, waiting for transfers between devices, backward_loop(): return (lax.ppermute(g, 'section', back_route), grads)  182 us
    ppermute x8, starting transfers between devices, forward_loop(): return (lax.ppermute(y, 'section', route), stash)  67 us
    ppermute x21, waiting for transfers between devices, hop(): return lax.ppermute(value, 'dp', route)  52.3 us
    ppermute x8, waiting for transfers between devices, forward_loop(): return (lax.ppermute(y, 'section', route), stash)  44.3 us
    ppermute x21, starting transfers between devices, hop(): return lax.ppermute(value, 'dp', route)  31.6 us
    pallas_call x9, Pallas kernels, forward_tick(): forward_call(tick.reshape(1), place, roster, received, images, taps, laye...  29.7 us
    pallas_call x9, Pallas kernels, backward_tick(): backward_call(tick.reshape(1), place, returned, cotangent, taps, layer_sc...  24 us
    pallas_call x1, Pallas kernels, body(): pl.pallas_call(functools.partial(weight_kernel, (*dims, real_rows, replic...  22.3 us
  transfers between devices with their start and end apart: 37, of which 26 were waited for; matrix products, arithmetic and copies ran while one was open for 1% of the time, Pallas kernels for 0%

profile of v4, /device:TPU:0, one launch (start us, length us, event | category | flops | bytes accessed | tf_op | source)
XLA Modules:
  0.0 482.0 jit_solution(16077736267970842006)
XLA Ops:
  0.8 1.7 reshape.122
  2.5 1.6 copy.44
  4.2 139.8 %while.46 = (s32[]{:T(128)}, bf16[256,768]{1,0:T(8,128)(2,1)}, bf16[2,256,768]{2,1,0:T(8,128)(2,1)}, bf16[2,256,768]{2,1,0:T(8,128)(2,1)}, bf16[2,256,768]{2,1,0...) while((s32[]{:T(128)}, bf16[256,768]{1,0:T(8,128)(2,1)}, ...), condition=%wide.region_1.2_spmd, body=%wide.region_0.1_spmd.sunk | while | flops 2 | bytes 1573061 | solution.py:634
  4.2 11.1 %block_forward.7 = (bf16[2,256,768]{2,1,0:T(8,128)(2,1)}, bf16[2,256,768]{2,1,0:T(8,128)(2,1)}, bf16[2,256,768]{2,1,0:T(8,128)(2,1)}, f32[2,256,128]{2,1,0:T(8,1...) custom-call(s32[1]{0:T(128)} %bitcast.96.tick, ...), custom_call_target="tpu_custom_call", output_to_operand_aliasing={{0}: (9, {}), {1}: (10, {}), {2}: (11, {}), {3}: (12, {}), ... | custom-call | tf_op jit(solution)/shard_map/while/body/eval_jaxpr/block_forward/pallas_call | solution.py:624
  15.3 2.0 collective-permute-start
  17.3 7.5 %collective-permute-done = bf16[256,768]{1,0:T(8,128)(2,1)} collective-permute-done((bf16[256,768]{1,0:T(8,128)(2,1)}, bf16[256,768]{1,0:T(8,128)(2,1)}, u32[]{:S(2)}, u32[]{:S(2)}) %collective-permute-start) | collective-permute-done | bytes 393248 | tf_op jit(solution)/shard_map/while/body/eval_jaxpr/ppermute | solution.py:632
  24.8 11.1 %block_forward.7 = (bf16[2,256,768]{2,1,0:T(8,128)(2,1)}, bf16[2,256,768]{2,1,0:T(8,128)(2,1)}, bf16[2,256,768]{2,1,0:T(8,128)(2,1)}, f32[2,256,128]{2,1,0:T(8,1...) custom-call(s32[1]{0:T(128)} %bitcast.96.tick, ...), custom_call_target="tpu_custom_call", output_to_operand_aliasing={{0}: (9, {}), {1}: (10, {}), {2}: (11, {}), {3}: (12, {}), ... | custom-call | tf_op jit(solution)/shard_map/while/body/eval_jaxpr/block_forward/pallas_call | solution.py:624
  35.9 5.1 %collective-permute-start = (bf16[256,768]{1,0:T(8,128)(2,1)}, bf16[256,768]{1,0:T(8,128)(2,1)}, u32[]{:S(2)}, u32[]{:S(2)}) collective-permute-start(bf16[256,768]{1,0:T(8,128)(2,1)} %get-tuple-element.812), channel_id=1, source_target_pairs={{0,16},{16,32},{32,48},{48,64},{64,80},{80,96},{96,112},{1,17},{17... | collective-permute-start | bytes 1179656 | tf_op jit(solution)/shard_map/while/body/eval_jaxpr/ppermute | solution.py:632
  41.0 6.6 %collective-permute-done = bf16[256,768]{1,0:T(8,128)(2,1)} collective-permute-done((bf16[256,768]{1,0:T(8,128)(2,1)}, bf16[256,768]{1,0:T(8,128)(2,1)}, u32[]{:S(2)}, u32[]{:S(2)}) %collective-permute-start) | collective-permute-done | bytes 393248 | tf_op jit(solution)/shard_map/while/body/eval_jaxpr/ppermute | solution.py:632
  48.7 15.2 %collective-permute-start = (bf16[256,768]{1,0:T(8,128)(2,1)}, bf16[256,768]{1,0:T(8,128)(2,1)}, u32[]{:S(2)}, u32[]{:S(2)}) collective-permute-start(bf16[256,768]{1,0:T(8,128)(2,1)} %get-tuple-element.812), channel_id=1, source_target_pairs={{0,16},{16,32},{32,48},{48,64},{64,80},{80,96},{96,112},{1,17},{17... | collective-permute-start | bytes 1179656 | tf_op jit(solution)/shard_map/while/body/eval_jaxpr/ppermute | solution.py:632
  63.9 5.8 %collective-permute-done = bf16[256,768]{1,0:T(8,128)(2,1)} collective-permute-done((bf16[256,768]{1,0:T(8,128)(2,1)}, bf16[256,768]{1,0:T(8,128)(2,1)}, u32[]{:S(2)}, u32[]{:S(2)}) %collective-permute-start) | collective-permute-done | bytes 393248 | tf_op jit(solution)/shard_map/while/body/eval_jaxpr/ppermute | solution.py:632
  70.8 5.1 %collective-permute-start = (bf16[256,768]{1,0:T(8,128)(2,1)}, bf16[256,768]{1,0:T(8,128)(2,1)}, u32[]{:S(2)}, u32[]{:S(2)}) collective-permute-start(bf16[256,768]{1,0:T(8,128)(2,1)} %get-tuple-element.812), channel_id=1, source_target_pairs={{0,16},{16,32},{32,48},{48,64},{64,80},{80,96},{96,112},{1,17},{17... | collective-permute-start | bytes 1179656 | tf_op jit(solution)/shard_map/while/body/eval_jaxpr/ppermute | solution.py:632
  75.9 4.9 %collective-permute-done = bf16[256,768]{1,0:T(8,128)(2,1)} collective-permute-done((bf16[256,768]{1,0:T(8,128)(2,1)}, bf16[256,768]{1,0:T(8,128)(2,1)}, u32[]{:S(2)}, u32[]{:S(2)}) %collective-permute-start) | collective-permute-done | bytes 393248 | tf_op jit(solution)/shard_map/while/body/eval_jaxpr/ppermute | solution.py:632
  81.9 15.4 %collective-permute-start = (bf16[256,768]{1,0:T(8,128)(2,1)}, bf16[256,768]{1,0:T(8,128)(2,1)}, u32[]{:S(2)}, u32[]{:S(2)}) collective-permute-start(bf16[256,768]{1,0:T(8,128)(2,1)} %get-tuple-element.812), channel_id=1, source_target_pairs={{0,16},{16,32},{32,48},{48,64},{64,80},{80,96},{96,112},{1,17},{17... | collective-permute-start | bytes 1179656 | tf_op jit(solution)/shard_map/while/body/eval_jaxpr/ppermute | solution.py:632
  97.2 4.9 %collective-permute-done = bf16[256,768]{1,0:T(8,128)(2,1)} collective-permute-done((bf16[256,768]{1,0:T(8,128)(2,1)}, bf16[256,768]{1,0:T(8,128)(2,1)}, u32[]{:S(2)}, u32[]{:S(2)}) %collective-permute-start) | collective-permute-done | bytes 393248 | tf_op jit(solution)/shard_map/while/body/eval_jaxpr/ppermute | solution.py:632
  103.1 6.0 %collective-permute-start = (bf16[256,768]{1,0:T(8,128)(2,1)}, bf16[256,768]{1,0:T(8,128)(2,1)}, u32[]{:S(2)}, u32[]{:S(2)}) collective-permute-start(bf16[256,768]{1,0:T(8,128)(2,1)} %get-tuple-element.812), channel_id=1, source_target_pairs={{0,16},{16,32},{32,48},{48,64},{64,80},{80,96},{96,112},{1,17},{17... | collective-permute-start | bytes 1179656 | tf_op jit(solution)/shard_map/while/body/eval_jaxpr/ppermute | solution.py:632
  109.2 4.9 %collective-permute-done = bf16[256,768]{1,0:T(8,128)(2,1)} collective-permute-done((bf16[256,768]{1,0:T(8,128)(2,1)}, bf16[256,768]{1,0:T(8,128)(2,1)}, u32[]{:S(2)}, u32[]{:S(2)}) %collective-permute-start) | collective-permute-done | bytes 393248 | tf_op jit(solution)/shard_map/while/body/eval_jaxpr/ppermute | solution.py:632
  115.1 12.1 %collective-permute-start = (bf16[256,768]{1,0:T(8,128)(2,1)}, bf16[256,768]{1,0:T(8,128)(2,1)}, u32[]{:S(2)}, u32[]{:S(2)}) collective-permute-start(bf16[256,768]{1,0:T(8,128)(2,1)} %get-tuple-element.812), channel_id=1, source_target_pairs={{0,16},{16,32},{32,48},{48,64},{64,80},{80,96},{96,112},{1,17},{17... | collective-permute-start | bytes 1179656 | tf_op jit(solution)/shard_map/while/body/eval_jaxpr/ppermute | solution.py:632
  127.2 4.9 %collective-permute-done = bf16[256,768]{1,0:T(8,128)(2,1)} collective-permute-done((bf16[256,768]{1,0:T(8,128)(2,1)}, bf16[256,768]{1,0:T(8,128)(2,1)}, u32[]{:S(2)}, u32[]{:S(2)}) %collective-permute-start) | collective-permute-done | bytes 393248 | tf_op jit(solution)/shard_map/while/body/eval_jaxpr/ppermute | solution.py:632
  133.1 6.0 %collective-permute-start = (bf16[256,768]{1,0:T(8,128)(2,1)}, bf16[256,768]{1,0:T(8,128)(2,1)}, u32[]{:S(2)}, u32[]{:S(2)}) collective-permute-start(bf16[256,768]{1,0:T(8,128)(2,1)} %get-tuple-element.812), channel_id=1, source_target_pairs={{0,16},{16,32},{32,48},{48,64},{64,80},{80,96},{96,112},{1,17},{17... | collective-permute-start | bytes 1179656 | tf_op jit(solution)/shard_map/while/body/eval_jaxpr/ppermute | solution.py:632
  139.1 4.9 %collective-permute-done = bf16[256,768]{1,0:T(8,128)(2,1)} collective-permute-done((bf16[256,768]{1,0:T(8,128)(2,1)}, bf16[256,768]{1,0:T(8,128)(2,1)}, u32[]{:S(2)}, u32[]{:S(2)}) %collective-permute-start) | collective-permute-done | bytes 393248 | tf_op jit(solution)/shard_map/while/body/eval_jaxpr/ppermute | solution.py:632
  144.0 1.2 block_forward.6
  145.2 208.5 %while.47 = (s32[]{:T(128)}, bf16[256,768]{1,0:T(8,128)(2,1)}, bf16[2,256,768]{2,1,0:T(8,128)(2,1)}, bf16[2,256,3072]{2,1,0:T(8,128)(2,1)}, bf16[2,256,768]{2,1,...) while((s32[]{:T(128)}, bf16[256,768]{1,0:T(8,128)(2,1)}, ...), condition=%wide.region_3.4_spmd, body=%wide.region_2.3_spmd.sunk | while | flops 2 | bytes 1573045 | solution.py:649
  145.2 1.1 block_backward.7
  146.3 1.3 collective-permute-start.1
  147.6 17.6 %collective-permute-done.1 = bf16[256,768]{1,0:T(8,128)(2,1)} collective-permute-done((bf16[256,768]{1,0:T(8,128)(2,1)}, bf16[256,768]{1,0:T(8,128)(2,1)}, u32[]{:S(2)}, u32[]{:S(2)}) %collective-permute-start.1) | collective-permute-done | bytes 393248 | tf_op jit(solution)/shard_map/while/body/eval_jaxpr/ppermute | solution.py:647
  165.2 1.1 block_backward.7
  166.3 1.3 collective-permute-start.1
  167.6 9.8 %collective-permute-done.1 = bf16[256,768]{1,0:T(8,128)(2,1)} collective-permute-done((bf16[256,768]{1,0:T(8,128)(2,1)}, bf16[256,768]{1,0:T(8,128)(2,1)}, u32[]{:S(2)}, u32[]{:S(2)}) %collective-permute-start.1) | collective-permute-done | bytes 393248 | tf_op jit(solution)/shard_map/while/body/eval_jaxpr/ppermute | solution.py:647
  178.5 1.3 collective-permute-start.1
  179.8 20.0 %collective-permute-done.1 = bf16[256,768]{1,0:T(8,128)(2,1)} collective-permute-done((bf16[256,768]{1,0:T(8,128)(2,1)}, bf16[256,768]{1,0:T(8,128)(2,1)}, u32[]{:S(2)}, u32[]{:S(2)}) %collective-permute-start.1) | collective-permute-done | bytes 393248 | tf_op jit(solution)/shard_map/while/body/eval_jaxpr/ppermute | solution.py:647
  200.9 1.3 collective-permute-start.1
  202.2 8.7 %collective-permute-done.1 = bf16[256,768]{1,0:T(8,128)(2,1)} collective-permute-done((bf16[256,768]{1,0:T(8,128)(2,1)}, bf16[256,768]{1,0:T(8,128)(2,1)}, u32[]{:S(2)}, u32[]{:S(2)}) %collective-permute-start.1) | collective-permute-done | bytes 393248 | tf_op jit(solution)/shard_map/while/body/eval_jaxpr/ppermute | solution.py:647
  212.0 1.3 collective-permute-start.1
  213.3 24.2 %collective-permute-done.1 = bf16[256,768]{1,0:T(8,128)(2,1)} collective-permute-done((bf16[256,768]{1,0:T(8,128)(2,1)}, bf16[256,768]{1,0:T(8,128)(2,1)}, u32[]{:S(2)}, u32[]{:S(2)}) %collective-permute-start.1) | collective-permute-done | bytes 393248 | tf_op jit(solution)/shard_map/while/body/eval_jaxpr/ppermute | solution.py:647
  238.6 1.3 collective-permute-start.1
  239.9 8.7 %collective-permute-done.1 = bf16[256,768]{1,0:T(8,128)(2,1)} collective-permute-done((bf16[256,768]{1,0:T(8,128)(2,1)}, bf16[256,768]{1,0:T(8,128)(2,1)}, u32[]{:S(2)}, u32[]{:S(2)}) %collective-permute-start.1) | collective-permute-done | bytes 393248 | tf_op jit(solution)/shard_map/while/body/eval_jaxpr/ppermute | solution.py:647
  249.7 1.3 collective-permute-start.1
  251.0 80.3 %collective-permute-done.1 = bf16[256,768]{1,0:T(8,128)(2,1)} collective-permute-done((bf16[256,768]{1,0:T(8,128)(2,1)}, bf16[256,768]{1,0:T(8,128)(2,1)}, u32[]{:S(2)}, u32[]{:S(2)}) %collective-permute-start.1) | collective-permute-done | bytes 393248 | tf_op jit(solution)/shard_map/while/body/eval_jaxpr/ppermute | solution.py:647
  331.2 8.3 %block_backward.7 = (bf16[2,256,768]{2,1,0:T(8,128)(2,1)}, bf16[2,256,3072]{2,1,0:T(8,128)(2,1)}, bf16[2,256,768]{2,1,0:T(8,128)(2,1)}, bf16[256,768]{1,0:T(8,128)(2,1)}) custom-call(s32[1]{0:T(128)} %bitcast.97.tick, s32[2]{0:T(128)S(1)} %get-tuple-element.924.place, ...), custom_call_target="tpu_custom_call", output_to_operand_aliasing={{0}: (11, {}), {1}: (12, {}), {2}: (13, {})} | custom-call | tf_op jit(solution)/shard_map/while/body/eval_jaxpr/block_backward/pallas_call | solution.py:639
  339.5 1.3 collective-permute-start.1
  340.8 13.0 %collective-permute-done.1 = bf16[256,768]{1,0:T(8,128)(2,1)} collective-permute-done((bf16[256,768]{1,0:T(8,128)(2,1)}, bf16[256,768]{1,0:T(8,128)(2,1)}, u32[]{:S(2)}, u32[]{:S(2)}) %collective-permute-start.1) | collective-permute-done | bytes 393248 | tf_op jit(solution)/shard_map/while/body/eval_jaxpr/ppermute | solution.py:647
  353.7 8.2 %block_backward.6 = (bf16[2,256,768]{2,1,0:T(8,128)(2,1)}, bf16[2,256,3072]{2,1,0:T(8,128)(2,1)}, bf16[2,256,768]{2,1,0:T(8,128)(2,1)}, bf16[256,768]{1,0:T(8,128)(2,1)}) custom-call(s32[1]{0:T(128)} %constant.180.clone.1.tick, s32[2]{0:T(128)S(1)} %get-tuple-element.984, ...), custom_call_target="tpu_custom_call", output_to_operand_aliasing={{0}: (11, {}), {1}: (12, {}), {2}: (13, {})} | custom-call | tf_op jit(solution)/shard_map/block_backward/pallas_call | solution.py:639
  362.6 22.3 %weight_grads.1 = (bf16[2,2464,128]{2,1,0:T(8,128)(2,1)}, bf16[2,2464,128]{2,1,0:T(8,128)(2,1)}, bf16[2,2464,128]{2,1,0:T(8,128)(2,1)}, bf16[2,2464,128]{2,1,0:T...) custom-call(s32[49]{0:T(128)} %bitcast.107, ...), custom_call_target="tpu_custom_call" | custom-call | tf_op jit(solution)/shard_map/weight_grads/pallas_call | solution.py:658
  385.7 2.6 collective-permute-done.5
  388.2 1.7 fusion.7
  390.0 5.8 %collective-permute-start.6 = (bf16[2464,128]{1,0:T(8,128)(2,1)S(1)}, bf16[2464,128]{1,0:T(8,128)(2,1)S(1)}, u32[]{:S(2)}, u32[]{:S(2)}) collective-permute-start(bf16[2464,128]{1,0:T(8,128)(2,1)S(1)} %get-tuple-element.624), channel_id=1, source_target_pairs={{0,2},{1,3},{2,4},{3,5},{4,6},{5,7},{6,0},{7,1},{8,10},{9,11},{10,... | collective-permute-start | bytes 1892360 | tf_op jit(solution)/shard_map/ppermute | solution.py:473
  395.8 1.3 collective-permute-start.9
  397.9 4.4 collective-permute-start.15
  402.3 9.2 %collective-permute-done.6 = bf16[2464,128]{1,0:T(8,128)(2,1)S(1)} collective-permute-done((bf16[2464,128]{1,0:T(8,128)(2,1)S(1)}, bf16[2464,128]{1,0:T(8,128)(2,1)S(1)}, u32[]{:S(2)}, u32[]{:S(2)}) %collective-permute-start.6) | collective-permute-done | bytes 630816 | tf_op jit(solution)/shard_map/ppermute | solution.py:473
  411.5 4.1 collective-permute-start.19
  416.1 1.6 collective-permute-start.10
  418.2 8.7 %collective-permute-done.19 = bf16[4,512,128]{2,1,0:T(8,128)(2,1)S(1)} collective-permute-done((bf16[4,512,128]{2,1,0:T(8,128)(2,1)S(1)}, bf16[4,512,128]{2,1,0:T(8,128)(2,1)S(1)}, u32[]{:S(2)}, u32[]{:S(2)}) %collective-permute-start.19) | collective-permute-done | bytes 524320 | tf_op jit(solution)/shard_map/ppermute | solution.py:473
  427.4 9.2 %collective-permute-done.16 = bf16[512,128]{1,0:T(8,128)(2,1)S(1)} collective-permute-done((bf16[512,128]{1,0:T(8,128)(2,1)S(1)}, bf16[512,128]{1,0:T(8,128)(2,1)S(1)}, u32[]{:S(2)}, u32[]{:S(2)}) %collective-permute-start.16) | collective-permute-done | bytes 131104 | tf_op jit(solution)/shard_map/ppermute | solution.py:473
  437.3 3.3 collective-permute-start.11
  440.6 2.3 collective-permute-done.17
  443.1 11.5 %collective-permute-done.20 = bf16[512,128]{1,0:T(8,128)(2,1)S(1)} collective-permute-done((bf16[512,128]{1,0:T(8,128)(2,1)S(1)}, bf16[512,128]{1,0:T(8,128)(2,1)S(1)}, u32[]{:S(2)}, u32[]{:S(2)}) %collective-permute-start.20) | collective-permute-done | bytes 131104 | tf_op jit(solution)/shard_map/ppermute | solution.py:473
  454.7 3.8 collective-permute-start.21
  458.8 1.5 collective-permute-start.12
  460.2 1.2 collective-permute-done.21
  461.5 3.8 collective-permute-start.22
  465.3 2.5 collective-permute-done.22
  467.9 4.4 collective-permute-done.8
  475.0 7.0 %adam.1 = (f32[871,4,128]{2,1,0:T(4,128)}, f32[871,4,128]{2,1,0:T(4,128)}, f32[871,4,128]{2,1,0:T(4,128)}) custom-call(bf16[3488,128]{1,0:T(8,128)(2,1)S(1)} %pad_maximum_fusion.g_i, f32[871,4,128]{2,1,0:T(4,128)S(1)} %bitcast.98, f32[871,4,128]{2,1,0:T(4,128)S(1)} %bitcast.99, f32[871,4,128]{2,1,0:T(4,128)S(1)} %bitcast.100), custom_call_target="tpu_custom_call" | custom-call | tf_op jit(solution)/shard_map/adam/pallas_call | solution.py:693
  (74 shorter events, 19.5 us)
Async XLA Ops:
  15.3 9.5 %collective-permute-start = (bf16[256,768]{1,0:T(8,128)(2,1)}, bf16[256,768]{1,0:T(8,128)(2,1)}, u32[]{:S(2)}, u32[]{:S(2)}) collective-permute-start(bf16[256,768]{1,0:T(8,128)(2,1)} %get-tuple-element.812), channel_id=1, source_target_pairs={{0,16},{16,32},{32,48},{48,64},{64,80},{80,96},{96,112},{1,17},{17... | collective-permute-start | bytes 1179656 | tf_op jit(solution)/shard_map/while/body/eval_jaxpr/ppermute | solution.py:632
  35.9 11.8 %collective-permute-start = (bf16[256,768]{1,0:T(8,128)(2,1)}, bf16[256,768]{1,0:T(8,128)(2,1)}, u32[]{:S(2)}, u32[]{:S(2)}) collective-permute-start(bf16[256,768]{1,0:T(8,128)(2,1)} %get-tuple-element.812), channel_id=1, source_target_pairs={{0,16},{16,32},{32,48},{48,64},{64,80},{80,96},{96,112},{1,17},{17... | collective-permute-start | bytes 1179656 | tf_op jit(solution)/shard_map/while/body/eval_jaxpr/ppermute | solution.py:632
  48.7 21.0 %collective-permute-start = (bf16[256,768]{1,0:T(8,128)(2,1)}, bf16[256,768]{1,0:T(8,128)(2,1)}, u32[]{:S(2)}, u32[]{:S(2)}) collective-permute-start(bf16[256,768]{1,0:T(8,128)(2,1)} %get-tuple-element.812), channel_id=1, source_target_pairs={{0,16},{16,32},{32,48},{48,64},{64,80},{80,96},{96,112},{1,17},{17... | collective-permute-start | bytes 1179656 | tf_op jit(solution)/shard_map/while/body/eval_jaxpr/ppermute | solution.py:632
  70.8 10.1 %collective-permute-start = (bf16[256,768]{1,0:T(8,128)(2,1)}, bf16[256,768]{1,0:T(8,128)(2,1)}, u32[]{:S(2)}, u32[]{:S(2)}) collective-permute-start(bf16[256,768]{1,0:T(8,128)(2,1)} %get-tuple-element.812), channel_id=1, source_target_pairs={{0,16},{16,32},{32,48},{48,64},{64,80},{80,96},{96,112},{1,17},{17... | collective-permute-start | bytes 1179656 | tf_op jit(solution)/shard_map/while/body/eval_jaxpr/ppermute | solution.py:632
  81.9 20.2 %collective-permute-start = (bf16[256,768]{1,0:T(8,128)(2,1)}, bf16[256,768]{1,0:T(8,128)(2,1)}, u32[]{:S(2)}, u32[]{:S(2)}) collective-permute-start(bf16[256,768]{1,0:T(8,128)(2,1)} %get-tuple-element.812), channel_id=1, source_target_pairs={{0,16},{16,32},{32,48},{48,64},{64,80},{80,96},{96,112},{1,17},{17... | collective-permute-start | bytes 1179656 | tf_op jit(solution)/shard_map/while/body/eval_jaxpr/ppermute | solution.py:632
  103.1 10.9 %collective-permute-start = (bf16[256,768]{1,0:T(8,128)(2,1)}, bf16[256,768]{1,0:T(8,128)(2,1)}, u32[]{:S(2)}, u32[]{:S(2)}) collective-permute-start(bf16[256,768]{1,0:T(8,128)(2,1)} %get-tuple-element.812), channel_id=1, source_target_pairs={{0,16},{16,32},{32,48},{48,64},{64,80},{80,96},{96,112},{1,17},{17... | collective-permute-start | bytes 1179656 | tf_op jit(solution)/shard_map/while/body/eval_jaxpr/ppermute | solution.py:632
  115.1 17.0 %collective-permute-start = (bf16[256,768]{1,0:T(8,128)(2,1)}, bf16[256,768]{1,0:T(8,128)(2,1)}, u32[]{:S(2)}, u32[]{:S(2)}) collective-permute-start(bf16[256,768]{1,0:T(8,128)(2,1)} %get-tuple-element.812), channel_id=1, source_target_pairs={{0,16},{16,32},{32,48},{48,64},{64,80},{80,96},{96,112},{1,17},{17... | collective-permute-start | bytes 1179656 | tf_op jit(solution)/shard_map/while/body/eval_jaxpr/ppermute | solution.py:632
  133.1 10.9 %collective-permute-start = (bf16[256,768]{1,0:T(8,128)(2,1)}, bf16[256,768]{1,0:T(8,128)(2,1)}, u32[]{:S(2)}, u32[]{:S(2)}) collective-permute-start(bf16[256,768]{1,0:T(8,128)(2,1)} %get-tuple-element.812), channel_id=1, source_target_pairs={{0,16},{16,32},{32,48},{48,64},{64,80},{80,96},{96,112},{1,17},{17... | collective-permute-start | bytes 1179656 | tf_op jit(solution)/shard_map/while/body/eval_jaxpr/ppermute | solution.py:632
  144.0 1.2 copy-start.8
  146.3 18.9 %collective-permute-start.1 = (bf16[256,768]{1,0:T(8,128)(2,1)}, bf16[256,768]{1,0:T(8,128)(2,1)}, u32[]{:S(2)}, u32[]{:S(2)}) collective-permute-start(bf16[256,768]{1,0:T(8,128)(2,1)} %get-tuple-element.834), channel_id=1, source_target_pairs={{16,0},{32,16},{48,32},{64,48},{80,64},{96,80},{112,96},{17,1},{33... | collective-permute-start | bytes 1179656 | tf_op jit(solution)/shard_map/while/body/eval_jaxpr/ppermute | solution.py:647
  166.3 11.1 %collective-permute-start.1 = (bf16[256,768]{1,0:T(8,128)(2,1)}, bf16[256,768]{1,0:T(8,128)(2,1)}, u32[]{:S(2)}, u32[]{:S(2)}) collective-permute-start(bf16[256,768]{1,0:T(8,128)(2,1)} %get-tuple-element.834), channel_id=1, source_target_pairs={{16,0},{32,16},{48,32},{64,48},{80,64},{96,80},{112,96},{17,1},{33... | collective-permute-start | bytes 1179656 | tf_op jit(solution)/shard_map/while/body/eval_jaxpr/ppermute | solution.py:647
  178.5 21.3 %collective-permute-start.1 = (bf16[256,768]{1,0:T(8,128)(2,1)}, bf16[256,768]{1,0:T(8,128)(2,1)}, u32[]{:S(2)}, u32[]{:S(2)}) collective-permute-start(bf16[256,768]{1,0:T(8,128)(2,1)} %get-tuple-element.834), channel_id=1, source_target_pairs={{16,0},{32,16},{48,32},{64,48},{80,64},{96,80},{112,96},{17,1},{33... | collective-permute-start | bytes 1179656 | tf_op jit(solution)/shard_map/while/body/eval_jaxpr/ppermute | solution.py:647
  200.9 10.0 %collective-permute-start.1 = (bf16[256,768]{1,0:T(8,128)(2,1)}, bf16[256,768]{1,0:T(8,128)(2,1)}, u32[]{:S(2)}, u32[]{:S(2)}) collective-permute-start(bf16[256,768]{1,0:T(8,128)(2,1)} %get-tuple-element.834), channel_id=1, source_target_pairs={{16,0},{32,16},{48,32},{64,48},{80,64},{96,80},{112,96},{17,1},{33... | collective-permute-start | bytes 1179656 | tf_op jit(solution)/shard_map/while/body/eval_jaxpr/ppermute | solution.py:647
  212.0 25.5 %collective-permute-start.1 = (bf16[256,768]{1,0:T(8,128)(2,1)}, bf16[256,768]{1,0:T(8,128)(2,1)}, u32[]{:S(2)}, u32[]{:S(2)}) collective-permute-start(bf16[256,768]{1,0:T(8,128)(2,1)} %get-tuple-element.834), channel_id=1, source_target_pairs={{16,0},{32,16},{48,32},{64,48},{80,64},{96,80},{112,96},{17,1},{33... | collective-permute-start | bytes 1179656 | tf_op jit(solution)/shard_map/while/body/eval_jaxpr/ppermute | solution.py:647
  238.6 10.0 %collective-permute-start.1 = (bf16[256,768]{1,0:T(8,128)(2,1)}, bf16[256,768]{1,0:T(8,128)(2,1)}, u32[]{:S(2)}, u32[]{:S(2)}) collective-permute-start(bf16[256,768]{1,0:T(8,128)(2,1)} %get-tuple-element.834), channel_id=1, source_target_pairs={{16,0},{32,16},{48,32},{64,48},{80,64},{96,80},{112,96},{17,1},{33... | collective-permute-start | bytes 1179656 | tf_op jit(solution)/shard_map/while/body/eval_jaxpr/ppermute | solution.py:647
  249.7 81.6 %collective-permute-start.1 = (bf16[256,768]{1,0:T(8,128)(2,1)}, bf16[256,768]{1,0:T(8,128)(2,1)}, u32[]{:S(2)}, u32[]{:S(2)}) collective-permute-start(bf16[256,768]{1,0:T(8,128)(2,1)} %get-tuple-element.834), channel_id=1, source_target_pairs={{16,0},{32,16},{48,32},{64,48},{80,64},{96,80},{112,96},{17,1},{33... | collective-permute-start | bytes 1179656 | tf_op jit(solution)/shard_map/while/body/eval_jaxpr/ppermute | solution.py:647
  339.5 14.3 %collective-permute-start.1 = (bf16[256,768]{1,0:T(8,128)(2,1)}, bf16[256,768]{1,0:T(8,128)(2,1)}, u32[]{:S(2)}, u32[]{:S(2)}) collective-permute-start(bf16[256,768]{1,0:T(8,128)(2,1)} %get-tuple-element.834), channel_id=1, source_target_pairs={{16,0},{32,16},{48,32},{64,48},{80,64},{96,80},{112,96},{17,1},{33... | collective-permute-start | bytes 1179656 | tf_op jit(solution)/shard_map/while/body/eval_jaxpr/ppermute | solution.py:647
  385.0 3.3 collective-permute-start.5
  385.1 12.8 %collective-permute-start.4 = (bf16[2,2464,128]{2,1,0:T(8,128)(2,1)}, bf16[2,2464,128]{2,1,0:T(8,128)(2,1)S(1)}, u32[]{:S(2)}, u32[]{:S(2)}) collective-permute-start(bf16[2,2464,128]{2,1,0:T(8,128)(2,1)} %get-tuple-element.542), channel_id=1, source_target_pairs={{0,1},{1,0},{2,3},{3,2},{4,5},{5,4},{6,7},{7,6},{8,9},{9,8},{10,11... | collective-permute-start | bytes 3784712 | tf_op jit(solution)/shard_map/ppermute | solution.py:473
  385.6 11.5 %collective-permute-start.14 = (bf16[8,512,128]{2,1,0:T(8,128)(2,1)}, bf16[8,512,128]{2,1,0:T(8,128)(2,1)S(1)}, u32[]{:S(2)}, u32[]{:S(2)}) collective-permute-start(bf16[8,512,128]{2,1,0:T(8,128)(2,1)} %get-tuple-element.548), channel_id=1, source_target_pairs={{0,1},{1,0},{2,3},{3,2},{4,5},{5,4},{6,7},{7,6},{8,9},{9,8},{10,11... | collective-permute-start | bytes 3145736 | tf_op jit(solution)/shard_map/ppermute | solution.py:473
  388.2 8.8 %copy-start.10 = (bf16[2,2464,128]{2,1,0:T(8,128)(2,1)S(1)}, bf16[2,2464,128]{2,1,0:T(8,128)(2,1)}, u32[]{:S(2)}) copy-start(bf16[2,2464,128]{2,1,0:T(8,128)(2,1)} %get-tuple-element.540) | copy-start | bytes 3784708
  388.2 8.8 %copy-start.11 = (bf16[8,512,128]{2,1,0:T(8,128)(2,1)S(1)}, bf16[8,512,128]{2,1,0:T(8,128)(2,1)}, u32[]{:S(2)}) copy-start(bf16[8,512,128]{2,1,0:T(8,128)(2,1)} %get-tuple-element.546) | copy-start | bytes 3145732
  388.2 9.4 %copy-start.6 = (bf16[8,512,128]{2,1,0:T(8,128)(2,1)S(1)}, bf16[8,512,128]{2,1,0:T(8,128)(2,1)}, u32[]{:S(2)}) copy-start(bf16[8,512,128]{2,1,0:T(8,128)(2,1)} %get-tuple-element.547) | copy-start | bytes 3145732
  390.0 21.5 %collective-permute-start.6 = (bf16[2464,128]{1,0:T(8,128)(2,1)S(1)}, bf16[2464,128]{1,0:T(8,128)(2,1)S(1)}, u32[]{:S(2)}, u32[]{:S(2)}) collective-permute-start(bf16[2464,128]{1,0:T(8,128)(2,1)S(1)} %get-tuple-element.624), channel_id=1, source_target_pairs={{0,2},{1,3},{2,4},{3,5},{4,6},{5,7},{6,0},{7,1},{8,10},{9,11},{10,... | collective-permute-start | bytes 1892360 | tf_op jit(solution)/shard_map/ppermute | solution.py:473
  395.8 19.8 %collective-permute-start.9 = (bf16[2464,128]{1,0:T(8,128)(2,1)S(1)}, bf16[2464,128]{1,0:T(8,128)(2,1)S(1)}, u32[]{:S(2)}, u32[]{:S(2)}) collective-permute-start(bf16[2464,128]{1,0:T(8,128)(2,1)S(1)} %get-tuple-element.625), channel_id=1, source_target_pairs={{0,6},{1,7},{2,0},{3,1},{4,2},{5,3},{6,4},{7,5},{8,14},{9,15},{10,... | collective-permute-start | bytes 1892360 | tf_op jit(solution)/shard_map/ppermute | solution.py:473
  397.1 39.7 %collective-permute-start.3 = (bf16[2,2464,128]{2,1,0:T(8,128)(2,1)S(1)}, bf16[2,2464,128]{2,1,0:T(8,128)(2,1)S(1)}, u32[]{:S(2)}, u32[]{:S(2)}) collective-permute-start(bf16[2,2464,128]{2,1,0:T(8,128)(2,1)S(1)} %copy-done.10), channel_id=1, source_target_pairs={{0,1},{1,0},{2,3},{3,2},{4,5},{5,4},{6,7},{7,6},{8,9},{9,8},{10,11... | collective-permute-start | bytes 3784712 | tf_op jit(solution)/shard_map/ppermute | solution.py:473
  397.1 20.6 %collective-permute-start.13 = (bf16[8,512,128]{2,1,0:T(8,128)(2,1)S(1)}, bf16[8,512,128]{2,1,0:T(8,128)(2,1)S(1)}, u32[]{:S(2)}, u32[]{:S(2)}) collective-permute-start(bf16[8,512,128]{2,1,0:T(8,128)(2,1)S(1)} %copy-done.11), channel_id=1, source_target_pairs={{0,1},{1,0},{2,3},{3,2},{4,5},{5,4},{6,7},{7,6},{8,9},{9,8},{10,11... | collective-permute-start | bytes 3145736 | tf_op jit(solution)/shard_map/ppermute | solution.py:473
  397.6 18.0 %copy-start.4 = (bf16[2,2464,128]{2,1,0:T(8,128)(2,1)S(1)}, bf16[2,2464,128]{2,1,0:T(8,128)(2,1)}, u32[]{:S(2)}) copy-start(bf16[2,2464,128]{2,1,0:T(8,128)(2,1)} %get-tuple-element.541) | copy-start | bytes 3784708
  397.9 20.3 %collective-permute-start.15 = (bf16[4,512,128]{2,1,0:T(8,128)(2,1)S(1)}, bf16[4,512,128]{2,1,0:T(8,128)(2,1)S(1)}, u32[]{:S(2)}, u32[]{:S(2)}) collective-permute-start(bf16[4,512,128]{2,1,0:T(8,128)(2,1)S(1)} %get-tuple-element.630), channel_id=1, source_target_pairs={{0,8},{1,9},{2,10},{3,11},{4,12},{5,13},{6,14},{7,15},{8,0},{9,1},... | collective-permute-start | bytes 1572872 | tf_op jit(solution)/shard_map/ppermute | solution.py:473
  411.5 15.4 %collective-permute-start.19 = (bf16[4,512,128]{2,1,0:T(8,128)(2,1)S(1)}, bf16[4,512,128]{2,1,0:T(8,128)(2,1)S(1)}, u32[]{:S(2)}, u32[]{:S(2)}) collective-permute-start(bf16[4,512,128]{2,1,0:T(8,128)(2,1)S(1)} %get-tuple-element.631), channel_id=1, source_target_pairs={{0,8},{1,9},{2,10},{3,11},{4,12},{5,13},{6,14},{7,15},{8,0},{9,1},... | collective-permute-start | bytes 1572872 | tf_op jit(solution)/shard_map/ppermute | solution.py:473
  415.6 11.4 %copy-start.7 = (bf16[8,512,128]{2,1,0:T(8,128)(2,1)S(1)}, bf16[8,512,128]{2,1,0:T(8,128)(2,1)}, u32[]{:S(2)}) copy-start(bf16[8,512,128]{2,1,0:T(8,128)(2,1)} %get-tuple-element.545) | copy-start | bytes 3145732
  415.6 11.8 %copy-start.9 = (bf16[2,2464,128]{2,1,0:T(8,128)(2,1)S(1)}, bf16[2,2464,128]{2,1,0:T(8,128)(2,1)}, u32[]{:S(2)}) copy-start(bf16[2,2464,128]{2,1,0:T(8,128)(2,1)} %get-tuple-element.538) | copy-start | bytes 3784708
  416.1 20.7 %copy-start.3 = (bf16[2,2464,128]{2,1,0:T(8,128)(2,1)S(1)}, bf16[2,2464,128]{2,1,0:T(8,128)(2,1)}, u32[]{:S(2)}) copy-start(bf16[2,2464,128]{2,1,0:T(8,128)(2,1)} %get-tuple-element.539) | copy-start | bytes 3784708
  416.1 20.7 %collective-permute-start.10 = (bf16[2464,128]{1,0:T(8,128)(2,1)S(1)}, bf16[2464,128]{1,0:T(8,128)(2,1)S(1)}, u32[]{:S(2)}, u32[]{:S(2)}) collective-permute-start(bf16[2464,128]{1,0:T(8,128)(2,1)S(1)} %get-tuple-element.623), channel_id=1, source_target_pairs={{0,6},{1,7},{2,0},{3,1},{4,2},{5,3},{6,4},{7,5},{8,14},{9,15},{10,... | collective-permute-start | bytes 1892360 | tf_op jit(solution)/shard_map/ppermute | solution.py:473
  417.7 19.0 %collective-permute-start.7 = (bf16[2464,128]{1,0:T(8,128)(2,1)S(1)}, bf16[2464,128]{1,0:T(8,128)(2,1)S(1)}, u32[]{:S(2)}, u32[]{:S(2)}) collective-permute-start(bf16[2464,128]{1,0:T(8,128)(2,1)S(1)} %get-tuple-element.622), channel_id=1, source_target_pairs={{0,2},{1,3},{2,4},{3,5},{4,6},{5,7},{6,0},{7,1},{8,10},{9,11},{10,... | collective-permute-start | bytes 1892360 | tf_op jit(solution)/shard_map/ppermute | solution.py:473
  427.0 9.5 %collective-permute-start.16 = (bf16[512,128]{1,0:T(8,128)(2,1)S(1)}, bf16[512,128]{1,0:T(8,128)(2,1)S(1)}, u32[]{:S(2)}, u32[]{:S(2)}) collective-permute-start(bf16[512,128]{1,0:T(8,128)(2,1)S(1)} %get-tuple-element.628), channel_id=1, source_target_pairs={{0,2},{1,3},{2,4},{3,5},{4,6},{5,7},{6,0},{7,1},{8,10},{9,11},{10,... | collective-permute-start | bytes 393224 | tf_op jit(solution)/shard_map/ppermute | solution.py:473
  427.4 31.1 %collective-permute-start.2 = (bf16[2,2464,128]{2,1,0:T(8,128)(2,1)S(1)}, bf16[2,2464,128]{2,1,0:T(8,128)(2,1)S(1)}, u32[]{:S(2)}, u32[]{:S(2)}) collective-permute-start(bf16[2,2464,128]{2,1,0:T(8,128)(2,1)S(1)} %copy-done.9), channel_id=1, source_target_pairs={{0,1},{1,0},{2,3},{3,2},{4,5},{5,4},{6,7},{7,6},{8,9},{9,8},{10,11... | collective-permute-start | bytes 3784712 | tf_op jit(solution)/shard_map/ppermute | solution.py:473
  436.6 6.2 %collective-permute-start.17 = (bf16[512,128]{1,0:T(8,128)(2,1)S(1)}, bf16[512,128]{1,0:T(8,128)(2,1)S(1)}, u32[]{:S(2)}, u32[]{:S(2)}) collective-permute-start(bf16[512,128]{1,0:T(8,128)(2,1)S(1)} %fusion.12), channel_id=1, source_target_pairs={{0,2},{1,3},{2,4},{3,5},{4,6},{5,7},{6,0},{7,1},{8,10},{9,11},{10,... | collective-permute-start | bytes 393224 | tf_op jit(solution)/shard_map/ppermute | solution.py:473
  437.3 21.2 %copy-start.5 = (bf16[2,2464,128]{2,1,0:T(8,128)(2,1)S(1)}, bf16[2,2464,128]{2,1,0:T(8,128)(2,1)}, u32[]{:S(2)}) copy-start(bf16[2,2464,128]{2,1,0:T(8,128)(2,1)} %get-tuple-element.537) | copy-start | bytes 3784708
  437.3 21.2 %collective-permute-start.11 = (bf16[2464,128]{1,0:T(8,128)(2,1)S(1)}, bf16[2464,128]{1,0:T(8,128)(2,1)S(1)}, u32[]{:S(2)}, u32[]{:S(2)}) collective-permute-start(bf16[2464,128]{1,0:T(8,128)(2,1)S(1)} %get-tuple-element.621), channel_id=1, source_target_pairs={{0,6},{1,7},{2,0},{3,1},{4,2},{5,3},{6,4},{7,5},{8,14},{9,15},{10,... | collective-permute-start | bytes 1892360 | tf_op jit(solution)/shard_map/ppermute | solution.py:473
  440.6 14.0 %collective-permute-start.20 = (bf16[512,128]{1,0:T(8,128)(2,1)S(1)}, bf16[512,128]{1,0:T(8,128)(2,1)S(1)}, u32[]{:S(2)}, u32[]{:S(2)}) collective-permute-start(bf16[512,128]{1,0:T(8,128)(2,1)S(1)} %get-tuple-element.629), channel_id=1, source_target_pairs={{0,6},{1,7},{2,0},{3,1},{4,2},{5,3},{6,4},{7,5},{8,14},{9,15},{10,... | collective-permute-start | bytes 393224 | tf_op jit(solution)/shard_map/ppermute | solution.py:473
  443.0 11.6 %collective-permute-start.18 = (bf16[512,128]{1,0:T(8,128)(2,1)S(1)}, bf16[512,128]{1,0:T(8,128)(2,1)S(1)}, u32[]{:S(2)}, u32[]{:S(2)}) collective-permute-start(bf16[512,128]{1,0:T(8,128)(2,1)S(1)} %fusion.13), channel_id=1, source_target_pairs={{0,2},{1,3},{2,4},{3,5},{4,6},{5,7},{6,0},{7,1},{8,10},{9,11},{10,... | collective-permute-start | bytes 393224 | tf_op jit(solution)/shard_map/ppermute | solution.py:473
  454.7 6.7 %collective-permute-start.21 = (bf16[512,128]{1,0:T(8,128)(2,1)S(1)}, bf16[512,128]{1,0:T(8,128)(2,1)S(1)}, u32[]{:S(2)}, u32[]{:S(2)}) collective-permute-start(bf16[512,128]{1,0:T(8,128)(2,1)S(1)} %get-tuple-element.627), channel_id=1, source_target_pairs={{0,6},{1,7},{2,0},{3,1},{4,2},{5,3},{6,4},{7,5},{8,14},{9,15},{10,... | collective-permute-start | bytes 393224 | tf_op jit(solution)/shard_map/ppermute | solution.py:473
  458.5 13.8 %collective-permute-start.8 = (bf16[2464,128]{1,0:T(8,128)(2,1)S(1)}, bf16[2464,128]{1,0:T(8,128)(2,1)S(1)}, u32[]{:S(2)}, u32[]{:S(2)}) collective-permute-start(bf16[2464,128]{1,0:T(8,128)(2,1)S(1)} %get-tuple-element.620), channel_id=1, source_target_pairs={{0,2},{1,3},{2,4},{3,5},{4,6},{5,7},{6,0},{7,1},{8,10},{9,11},{10,... | collective-permute-start | bytes 1892360 | tf_op jit(solution)/shard_map/ppermute | solution.py:473
  458.5 14.8 %copy-start.2 = (f32[1,3484,128]{2,0,1:T(1,128)S(1)}, f32[1,3484,128]{2,0,1:T(1,128)}, u32[]{:S(2)}) copy-start(f32[1,3484,128]{2,0,1:T(1,128)} %param.25) | copy-start | bytes 5351428
  458.8 14.1 %collective-permute-start.12 = (bf16[2464,128]{1,0:T(8,128)(2,1)S(1)}, bf16[2464,128]{1,0:T(8,128)(2,1)S(1)}, u32[]{:S(2)}, u32[]{:S(2)}) collective-permute-start(bf16[2464,128]{1,0:T(8,128)(2,1)S(1)} %fusion.2), channel_id=1, source_target_pairs={{0,8},{1,9},{2,10},{3,11},{4,12},{5,13},{6,14},{7,15},{8,0},{9,1},... | collective-permute-start | bytes 1892360 | tf_op jit(solution)/shard_map/ppermute | solution.py:473
  461.5 6.3 %collective-permute-start.22 = (bf16[512,128]{1,0:T(8,128)(2,1)S(1)}, bf16[512,128]{1,0:T(8,128)(2,1)S(1)}, u32[]{:S(2)}, u32[]{:S(2)}) collective-permute-start(bf16[512,128]{1,0:T(8,128)(2,1)S(1)} %fusion.10), channel_id=1, source_target_pairs={{0,6},{1,7},{2,0},{3,1},{4,2},{5,3},{6,4},{7,5},{8,14},{9,15},{10,... | collective-permute-start | bytes 393224 | tf_op jit(solution)/shard_map/ppermute | solution.py:473
  472.9 1.5 copy-start.1
  473.3 1.8 copy-start
